TPU v7x, 128 devices: a whole 4x4x4 slice. The times are simulated.
128 devices in a mesh: req: 32 (over x, z_hi, y), tp: 4 (over z_lo, core).
Axes of the slice: x: 4, y: 4, z: 4 (z_hi: 2, z_lo: 2; z = z_hi * 2 + z_lo), core: 2. Of those that a mesh axis runs over, the one named last changes fastest.
Arguments:
- hidden_in: bfloat16 [12288, 1536], P('req', 'tp'), may hold values from -100 to 100
- norm_attn: float32 [1536], P('tp'), may hold values from 0.25 to 1.75
- w_query: bfloat16 [1536, 1536], P(None, 'tp'), may hold values from -0.15625 to 0.15625
- w_key: bfloat16 [1536, 256], replicated, may hold values from -0.3125 to 0.3125
- w_value: bfloat16 [1536, 256], replicated, may hold values from -0.15625 to 0.15625
- w_out: bfloat16 [1536, 1536], P('tp'), may hold values from -0.5 to 0.5
- prefix_cache: bfloat16 [512, 2, 2, 128, 128], P('req'), may hold values from -260 to 260
- page_table: int32 [8, 64], replicated, may hold values from 0 to 511, as said below
- group_of: int32 [32], replicated, may hold values from 0 to 7, as said below
- suffix_len: int32 [32], P('req'), may hold values from 96 to 384, as said below
- norm_moe: float32 [1536], P('tp'), may hold values from 0.25 to 1.75
- expert_ids: int32 [12288, 4], P('req'), may hold values from 0 to 31, all different within a row; in each aligned block of 384 rows (0 to 383, 384 to 767, ...) at most 72 rows name the same one
- expert_weights: float32 [12288, 4], P('req'), may hold values from 0.2 to 1
- w_gate: bfloat16 [32, 1536, 768], P('req', None, 'tp'), may hold values from -0.15625 to 0.15625
- w_up: bfloat16 [32, 1536, 768], P('req', None, 'tp'), may hold values from -0.15625 to 0.15625
- w_down: bfloat16 [32, 768, 1536], P('req', 'tp'), may hold values from -0.21875 to 0.21875
Outputs:
- layer_out: bfloat16 [12288, 1536], P('req', 'tp')
Inputs may be any that keep to these rules, and one draw needn't show every extreme that they name: `page_table`: every page 0 to 511 appears exactly once; page p lies in row p // 16 of the req-sharded prefix_cache, in local slot p mod 16; every req index holds either none or exactly 4 pages of a prefix. `group_of`: every prefix serves exactly 4 requests. `suffix_len`: some request has exactly 384 suffix tokens. `expert_ids`: the 4 experts of a slot differ; in the 384 slots of one request no expert is named more than 72 times.
All inputs are finite; a program needn't handle non-finite values.
Results may differ from a plain program's by a relative error of at most 0.012.
The roundings to bfloat16 on the way count: a program that leaves them out, or rounds other values in their place, can miss the bound.
Values may be sent and summed in bfloat16 or wider, within the bound.
A program may use at most 128 MiB of HBM per device.

v0:
```python
import math

import jax
import jax.numpy as jnp
from jax import lax
from jax.sharding import PartitionSpec as P

D = 1536
KVH = 2
HD = 128
TOP = 4
PREFIX = 8192


EPSILON = 1e-06
ROPE_BASE = 1000000.0
MASKED = -1e30


def rotate(values, positions):
    half_dim = values.shape[-1] // 2
    frequency = jnp.power(
        ROPE_BASE, -2.0 * jnp.arange(half_dim).astype(jnp.float32) / values.shape[-1]
    )
    angles = positions[:, None] * frequency[None, :]
    cosine = jnp.cos(angles)[:, None, :]
    sine_part = jnp.sin(angles)[:, None, :]
    first_half = values[..., :half_dim]
    second = values[..., half_dim:]
    return jnp.concatenate(
        [first_half * cosine - second * sine_part, second * cosine + first_half * sine_part],
        axis=-1,
    )


def body(
    hidden_in,
    norm_attn,
    w_query,
    w_key,
    w_value,
    w_out,
    prefix_cache,
    page_table,
    group_of,
    suffix_len,
    norm_moe,
    expert_ids,
    expert_weights,
    w_gate,
    w_up,
    w_down,
):
    req_count = lax.axis_size("req")
    tp_count = lax.axis_size("tp")
    req_index = lax.axis_index("req")
    tp_index = lax.axis_index("tp")
    rows_here = hidden_in.shape[0]
    feature_cols = hidden_in.shape[1]
    heads_here = w_query.shape[1] // HD
    shared_head = tp_index // (tp_count // KVH)
    hidden = hidden_in.astype(jnp.float32)
    sq_in = lax.psum(jnp.sum(hidden * hidden, axis=1), "tp")
    normed = (hidden * lax.rsqrt(sq_in / D + EPSILON)[:, None] * norm_attn).astype(jnp.bfloat16)
    key_cols = lax.dynamic_slice_in_dim(w_key, shared_head * HD, HD, 1)
    value_cols = lax.dynamic_slice_in_dim(w_value, shared_head * HD, HD, 1)
    w_both = jnp.concatenate([key_cols, value_cols], axis=1)
    shard_piece = lax.all_gather(normed, "tp", axis=1, tiled=True)
    query_lin = jnp.dot(shard_piece, w_query, preferred_element_type=jnp.float32)
    pair_lin = jnp.dot(shard_piece, w_both, preferred_element_type=jnp.float32)
    positions = (PREFIX + jnp.arange(rows_here)).astype(jnp.float32)
    query_rot = rotate(query_lin.reshape(rows_here, heads_here, HD), positions).astype(jnp.bfloat16)
    key_suf = rotate(pair_lin[:, None, :HD], positions)[:, 0].astype(jnp.bfloat16)
    value_suf = pair_lin[:, HD:].astype(jnp.bfloat16)
    groups = page_table.shape[0]
    local_pages = prefix_cache.shape[0]
    page_rows = prefix_cache.shape[3]
    most_pages = min(local_pages // 2, 2 * page_table.shape[1] // req_count)
    my_group = group_of[req_index]
    owner_of = page_table // local_pages
    slot_of = page_table % local_pages
    owned_here = (owner_of == req_index).astype(jnp.int32)
    slot_rank = jnp.cumsum(owned_here, axis=1) - 1
    picker = (
        owned_here[:, :, None, None]
        * (slot_rank[:, :, None, None] == jnp.arange(most_pages)[None, None, :, None])
        * (slot_of[:, :, None, None] == jnp.arange(local_pages)[None, None, None, :])
    )
    picker = jnp.sum(picker, axis=1).astype(jnp.float32)
    peer_group = (group_of[:, None] == jnp.arange(groups)[None, :]).astype(jnp.float32)
    choose = jnp.einsum("qg,grs->qrs", peer_group, picker).astype(jnp.bfloat16)
    local_head = lax.dynamic_index_in_dim(prefix_cache, shared_head, axis=2, keepdims=False)
    flat_cache = local_head.reshape(local_pages, -1)
    outgoing = jnp.einsum(
        "qrs,sx->qrx", choose, flat_cache, preferred_element_type=jnp.float32
    ).astype(jnp.bfloat16)
    incoming = lax.all_to_all(
        outgoing.reshape(req_count, most_pages, 2, page_rows, HD),
        "req",
        split_axis=0,
        concat_axis=0,
        tiled=True,
    )
    keys_pre = incoming[:, :, 0]
    values_pre = incoming[:, :, 1]
    my_owners = lax.dynamic_index_in_dim(owner_of, my_group, axis=0, keepdims=False)
    page_count = jnp.sum(my_owners[None, :] == jnp.arange(req_count)[:, None], axis=1)
    live_slots = jnp.arange(most_pages)[None, :] < page_count[:, None]
    live_keys = jnp.broadcast_to(
        live_slots[:, :, None], (req_count, most_pages, page_rows)
    ).reshape(-1)
    key_total = req_count * most_pages * page_rows
    block_len = math.gcd(key_total, 2048)
    block_count = key_total // block_len
    score_scale = 1.0 / math.sqrt(HD)
    scores = (
        jnp.einsum("thd,jd->thj", query_rot, key_suf, preferred_element_type=jnp.float32)
        * score_scale
    )
    causal = jnp.arange(rows_here)[:, None] >= jnp.arange(rows_here)[None, :]
    scores = jnp.where(causal[:, None, :], scores, MASKED)
    row_max = jnp.max(scores, axis=2)
    weights = jnp.exp(scores - row_max[:, :, None])
    row_sum = jnp.sum(weights, axis=2)
    weighted = jnp.einsum(
        "thj,jd->thd", weights.astype(jnp.bfloat16), value_suf, preferred_element_type=jnp.float32
    )

    def absorb(running, block_parts):
        old_max, old_sum, old_weighted = running
        key_block, value_block, valid_block = block_parts
        block_scores = (
            jnp.einsum("thd,kd->thk", query_rot, key_block, preferred_element_type=jnp.float32)
            * score_scale
        )
        block_scores = jnp.where(valid_block[None, None, :], block_scores, MASKED)
        new_max = jnp.maximum(old_max, jnp.max(block_scores, axis=2))
        rescale = jnp.exp(old_max - new_max)
        block_weights = jnp.exp(block_scores - new_max[:, :, None])
        new_sum = old_sum * rescale + jnp.sum(block_weights, axis=2)
        new_weighted = old_weighted * rescale[:, :, None] + jnp.einsum(
            "thk,kd->thd",
            block_weights.astype(jnp.bfloat16),
            value_block,
            preferred_element_type=jnp.float32,
        )
        return ((new_max, new_sum, new_weighted), None)

    block_inputs = (
        keys_pre.reshape(block_count, block_len, HD),
        values_pre.reshape(block_count, block_len, HD),
        live_keys.reshape(block_count, block_len),
    )
    (row_max, row_sum, weighted), _ = lax.scan(absorb, (row_max, row_sum, weighted), block_inputs)
    attention = (
        (weighted / row_sum[:, :, None]).astype(jnp.bfloat16).reshape(rows_here, heads_here * HD)
    )
    proj_part = jnp.dot(attention, w_out, preferred_element_type=jnp.float32)
    attn_slice = lax.psum_scatter(
        proj_part.astype(jnp.bfloat16), "tp", scatter_dimension=1, tiled=True
    ).astype(jnp.float32)
    residual = hidden + attn_slice
    sq_mid = lax.psum(jnp.sum(residual * residual, axis=1), "tp")
    moe_in = (residual * lax.rsqrt(sq_mid / D + EPSILON)[:, None] * norm_moe).astype(jnp.bfloat16)
    expert_count = w_gate.shape[0] * req_count
    capacity = 3 * rows_here * TOP // (2 * expert_count)
    onehot_exp = (
        (expert_ids[:, :, None] == jnp.arange(expert_count)[None, None, :])
        .astype(jnp.int32)
        .reshape(rows_here * TOP, expert_count)
    )
    pair_rank = jnp.sum(jnp.cumsum(onehot_exp, axis=0) * onehot_exp, axis=1) - 1
    slot_pos = expert_ids.reshape(-1) * capacity + pair_rank
    pair_token = jnp.arange(rows_here * TOP) // TOP
    slot_match = slot_pos[None, :] == jnp.arange(expert_count * capacity)[:, None]
    slot_token = jnp.sum(jnp.where(slot_match, pair_token[None, :], 0), axis=1)
    full_rows = lax.all_gather(moe_in, "tp", axis=1, tiled=True)
    outgoing_rows = jnp.take(full_rows, slot_token, axis=0).reshape(
        req_count, -1, full_rows.shape[1]
    )
    rows_in = lax.all_to_all(outgoing_rows, "req", split_axis=0, concat_axis=0, tiled=True)
    src_count, item_count, width_all = rows_in.shape
    flat_rows = rows_in.reshape(src_count * item_count, width_all)
    gate_lin = jnp.dot(flat_rows, w_gate[0], preferred_element_type=jnp.float32)
    up_lin = jnp.dot(flat_rows, w_up[0], preferred_element_type=jnp.float32)
    hidden_act = (jnp.maximum(gate_lin, 0.0) * up_lin).astype(jnp.bfloat16)
    down_part = jnp.dot(hidden_act, w_down[0], preferred_element_type=jnp.float32).reshape(
        src_count, item_count, width_all
    )
    expert_out = lax.psum_scatter(
        down_part.astype(jnp.bfloat16), "tp", scatter_dimension=2, tiled=True
    )
    returned = lax.all_to_all(expert_out, "req", split_axis=0, concat_axis=0, tiled=True)
    flat_back = returned.reshape(-1, feature_cols)
    picked = jnp.take(flat_back, slot_pos, axis=0).reshape(rows_here, TOP, feature_cols)
    moe_part = jnp.sum(expert_weights[:, :, None] * picked.astype(jnp.float32), axis=1)
    layer_out = residual + moe_part
    live_rows = jnp.arange(rows_here) < suffix_len[0]
    return jnp.where(live_rows[:, None], layer_out, 0.0).astype(jnp.bfloat16)


def solution(mesh):
    in_specs = (
        P("req", "tp"),
        P("tp"),
        P(None, "tp"),
        P(),
        P(),
        P("tp", None),
        P("req", None, None, None, None),
        P(),
        P(),
        P("req"),
        P("tp"),
        P("req", None),
        P("req", None),
        P("req", None, "tp"),
        P("req", None, "tp"),
        P("req", "tp", None),
    )
    out_specs = P("req", "tp")
    return jax.shard_map(body, mesh=mesh, in_specs=in_specs, out_specs=out_specs, check_vma=False)
```

profile of v0, /device:TPU:1, one launch (start us, length us, event | category | flops | bytes accessed | tf_op | source)
XLA Modules:
  0.0 634.7 jit_solution(4992400756129000989)
XLA Ops:
  6.5 1.6 copy-done
  9.6 4.9 convolution_convert_fusion
  14.5 9.1 %copy.105 = bf16[16,8,256,128]{3,2,1,0:T(8,128)(2,1)} copy(bf16[16,8,256,128]{3,1,2,0:T(8,128)(2,1)} %bitcast.112) | data formatting | bytes 16777216
  23.6 10.3 %copy.82 = bf16[32,4,2,128,128]{4,3,2,1,0:T(8,128)(2,1)} copy(bf16[32,4,2,128,128]{4,3,2,0,1:T(8,128)(2,1)} %bitcast.113) | data formatting | bytes 16777216 | tf_op jit(solution)/shard_map/reshape | solution.py:98
  34.0 11.4 %all-to-all-start = ((bf16[32,4,2,128,128]{4,3,2,1,0:T(8,128)(2,1)}), bf16[32,4,2,128,128]{4,3,2,1,0:T(8,128)(2,1)}, u32[]{:S(2)}, u32[]{:S(2)}) async-start(bf16[32,4,2,128,128]{4,3,2,1,0:T(8,128)(2,1)} %copy.82), calls=%async_computation | async-start | bytes 16777216 | tf_op jit(solution)/shard_map/all_to_all | solution.py:97
  45.6 42.0 %psum.14 = f32[384]{0:T(512)S(1)} all-reduce(f32[384]{0:T(512)S(1)} %fusion.32), channel_id=1, replica_groups=mesh['req'=32,'tp'=4] {'tp'}, use_global_device_ids=true, to_apply=%region_1.2 | all-reduce | flops 384 | bytes 3072 | tf_op jit(solution)/shard_map/psum | solution.py:63
  87.7 0.9 fusion.34
  91.7 0.8 multiply_cosine_fusion
  92.6 78.3 %all-gather.3.cloned.1.call-done = bf16[384,1536]{1,0:T(8,128)(2,1)} async-done(((bf16[384,384]{1,0:T(8,128)(2,1)}), bf16[384,1536]{1,0:T(8,128)(2,1)}) %all-gather.3.cloned.1.call-update) | async-done | bytes 1179664 | tf_op jit(solution)/shard_map/all_gather | solution.py:68
  170.9 2.4 fusion.75
  174.3 0.9 copy-done.12
  177.9 20.8 %all-to-all-done = bf16[32,4,2,128,128]{4,3,2,1,0:T(8,128)(2,1)} async-done(((bf16[32,4,2,128,128]{4,3,2,1,0:T(8,128)(2,1)}), bf16[32,4,2,128,128]{4,3,2,1,0:T(8,128)(2,1)}, u32[]{:S(2)}, u32[]{:S(2)}) %all-to-all-start) | async-done | bytes 8388640 | tf_op jit(solution)/shard_map/all_to_all | solution.py:97
  198.7 6.0 fusion.73
  204.7 70.1 %while.14 = (s32[]{:T(128)}, f32[384,3]{0,1:T(4,128)S(1)}, f32[384,3]{0,1:T(4,128)S(1)}, f32[384,3,128]{2,0,1:T(8,128)S(1)}, pred[8,2048]{1,0:T(8,128)(4,1)S(1)}...) while((s32[]{:T(128)}, f32[384,3]{0,1:T(4,128)S(1)}, ...), condition=%wide.region_10.11_spmd, body=%wide.region_7.10_spmd.sunk | while | flops 1234209024 | bytes 30919776 | solution.py:154
  204.8 2.7 bitcast_reduce_fusion.2
  207.5 2.1 fusion.95
  209.6 3.8 fusion.96
  213.5 2.8 bitcast_reduce_fusion.2
  216.3 2.1 fusion.95
  218.4 3.8 fusion.96
  222.3 2.7 bitcast_reduce_fusion.2
  225.0 2.1 fusion.95
  227.1 3.8 fusion.96
  231.0 2.7 bitcast_reduce_fusion.2
  233.8 2.1 fusion.95
  235.9 3.8 fusion.96
  239.8 2.8 bitcast_reduce_fusion.2
  242.6 2.1 fusion.95
  244.7 3.8 fusion.96
  248.6 2.7 bitcast_reduce_fusion.2
  251.3 2.1 fusion.95
  253.4 3.8 fusion.96
  257.3 2.7 bitcast_reduce_fusion.2
  260.1 2.1 fusion.95
  262.2 3.8 fusion.96
  266.1 2.8 bitcast_reduce_fusion.2
  268.8 2.1 fusion.95
  270.9 3.8 fusion.96
  275.1 2.1 convolution_convert_fusion.2
  277.2 1.4 copy.99
  278.7 28.7 %reduce-scatter.7.cloned.1.call-done = bf16[384,384]{1,0:T(8,128)(2,1)} async-done(((bf16[1536,384]{1,0:T(8,128)(2,1)}), bf16[384,384]{1,0:T(8,128)(2,1)}) %reduce-scatter.7.cloned.1.call-update) | async-done | bytes 294928
  307.4 1.2 copy.100
  308.7 5.1 psum.15
  313.8 0.8 multiply_convert_fusion
  315.4 9.1 %reduce-window.6 = s32[32,12,128]{2,1,0:T(8,128)S(1)} reduce-window(s32[32,12,128]{2,1,0:T(8,128)S(1)} %fusion.38, s32[]{:T(128)} %constant.134.clone.1), window={size=1x1x128 pad=0_0x0_0x127_0}, to_apply=%region_12.13 | reduce-window | flops 6242304 | bytes 393220 | tf_op jit(solution)/shard_map/reduce-window
  325.2 1.5 select_reduce_fusion
  326.9 11.8 %all-gather.5.cloned.1.call-done = bf16[384,1536]{1,0:T(8,128)(2,1)} async-done(((bf16[384,384]{1,0:T(8,128)(2,1)}), bf16[384,1536]{1,0:T(8,128)(2,1)}) %all-gather.5.cloned.1.call-update) | async-done | bytes 1179664 | tf_op jit(solution)/shard_map/all_gather | solution.py:177
  338.7 16.3 %gather_fusion = bf16[2304,1536]{1,0:T(8,128)(2,1)} fusion(bf16[384,1536]{1,0:T(8,128)(2,1)} %all-gather.5.cloned.1.call-done, s32[3072]{0:T(1024)S(1)} %pad_clamp_fusion), kind=kCustom, calls=%fused_computation | custom fusion | bytes 14164992 | tf_op jit(solution)/shard_map/jit(_take)/gather | solution.py:178
  355.0 3.7 broadcast_select_fusion
  358.7 90.5 %all_to_all.15 = bf16[32,72,1536]{2,1,0:T(8,128)(2,1)S(1)} all-to-all(bf16[32,72,1536]{2,1,0:T(8,128)(2,1)S(1)} %broadcast_select_fusion), channel_id=1, replica_groups=mesh['req'=32,'tp'=4] {'req'}, dimensions={0} | all-to-all | bytes 14155776 | tf_op jit(solution)/shard_map/all_to_all | solution.py:181
  449.2 2.4 convolution_maximum_fusion
  451.7 2.5 fusion.18
  455.2 4.8 convolution_convert_fusion.1
  460.1 15.5 %copy.101 = bf16[32,72,1536]{1,0,2:T(8,128)(2,1)} copy(bf16[32,72,1536]{2,1,0:T(8,128)(2,1)} %convolution_convert_fusion.1) | data formatting | bytes 14155776
  475.6 21.4 %reshape.354 = bf16[1536,2304]{1,0:T(8,128)(2,1)} reshape(bf16[1536,32,72]{2,1,0:T(8,128)(2,1)} %bitcast.111) | data formatting | bytes 14155776
  497.0 68.5 %reduce-scatter.9.cloned.1.call-done = bf16[384,2304]{1,0:T(8,128)(2,1)} async-done(((bf16[1536,2304]{1,0:T(8,128)(2,1)}), bf16[384,2304]{1,0:T(8,128)(2,1)}) %reduce-scatter.9.cloned.1.call-update) | async-done | bytes 1769488
  565.5 8.8 %reshape.355 = bf16[384,32,72]{2,1,0:T(8,128)(2,1)} reshape(bf16[384,2304]{1,0:T(8,128)(2,1)} %reduce-scatter.9.cloned.1.call-done) | data formatting | bytes 3538944
  574.3 4.7 copy.102
  579.0 9.4 %all-to-all-start.2 = ((bf16[32,72,384]{2,1,0:T(8,128)(2,1)}), bf16[32,72,384]{2,1,0:T(8,128)(2,1)}, u32[]{:S(2)}, u32[]{:S(2)}) async-start(bf16[32,72,384]{2,1,0:T(8,128)(2,1)} %copy.102), calls=%async_computation.2 | async-start | bytes 3538944 | tf_op jit(solution)/shard_map/all_to_all | solution.py:193
  590.0 23.4 %all-to-all-done.2 = bf16[32,72,384]{2,1,0:T(8,128)(2,1)} async-done(((bf16[32,72,384]{2,1,0:T(8,128)(2,1)}), bf16[32,72,384]{2,1,0:T(8,128)(2,1)}, u32[]{:S(2)}, u32[]{:S(2)}) %all-to-all-start.2) | async-done | bytes 1769504 | tf_op jit(solution)/shard_map/all_to_all | solution.py:193
  613.4 6.8 %gather_fusion.1 = bf16[1536,384]{1,0:T(8,128)(2,1)} fusion(bf16[2304,384]{1,0:T(8,128)(2,1)} %bitcast.26, s32[2048]{0:T(1024)S(1)} %pad_clamp_fusion.1), kind=kCustom, calls=%fused_computation.1 | custom fusion | bytes 2365440 | tf_op jit(solution)/shard_map/jit(_take)/gather | solution.py:195
  620.2 3.2 gather.15
  623.5 3.8 multiply_reduce_fusion
  627.3 0.8 select_convert_fusion
  (131 shorter events, 11.1 us)
Async XLA Ops:
  6.5 1.6 copy-start
  6.5 2.2 copy-start.7
  6.5 3.1 copy-start.11
  34.0 11.5 %copy-start.2 = (bf16[384,384]{1,0:T(8,128)(2,1)S(1)}, bf16[384,384]{1,0:T(8,128)(2,1)}, u32[]{:S(2)}) copy-start(bf16[384,384]{1,0:T(8,128)(2,1)} %param.18) | copy-start | bytes 884740
  34.0 53.7 %copy-start.9 = (f32[384]{0:T(512)S(1)}, f32[384]{0:T(512)}, u32[]{:S(2)}) copy-start(f32[384]{0:T(512)} %param.19) | copy-start | bytes 4612
  34.0 58.5 %copy-start.4 = (bf16[1536,256]{1,0:T(8,128)(2,1)S(1)}, bf16[1536,256]{1,0:T(8,128)(2,1)}, u32[]{:S(2)}) copy-start(bf16[1536,256]{1,0:T(8,128)(2,1)} %param.22) | copy-start | bytes 2359300
  34.0 58.5 %copy-start.5 = (bf16[1536,256]{1,0:T(8,128)(2,1)S(1)}, bf16[1536,256]{1,0:T(8,128)(2,1)}, u32[]{:S(2)}) copy-start(bf16[1536,256]{1,0:T(8,128)(2,1)} %param.21) | copy-start | bytes 2359300
  34.0 164.7 %all-to-all-start = ((bf16[32,4,2,128,128]{4,3,2,1,0:T(8,128)(2,1)}), bf16[32,4,2,128,128]{4,3,2,1,0:T(8,128)(2,1)}, u32[]{:S(2)}, u32[]{:S(2)}) async-start(bf16[32,4,2,128,128]{4,3,2,1,0:T(8,128)(2,1)} %copy.82), calls=%async_computation | async-start | bytes 16777216 | tf_op jit(solution)/shard_map/all_to_all | solution.py:97
  45.4 125.5 %all-gather.3.cloned.1.call-start = ((), (), s32[]{:S(2)}) async-start(), calls=%async_computation.5 | async-start | bytes 1474560 | tf_op jit(solution)/shard_map/all_gather | solution.py:68
  88.6 218.8 %reduce-scatter.7.cloned.1.call-start = ((), (), s32[]{:S(2)}) async-start(), calls=%async_computation.7 | async-start | bytes 1474560
  173.9 1.3 copy-start.12
  277.2 36.7 %copy-start.10 = (f32[384]{0:T(512)S(1)}, f32[384]{0:T(512)}, u32[]{:S(2)}) copy-start(f32[384]{0:T(512)} %param.28) | copy-start | bytes 4612
  278.6 36.4 %copy-start.6 = (s32[384,4]{0,1:T(4,128)S(1)}, s32[384,4]{0,1:T(4,128)}, u32[]{:S(2)}) copy-start(s32[384,4]{0,1:T(4,128)} %param.29) | copy-start | bytes 18436
  278.6 60.1 %all-gather.5.cloned.1.call-start = ((), (), s32[]{:S(2)}) async-start(), calls=%async_computation.6 | async-start | bytes 1474560 | tf_op jit(solution)/shard_map/all_gather | solution.py:177
  314.7 250.8 %reduce-scatter.9.cloned.1.call-start = ((), (), s32[]{:S(2)}) async-start(), calls=%async_computation.8 | async-start | bytes 8847360
  358.7 90.5 %copy-start.13 = (bf16[1,1536,192]{1,2,0:T(8,128)(2,1)S(1)}, bf16[1,1536,192]{1,2,0:T(8,128)(2,1)}, u32[]{:S(2)}) copy-start(bf16[1,1536,192]{1,2,0:T(8,128)(2,1)} %param.31) | copy-start | bytes 1769476
  449.2 2.4 copy-start.14
  454.2 1.1 copy-start.3
  579.0 10.2 %copy-start.8 = (f32[384,4]{0,1:T(4,128)S(1)}, f32[384,4]{0,1:T(4,128)}, u32[]{:S(2)}) copy-start(f32[384,4]{0,1:T(4,128)} %param.30) | copy-start | bytes 18436
  579.0 34.4 %all-to-all-start.2 = ((bf16[32,72,384]{2,1,0:T(8,128)(2,1)}), bf16[32,72,384]{2,1,0:T(8,128)(2,1)}, u32[]{:S(2)}, u32[]{:S(2)}) async-start(bf16[32,72,384]{2,1,0:T(8,128)(2,1)} %copy.102), calls=%async_computation.2 | async-start | bytes 3538944 | tf_op jit(solution)/shard_map/all_to_all | solution.py:193
  613.4 14.7 %copy-start.1 = (bf16[16,2,2,128,128]{4,3,2,1,0:T(8,128)(2,1)S(1)}, bf16[16,2,2,128,128]{4,3,2,1,0:T(8,128)(2,1)}, u32[]{:S(2)}) copy-start(bf16[16,2,2,128,128]{4,3,2,1,0:T(8,128)(2,1)} %param.24) | copy-start | bytes 6291460
Sparse Core Ops, SparseCore 0:
  88.7 82.2 all-gather.2
  278.7 28.5 reduce-scatter.6
  314.8 23.8 all-gather.4
  497.2 68.2 reduce-scatter.8
where the time goes:
time: 638 us; the launch traced here: 635 us
  waiting for transfers between devices  232 us (36%)
  blocking collectives  138 us (22%)
  local copies, waits for them, and re-layouts  113 us (18%)
  matrix products  73.5 us (12%)
  other arithmetic  41.2 us (6%)
  starting transfers between devices  21.4 us (3%)
  between operations  16.2 us (3%)
    unnamed x6, waiting for transfers between devices  97.2 us
    all_to_all x1, blocking collectives, body(): lax.all_to_all(outgoing_rows, 'req', split_axis=0, concat_axis=0, tiled=T...  90.5 us
    all_gather x1, waiting for transfers between devices, body(): shard_piece = lax.all_gather(normed, 'tp', axis=1, tiled=True)  78.3 us
    unnamed x41, local copies, waits for them, and re-layouts  65.8 us
    psum x1, blocking collectives, body(): sq_in = lax.psum(jnp.sum(hidden * hidden, axis=1), 'tp')  42 us
    dot_general x8, matrix products, absorb(): jnp.einsum('thk,kd->thd', block_weights.astype(jnp.bfloat16), value_block...  30.6 us
    all_to_all x1, waiting for transfers between devices, body(): lax.all_to_all(expert_out, 'req', split_axis=0, concat_axis=0, tiled=True)  23.4 us
    dot_general x8, matrix products, absorb(): jnp.einsum('thd,kd->thk', query_rot, key_block, preferred_element_type=jn...  22 us
  transfers between devices with their start and end apart: 6, of which 6 were waited for; matrix products, arithmetic and copies ran while one was open for 3% of the time, Pallas kernels for 0%

commit v1 on v0

--- a/solution.py
+++ b/solution.py
@@ -60,12 +60,14 @@
     heads_here = w_query.shape[1] // HD
     shared_head = tp_index // (tp_count // KVH)
     hidden = hidden_in.astype(jnp.float32)
-    sq_in = lax.psum(jnp.sum(hidden * hidden, axis=1), "tp")
-    normed = (hidden * lax.rsqrt(sq_in / D + EPSILON)[:, None] * norm_attn).astype(jnp.bfloat16)
+    full_in = lax.all_gather(hidden_in, "tp", axis=1, tiled=True).astype(jnp.float32)
+    sq_in = jnp.sum(full_in * full_in, axis=1)
+    shard_piece = (full_in * lax.rsqrt(sq_in / D + EPSILON)[:, None] * norm_attn).astype(
+        jnp.bfloat16
+    )
     key_cols = lax.dynamic_slice_in_dim(w_key, shared_head * HD, HD, 1)
     value_cols = lax.dynamic_slice_in_dim(w_value, shared_head * HD, HD, 1)
     w_both = jnp.concatenate([key_cols, value_cols], axis=1)
-    shard_piece = lax.all_gather(normed, "tp", axis=1, tiled=True)
     query_lin = jnp.dot(shard_piece, w_query, preferred_element_type=jnp.float32)
     pair_lin = jnp.dot(shard_piece, w_both, preferred_element_type=jnp.float32)
     positions = (PREFIX + jnp.arange(rows_here)).astype(jnp.float32)
@@ -164,36 +166,51 @@
     moe_in = (residual * lax.rsqrt(sq_mid / D + EPSILON)[:, None] * norm_moe).astype(jnp.bfloat16)
     expert_count = w_gate.shape[0] * req_count
     capacity = 3 * rows_here * TOP // (2 * expert_count)
+    sub = capacity // tp_count
+    gate_full = lax.all_gather(w_gate[0], "tp", axis=1, tiled=True)
+    up_full = lax.all_gather(w_up[0], "tp", axis=1, tiled=True)
+    down_full = lax.all_gather(w_down[0], "tp", axis=0, tiled=True)
     onehot_exp = (
         (expert_ids[:, :, None] == jnp.arange(expert_count)[None, None, :])
         .astype(jnp.int32)
         .reshape(rows_here * TOP, expert_count)
     )
     pair_rank = jnp.sum(jnp.cumsum(onehot_exp, axis=0) * onehot_exp, axis=1) - 1
-    slot_pos = expert_ids.reshape(-1) * capacity + pair_rank
+    mine = (pair_rank // sub) == tp_index
+    send_pos = expert_ids.reshape(-1) * sub + pair_rank % sub
     pair_token = jnp.arange(rows_here * TOP) // TOP
-    slot_match = slot_pos[None, :] == jnp.arange(expert_count * capacity)[:, None]
+    slot_match = (send_pos[None, :] == jnp.arange(expert_count * sub)[:, None]) & mine[None, :]
     slot_token = jnp.sum(jnp.where(slot_match, pair_token[None, :], 0), axis=1)
     full_rows = lax.all_gather(moe_in, "tp", axis=1, tiled=True)
     outgoing_rows = jnp.take(full_rows, slot_token, axis=0).reshape(
-        req_count, -1, full_rows.shape[1]
+        req_count, sub, full_rows.shape[1]
     )
     rows_in = lax.all_to_all(outgoing_rows, "req", split_axis=0, concat_axis=0, tiled=True)
     src_count, item_count, width_all = rows_in.shape
     flat_rows = rows_in.reshape(src_count * item_count, width_all)
-    gate_lin = jnp.dot(flat_rows, w_gate[0], preferred_element_type=jnp.float32)
-    up_lin = jnp.dot(flat_rows, w_up[0], preferred_element_type=jnp.float32)
+    gate_lin = jnp.dot(flat_rows, gate_full, preferred_element_type=jnp.float32)
+    up_lin = jnp.dot(flat_rows, up_full, preferred_element_type=jnp.float32)
     hidden_act = (jnp.maximum(gate_lin, 0.0) * up_lin).astype(jnp.bfloat16)
-    down_part = jnp.dot(hidden_act, w_down[0], preferred_element_type=jnp.float32).reshape(
-        src_count, item_count, width_all
-    )
-    expert_out = lax.psum_scatter(
-        down_part.astype(jnp.bfloat16), "tp", scatter_dimension=2, tiled=True
-    )
-    returned = lax.all_to_all(expert_out, "req", split_axis=0, concat_axis=0, tiled=True)
-    flat_back = returned.reshape(-1, feature_cols)
-    picked = jnp.take(flat_back, slot_pos, axis=0).reshape(rows_here, TOP, feature_cols)
-    moe_part = jnp.sum(expert_weights[:, :, None] * picked.astype(jnp.float32), axis=1)
+    block = hidden_act.shape[1] // tp_count
+    down_parts = jnp.einsum(
+        "rqf,qfd->qrd",
+        hidden_act.reshape(-1, tp_count, block),
+        down_full.reshape(tp_count, block, width_all),
+        preferred_element_type=jnp.float32,
+    ).astype(jnp.bfloat16)
+    expert_out = jnp.sum(down_parts.astype(jnp.float32), axis=0).astype(jnp.bfloat16)
+    returned = lax.all_to_all(
+        expert_out.reshape(src_count, item_count, width_all),
+        "req",
+        split_axis=0,
+        concat_axis=0,
+        tiled=True,
+    )
+    flat_back = returned.reshape(-1, width_all)
+    picked = jnp.take(flat_back, send_pos, axis=0).reshape(rows_here, TOP, width_all)
+    pick_weight = jnp.where(mine.reshape(rows_here, TOP), expert_weights, 0.0)
+    moe_full = jnp.sum(pick_weight[:, :, None] * picked.astype(jnp.float32), axis=1)
+    moe_part = lax.psum_scatter(moe_full, "tp", scatter_dimension=1, tiled=True)
     layer_out = residual + moe_part
     live_rows = jnp.arange(rows_here) < suffix_len[0]
     return jnp.where(live_rows[:, None], layer_out, 0.0).astype(jnp.bfloat16)
@@ -202,7 +219,7 @@
 def solution(mesh):
     in_specs = (
         P("req", "tp"),
-        P("tp"),
+        P(),
         P(None, "tp"),
         P(),
         P(),

time: 638 us -> 589 us (0.923)
  blocking collectives: 138 us -> 91.6 us
  local copies, waits for them, and re-layouts: 113 us -> 69.4 us
  waiting for transfers between devices: 232 us -> 253 us
  matrix products: 73.5 us -> 85.1 us
  other arithmetic: 41.2 us -> 50.4 us
    all_to_all x1, waiting for transfers between devices: 20.8 us -> 91.2 us  [body(): lax.all_to_all(outgoing.reshape(req_count, most_pages, 2, page_rows, HD),...]
    unnamed x6 -> x8, waiting for transfers between devices: 97.2 us -> 30.2 us
    unnamed x41 -> x34, local copies, waits for them, and re-layouts: 65.8 us -> 13.9 us
    all_to_all x1, blocking collectives: 90.5 us -> 41.3 us  [body(): lax.all_to_all(outgoing_rows, 'req', split_axis=0, concat_axis=0, tiled=T...]
    unnamed x0 -> x1, blocking collectives: none -> 45.2 us
    psum x1 -> x0, blocking collectives: 42 us -> none  [body(): sq_in = lax.psum(jnp.sum(hidden * hidden, axis=1), 'tp')]
    reduce_scatter x0 -> x1, waiting for transfers between devices: none -> 29.7 us  [body(): moe_part = lax.psum_scatter(moe_full, 'tp', scatter_dimension=1, tiled=True)]
    all_gather x1 -> x4, waiting for transfers between devices: 78.3 us -> 60.8 us  [the longest x1 29.2 us: body(): gate_full = lax.all_gather(w_gate[0], 'tp', axis=1, tiled=True)]
  transfers between devices with their start and end apart: 6 -> 9, of which waited for: 6 -> 8; matrix products, arithmetic and copies ran while one was open for 3% -> 9% of each run, Pallas kernels for 0% -> 0%
where the time goes in v1:
time: 589 us; the launch traced here: 588 us
  waiting for transfers between devices  253 us (43%)
  blocking collectives  91.6 us (16%)
  matrix products  85.1 us (14%)
  local copies, waits for them, and re-layouts  69.4 us (12%)
  other arithmetic  50.4 us (9%)
  starting transfers between devices  21.5 us (4%)
  between operations  16.6 us (3%)
    all_to_all x1, waiting for transfers between devices, body(): lax.all_to_all(outgoing.reshape(req_count, most_pages, 2, page_rows, HD),...  91.2 us
    unnamed x1, blocking collectives  45.2 us
    all_to_all x1, blocking collectives, body(): lax.all_to_all(outgoing_rows, 'req', split_axis=0, concat_axis=0, tiled=T...  41.3 us
    dot_general x8, matrix products, absorb(): jnp.einsum('thk,kd->thd', block_weights.astype(jnp.bfloat16), value_block...  37.8 us
    unnamed x8, waiting for transfers between devices  30.2 us
    all_to_all x1, waiting for transfers between devices, body(): lax.all_to_all(expert_out.reshape(src_count, item_count, width_all), 'req...  29.9 us
    reduce_scatter x1, waiting for transfers between devices, body(): moe_part = lax.psum_scatter(moe_full, 'tp', scatter_dimension=1, tiled=True)  29.7 us
    all_gather x1, waiting for transfers between devices, body(): gate_full = lax.all_gather(w_gate[0], 'tp', axis=1, tiled=True)  29.2 us
  transfers between devices with their start and end apart: 9, of which 8 were waited for; matrix products, arithmetic and copies ran while one was open for 9% of the time, Pallas kernels for 0%

profile of v1, /device:TPU:1, one launch (start us, length us, event | category | flops | bytes accessed | tf_op | source)
XLA Modules:
  0.0 587.6 jit_solution(2125378602592705042)
XLA Ops:
  6.5 1.6 copy-done
  9.6 4.9 convolution_convert_fusion
  14.5 9.1 %copy.115 = bf16[16,8,256,128]{3,2,1,0:T(8,128)(2,1)} copy(bf16[16,8,256,128]{3,1,2,0:T(8,128)(2,1)} %bitcast.104) | data formatting | bytes 16777216
  23.6 10.3 %copy.88 = bf16[32,4,2,128,128]{4,3,2,1,0:T(8,128)(2,1)} copy(bf16[32,4,2,128,128]{4,3,2,0,1:T(8,128)(2,1)} %bitcast.105) | data formatting | bytes 16777216 | tf_op jit(solution)/shard_map/reshape | solution.py:100
  34.0 11.4 %all-to-all-start = ((bf16[32,4,2,128,128]{4,3,2,1,0:T(8,128)(2,1)}), bf16[32,4,2,128,128]{4,3,2,1,0:T(8,128)(2,1)}, u32[]{:S(2)}, u32[]{:S(2)}) async-start(bf16[32,4,2,128,128]{4,3,2,1,0:T(8,128)(2,1)} %copy.88), calls=%async_computation | async-start | bytes 16777216 | tf_op jit(solution)/shard_map/all_to_all | solution.py:99
  46.2 45.2 %all-gather.4 = f32[4,1,384]{2,1,0:T(1,128)S(1)} all-gather(f32[1,1,384]{2,1,0:T(1,128)S(1)} %reshape.403), channel_id=2, replica_groups=mesh['req'=32,'tp'=4] {'tp'}, dimensions={0}, use_global_device_ids=true | all-gather | bytes 7680 | tf_op args[1]
  94.5 1.4 multiply_cosine_fusion
  96.9 1.6 fusion.19
  98.5 2.5 fusion.42
  102.8 1.8 fusion.37
  106.1 1.4 fusion.31
  107.5 91.2 %all-to-all-done = bf16[32,4,2,128,128]{4,3,2,1,0:T(8,128)(2,1)} async-done(((bf16[32,4,2,128,128]{4,3,2,1,0:T(8,128)(2,1)}), bf16[32,4,2,128,128]{4,3,2,1,0:T(8,128)(2,1)}, u32[]{:S(2)}, u32[]{:S(2)}) %all-to-all-start) | async-done | bytes 8388640 | tf_op jit(solution)/shard_map/all_to_all | solution.py:99
  198.7 6.0 %fusion.85 = (bf16[32,4,1,128,128]{4,3,2,1,0:T(8,128)(2,1)}, bf16[32,4,1,128,128]{4,3,2,1,0:T(8,128)(2,1)}) fusion(bf16[32,4,2,128,128]{4,3,2,1,0:T(8,128)(2,1)} %all-to-all-done), kind=kLoop, calls=%fused_computation.162 | loop fusion | bytes 16777216 | tf_op jit(solution)/shard_map/slice | solution.py:107
  204.7 77.0 %while.14 = (s32[]{:T(128)}, f32[384,3]{0,1:T(4,128)S(1)}, f32[384,3]{0,1:T(4,128)S(1)}, f32[384,3,128]{2,0,1:T(8,128)}, pred[8,2048]{1,0:T(8,128)(4,1)S(1)}, /*...) while((s32[]{:T(128)}, f32[384,3]{0,1:T(4,128)S(1)}, ...), condition=%wide.region_9.10_spmd, body=%wide.region_6.9_spmd.sunk | while | flops 1234209024 | bytes 30919776 | solution.py:156
  204.7 2.7 bitcast_reduce_fusion.2
  207.5 2.1 fusion.105
  209.6 4.7 fusion.106
  214.4 2.7 bitcast_reduce_fusion.2
  217.1 2.1 fusion.105
  219.2 4.7 fusion.106
  224.0 2.7 bitcast_reduce_fusion.2
  226.7 2.1 fusion.105
  228.8 4.7 fusion.106
  233.6 2.7 bitcast_reduce_fusion.2
  236.4 2.1 fusion.105
  238.5 4.7 fusion.106
  243.2 2.7 bitcast_reduce_fusion.2
  246.0 2.1 fusion.105
  248.1 4.7 fusion.106
  252.8 2.7 bitcast_reduce_fusion.2
  255.6 2.1 fusion.105
  257.7 4.7 fusion.106
  262.5 2.7 bitcast_reduce_fusion.2
  265.2 2.1 fusion.105
  267.3 4.7 fusion.106
  272.1 2.7 bitcast_reduce_fusion.2
  274.9 2.1 fusion.105
  276.9 4.7 fusion.106
  284.0 1.4 copy.111
  285.7 27.9 %reduce-scatter.7.cloned.1.call-done = bf16[384,384]{1,0:T(8,128)(2,1)} async-done(((bf16[1536,384]{1,0:T(8,128)(2,1)}), bf16[384,384]{1,0:T(8,128)(2,1)}) %reduce-scatter.7.cloned.1.call-update) | async-done | bytes 294928
  314.9 5.1 psum.7
  323.1 9.1 %reduce-window.6 = s32[32,12,128]{2,1,0:T(8,128)S(1)} reduce-window(s32[32,12,128]{2,1,0:T(8,128)S(1)} %fusion.44, s32[]{:T(128)} %constant.149.clone.1), window={size=1x1x128 pad=0_0x0_0x127_0}, to_apply=%region_11.12 | reduce-window | flops 6242304 | bytes 393220 | tf_op jit(solution)/shard_map/reduce-window
  333.9 11.0 %all-gather.13.cloned.1.call-done = bf16[384,1536]{1,0:T(8,128)(2,1)} async-done(((bf16[384,384]{1,0:T(8,128)(2,1)}), bf16[384,1536]{1,0:T(8,128)(2,1)}) %all-gather.13.cloned.1.call-update) | async-done | bytes 1179664 | tf_op jit(solution)/shard_map/all_gather | solution.py:184
  344.9 6.7 %gather_fusion = bf16[576,1536]{1,0:T(8,128)(2,1)S(1)} fusion(bf16[384,1536]{1,0:T(8,128)(2,1)} %all-gather.13.cloned.1.call-done, s32[1024]{0:T(1024)S(1)} %pad_clamp_fusion.1), kind=kCustom, calls=%fused_computation | custom fusion | bytes 3541248 | tf_op jit(solution)/shard_map/jit(_take)/gather | solution.py:185
  351.6 1.7 gather.13
  353.4 1.9 broadcast_select_fusion
  355.3 41.3 %all_to_all.15 = bf16[32,18,1536]{2,1,0:T(8,128)(2,1)} all-to-all(bf16[32,18,1536]{2,1,0:T(8,128)(2,1)S(1)} %broadcast_select_fusion), channel_id=1, replica_groups=mesh['req'=32,'tp'=4] {'req'}, dimensions={0} | all-to-all | bytes 3538944 | tf_op jit(solution)/shard_map/all_to_all | solution.py:188
  396.6 2.6 reshape.378
  399.2 4.7 all-gather.17.cloned.1.call-done
  403.9 4.5 fusion.22
  408.5 29.2 %all-gather.15.cloned.1.call-done = bf16[1,1536,768]{1,2,0:T(8,128)(2,1)} async-done(((bf16[1,1536,192]{1,2,0:T(8,128)(2,1)}), bf16[1,1536,768]{1,2,0:T(8,128)(2,1)}) %all-gather.15.cloned.1.call-update) | async-done | bytes 2359312 | tf_op jit(solution)/shard_map/all_gather | solution.py:170
  437.7 4.7 multiply_convert_fusion
  442.4 2.2 copy.103
  444.6 26.8 %all-gather.19.cloned.1.call-done = bf16[1,768,1536]{2,1,0:T(8,128)(2,1)} async-done(((bf16[1,192,1536]{2,1,0:T(8,128)(2,1)}), bf16[1,768,1536]{2,1,0:T(8,128)(2,1)}) %all-gather.19.cloned.1.call-update) | async-done | bytes 2359312 | tf_op jit(solution)/shard_map/all_gather | solution.py:172
  471.4 4.2 convert_reduce_fusion
  475.6 1.7 reshape.381
  477.3 9.3 %all-to-all-start.2 = ((bf16[32,18,1536]{2,1,0:T(8,128)(2,1)}), bf16[32,18,1536]{2,1,0:T(8,128)(2,1)}, u32[]{:S(2)}, u32[]{:S(2)}) async-start(bf16[32,18,1536]{2,1,0:T(8,128)(2,1)} %reshape.381), calls=%async_computation.2 | async-start | bytes 4718592 | tf_op jit(solution)/shard_map/all_to_all | solution.py:202
  488.7 29.9 %all-to-all-done.2 = bf16[32,18,1536]{2,1,0:T(8,128)(2,1)} async-done(((bf16[32,18,1536]{2,1,0:T(8,128)(2,1)}), bf16[32,18,1536]{2,1,0:T(8,128)(2,1)}, u32[]{:S(2)}, u32[]{:S(2)}) %all-to-all-start.2) | async-done | bytes 1769504 | tf_op jit(solution)/shard_map/all_to_all | solution.py:202
  518.6 2.6 reshape.382
  521.2 6.3 %gather_fusion.1 = bf16[1536,1536]{1,0:T(8,128)(2,1)} fusion(bf16[576,1536]{1,0:T(8,128)(2,1)S(1)} %reshape.382, s32[2048]{0:T(1024)S(1)} %pad_clamp_fusion), kind=kCustom, calls=%fused_computation.1 | custom fusion | bytes 9443328 | tf_op jit(solution)/shard_map/jit(_take)/gather | solution.py:210
  527.5 8.8 %gather.15 = bf16[384,4,1536]{2,1,0:T(4,128)(2,1)} reshape(bf16[1536,1536]{1,0:T(8,128)(2,1)} %gather_fusion.1) | data formatting | bytes 9437184 | tf_op jit(solution)/shard_map/jit(_take)/gather | solution.py:210
  536.4 12.2 %multiply_reduce_fusion = f32[384,1536]{1,0:T(8,128)} fusion(bf16[384,4,1536]{2,1,0:T(4,128)(2,1)} %gather.15, f32[384,4]{1,0:T(8,128)S(1)} %copy.98, pred[384,4]{1,0:T(8,128)(4,1)S(1)} %copy.102), kind=kLoop, calls=%fused_computation.24 | loop fusion | flops 8847360 | bytes 7085568 | tf_op jit(solution)/shard_map/reduce_sum | solution.py:212
  549.2 29.7 %reduce-scatter.5.cloned.1.call-done = f32[384,384]{1,0:T(8,128)} async-done(((f32[384,1536]{1,0:T(8,128)}), f32[384,384]{1,0:T(8,128)}) %reduce-scatter.5.cloned.1.call-update) | async-done | bytes 589840 | tf_op jit(solution)/shard_map/reduce_scatter | solution.py:213
  578.9 1.9 select_convert_fusion
  (144 shorter events, 18.4 us)
Async XLA Ops:
  6.5 1.6 copy-start
  6.5 2.2 copy-start.8
  6.5 3.1 copy-start.12
  34.0 12.2 %copy-start.11 = (f32[384]{0:T(512)S(1)}, f32[384]{0:T(512)}, u32[]{:S(2)}) copy-start(f32[384]{0:T(512)} %param.19) | copy-start | bytes 4612
  34.0 61.9 %copy-start.5 = (bf16[1536,256]{1,0:T(8,128)(2,1)S(1)}, bf16[1536,256]{1,0:T(8,128)(2,1)}, u32[]{:S(2)}) copy-start(bf16[1536,256]{1,0:T(8,128)(2,1)} %param.22) | copy-start | bytes 2359300
  34.0 61.9 %copy-start.6 = (bf16[1536,256]{1,0:T(8,128)(2,1)S(1)}, bf16[1536,256]{1,0:T(8,128)(2,1)}, u32[]{:S(2)}) copy-start(bf16[1536,256]{1,0:T(8,128)(2,1)} %param.21) | copy-start | bytes 2359300
  34.0 164.7 %all-to-all-start = ((bf16[32,4,2,128,128]{4,3,2,1,0:T(8,128)(2,1)}), bf16[32,4,2,128,128]{4,3,2,1,0:T(8,128)(2,1)}, u32[]{:S(2)}, u32[]{:S(2)}) async-start(bf16[32,4,2,128,128]{4,3,2,1,0:T(8,128)(2,1)} %copy.88), calls=%async_computation | async-start | bytes 16777216 | tf_op jit(solution)/shard_map/all_to_all | solution.py:99
  45.4 51.5 %all-gather.11.cloned.1.call-start = ((), (), s32[]{:S(2)}) async-start(), calls=%async_computation.5 | async-start | bytes 1474560 | tf_op jit(solution)/shard_map/all_gather | solution.py:63
  46.2 267.4 %reduce-scatter.7.cloned.1.call-start = ((), (), s32[]{:S(2)}) async-start(), calls=%async_computation.11 | async-start | bytes 1474560
  101.1 1.8 copy-start.3
  281.7 1.5 copy-start.4
  283.9 30.8 %copy-start.2 = (bf16[384,384]{1,0:T(8,128)(2,1)S(1)}, bf16[384,384]{1,0:T(8,128)(2,1)}, u32[]{:S(2)}) copy-start(bf16[384,384]{1,0:T(8,128)(2,1)} %param.18) | copy-start | bytes 884740
  284.0 36.1 %copy-start.10 = (f32[384]{0:T(512)S(1)}, f32[384]{0:T(512)}, u32[]{:S(2)}) copy-start(f32[384]{0:T(512)} %param.28) | copy-start | bytes 4612
  285.4 37.3 %copy-start.7 = (s32[384,4]{0,1:T(4,128)S(1)}, s32[384,4]{0,1:T(4,128)}, u32[]{:S(2)}) copy-start(s32[384,4]{0,1:T(4,128)} %param.29) | copy-start | bytes 18436
  285.4 59.5 %all-gather.13.cloned.1.call-start = ((), (), s32[]{:S(2)}) async-start(), calls=%async_computation.6 | async-start | bytes 1474560 | tf_op jit(solution)/shard_map/all_gather | solution.py:184
  320.9 83.0 %all-gather.17.cloned.1.call-start = ((), (), s32[]{:S(2)}) async-start(), calls=%async_computation.9 | async-start | bytes 2949120 | tf_op jit(solution)/shard_map/all_gather | solution.py:171
  321.5 116.2 %all-gather.15.cloned.1.call-start = ((), (), s32[]{:S(2)}) async-start(), calls=%async_computation.8 | async-start | bytes 2949120 | tf_op jit(solution)/shard_map/all_gather | solution.py:170
  322.1 149.4 %all-gather.19.cloned.1.call-start = ((), (), s32[]{:S(2)}) async-start(), calls=%async_computation.10 | async-start | bytes 2949120 | tf_op jit(solution)/shard_map/all_gather | solution.py:172
  477.3 10.9 %copy-start.9 = (f32[384,4]{0,1:T(4,128)S(1)}, f32[384,4]{0,1:T(4,128)}, u32[]{:S(2)}) copy-start(f32[384,4]{0,1:T(4,128)} %param.30) | copy-start | bytes 18436
  477.3 41.3 %all-to-all-start.2 = ((bf16[32,18,1536]{2,1,0:T(8,128)(2,1)}), bf16[32,18,1536]{2,1,0:T(8,128)(2,1)}, u32[]{:S(2)}, u32[]{:S(2)}) async-start(bf16[32,18,1536]{2,1,0:T(8,128)(2,1)} %reshape.381), calls=%async_computation.2 | async-start | bytes 4718592 | tf_op jit(solution)/shard_map/all_to_all | solution.py:202
  486.7 92.2 %reduce-scatter.5.cloned.1.call-start = ((), (), s32[]{:S(2)}) async-start(), calls=%async_computation.7 | async-start | bytes 2949120 | tf_op jit(solution)/shard_map/reduce_scatter | solution.py:213
  536.4 44.4 %copy-start.1 = (bf16[16,2,2,128,128]{4,3,2,1,0:T(8,128)(2,1)S(1)}, bf16[16,2,2,128,128]{4,3,2,1,0:T(8,128)(2,1)}, u32[]{:S(2)}) copy-start(bf16[16,2,2,128,128]{4,3,2,1,0:T(8,128)(2,1)} %param.24) | copy-start | bytes 6291460
Sparse Core Ops, SparseCore 0:
  47.9 48.8 all-gather.10
  285.5 27.9 reduce-scatter.6
  321.0 23.8 all-gather.12
  346.4 57.4 all-gather.16
  405.5 32.1 all-gather.14
  439.2 32.1 all-gather.18
  548.7 30.1 reduce-scatter.4

commit v2 on v1

--- a/solution.py
+++ b/solution.py
@@ -91,27 +91,36 @@
     picker = jnp.sum(picker, axis=1).astype(jnp.float32)
     peer_group = (group_of[:, None] == jnp.arange(groups)[None, :]).astype(jnp.float32)
     choose = jnp.einsum("qg,grs->qrs", peer_group, picker).astype(jnp.bfloat16)
+    pair_size = tp_count // KVH
+    half_index = tp_index % pair_size
+    half_rows = page_rows // pair_size
     local_head = lax.dynamic_index_in_dim(prefix_cache, shared_head, axis=2, keepdims=False)
-    flat_cache = local_head.reshape(local_pages, -1)
+    local_half = lax.dynamic_slice_in_dim(local_head, half_index * half_rows, half_rows, 2)
+    flat_cache = local_half.reshape(local_pages, -1)
     outgoing = jnp.einsum(
         "qrs,sx->qrx", choose, flat_cache, preferred_element_type=jnp.float32
     ).astype(jnp.bfloat16)
     incoming = lax.all_to_all(
-        outgoing.reshape(req_count, most_pages, 2, page_rows, HD),
+        outgoing.reshape(req_count, most_pages, 2, half_rows, HD),
         "req",
         split_axis=0,
         concat_axis=0,
         tiled=True,
     )
-    keys_pre = incoming[:, :, 0]
-    values_pre = incoming[:, :, 1]
     my_owners = lax.dynamic_index_in_dim(owner_of, my_group, axis=0, keepdims=False)
     page_count = jnp.sum(my_owners[None, :] == jnp.arange(req_count)[:, None], axis=1)
-    live_slots = jnp.arange(most_pages)[None, :] < page_count[:, None]
-    live_keys = jnp.broadcast_to(
-        live_slots[:, :, None], (req_count, most_pages, page_rows)
-    ).reshape(-1)
-    key_total = req_count * most_pages * page_rows
+    live_count = page_table.shape[1] // most_pages
+    owner_live = page_count > 0
+    live_rank = jnp.cumsum(owner_live.astype(jnp.int32)) - 1
+    live_pick = (live_rank[None, :] == jnp.arange(live_count)[:, None]) & owner_live[None, :]
+    live_owner = jnp.sum(jnp.where(live_pick, jnp.arange(req_count)[None, :], 0), axis=1)
+    compact = jnp.take(incoming, live_owner, axis=0)
+    keys_pre = compact[:, :, 0]
+    values_pre = compact[:, :, 1]
+    pair_perm = [(i, i ^ 1) for i in range(tp_count)]
+    partner_query = lax.ppermute(query_rot, "tp", pair_perm)
+    query_six = jnp.concatenate([query_rot, partner_query], axis=1)
+    key_total = live_count * most_pages * half_rows
     block_len = math.gcd(key_total, 2048)
     block_count = key_total // block_len
     score_scale = 1.0 / math.sqrt(HD)
@@ -121,21 +130,20 @@
     )
     causal = jnp.arange(rows_here)[:, None] >= jnp.arange(rows_here)[None, :]
     scores = jnp.where(causal[:, None, :], scores, MASKED)
-    row_max = jnp.max(scores, axis=2)
-    weights = jnp.exp(scores - row_max[:, :, None])
-    row_sum = jnp.sum(weights, axis=2)
-    weighted = jnp.einsum(
+    suf_max = jnp.max(scores, axis=2)
+    weights = jnp.exp(scores - suf_max[:, :, None])
+    suf_sum = jnp.sum(weights, axis=2)
+    suf_weighted = jnp.einsum(
         "thj,jd->thd", weights.astype(jnp.bfloat16), value_suf, preferred_element_type=jnp.float32
     )
 
     def absorb(running, block_parts):
         old_max, old_sum, old_weighted = running
-        key_block, value_block, valid_block = block_parts
+        key_block, value_block = block_parts
         block_scores = (
-            jnp.einsum("thd,kd->thk", query_rot, key_block, preferred_element_type=jnp.float32)
+            jnp.einsum("thd,kd->thk", query_six, key_block, preferred_element_type=jnp.float32)
             * score_scale
         )
-        block_scores = jnp.where(valid_block[None, None, :], block_scores, MASKED)
         new_max = jnp.maximum(old_max, jnp.max(block_scores, axis=2))
         rescale = jnp.exp(old_max - new_max)
         block_weights = jnp.exp(block_scores - new_max[:, :, None])
@@ -151,9 +159,37 @@
     block_inputs = (
         keys_pre.reshape(block_count, block_len, HD),
         values_pre.reshape(block_count, block_len, HD),
-        live_keys.reshape(block_count, block_len),
-    )
-    (row_max, row_sum, weighted), _ = lax.scan(absorb, (row_max, row_sum, weighted), block_inputs)
+    )
+    gate_full = lax.all_gather(w_gate[0], "tp", axis=1, tiled=True)
+    up_full = lax.all_gather(w_up[0], "tp", axis=1, tiled=True)
+    down_full = lax.all_gather(w_down[0], "tp", axis=0, tiled=True)
+    gate_full, up_full, down_full, block_inputs = lax.optimization_barrier(
+        (gate_full, up_full, down_full, block_inputs)
+    )
+    six = 2 * heads_here
+    start_state = (
+        jnp.full((rows_here, six), MASKED, jnp.float32),
+        jnp.zeros((rows_here, six), jnp.float32),
+        jnp.zeros((rows_here, six, HD), jnp.float32),
+    )
+    (pre_max, pre_sum, pre_weighted), _ = lax.scan(absorb, start_state, block_inputs)
+    back = lax.ppermute(
+        (pre_max[:, heads_here:], pre_sum[:, heads_here:], pre_weighted[:, heads_here:]),
+        "tp",
+        pair_perm,
+    )
+    parts = (
+        (suf_max, suf_sum, suf_weighted),
+        (pre_max[:, :heads_here], pre_sum[:, :heads_here], pre_weighted[:, :heads_here]),
+        back,
+    )
+    row_max = jnp.maximum(jnp.maximum(parts[0][0], parts[1][0]), parts[2][0])
+    row_sum = jnp.zeros_like(row_max)
+    weighted = jnp.zeros_like(suf_weighted)
+    for part_max, part_sum, part_weighted in parts:
+        rescale = jnp.exp(part_max - row_max)
+        row_sum = row_sum + part_sum * rescale
+        weighted = weighted + part_weighted * rescale[:, :, None]
     attention = (
         (weighted / row_sum[:, :, None]).astype(jnp.bfloat16).reshape(rows_here, heads_here * HD)
     )
@@ -167,9 +203,6 @@
     expert_count = w_gate.shape[0] * req_count
     capacity = 3 * rows_here * TOP // (2 * expert_count)
     sub = capacity // tp_count
-    gate_full = lax.all_gather(w_gate[0], "tp", axis=1, tiled=True)
-    up_full = lax.all_gather(w_up[0], "tp", axis=1, tiled=True)
-    down_full = lax.all_gather(w_down[0], "tp", axis=0, tiled=True)
     onehot_exp = (
         (expert_ids[:, :, None] == jnp.arange(expert_count)[None, None, :])
         .astype(jnp.int32)

time: 589 us -> 473 us (0.80)
  waiting for transfers between devices: 253 us -> 201 us
  matrix products: 85.1 us -> 55.1 us
  blocking collectives: 91.6 us -> 66.8 us
  local copies, waits for them, and re-layouts: 69.4 us -> 55.4 us
    all_to_all x1, waiting for transfers between devices: 91.2 us -> 23.6 us  [body(): lax.all_to_all(outgoing.reshape(req_count, most_pages, 2, half_rows, HD),...]
    all_gather x1, waiting for transfers between devices: 4.72 us -> 33.9 us  [body(): up_full = lax.all_gather(w_up[0], 'tp', axis=1, tiled=True)]
    unnamed x1, blocking collectives: 45.2 us -> 20.5 us
    dot_general x8 -> x2, matrix products: 37.8 us -> 16.4 us  [absorb(): jnp.einsum('thk,kd->thd', block_weights.astype(jnp.bfloat16), value_block...]
    all_gather x1, waiting for transfers between devices: 29.2 us -> 12.8 us  [body(): gate_full = lax.all_gather(w_gate[0], 'tp', axis=1, tiled=True)]
    reshape x2, local copies, waits for them, and re-layouts: 10.8 us -> 3.16 us  [the longest x1 2.94 us: body(): outgoing.reshape(req_count, most_pages, 2, half_rows, HD)]
    all_gather x1, waiting for transfers between devices: 26.8 us -> 33.7 us  [body(): down_full = lax.all_gather(w_down[0], 'tp', axis=0, tiled=True)]
    unnamed x34 -> x46, local copies, waits for them, and re-layouts: 13.9 us -> 8.45 us
  transfers between devices with their start and end apart: 9 -> 13, of which waited for: 8 -> 10; matrix products, arithmetic and copies ran while one was open for 9% -> 9% of each run, Pallas kernels for 0% -> 0%
where the time goes in v2:
time: 473 us; the launch traced here: 467 us
  waiting for transfers between devices  201 us (42%)
  blocking collectives  66.8 us (14%)
  local copies, waits for them, and re-layouts  55.4 us (12%)
  matrix products  55.1 us (12%)
  other arithmetic  53.2 us (11%)
  starting transfers between devices  18.3 us (4%)
  between operations  17.1 us (4%)
    all_to_all x1, blocking collectives, body(): lax.all_to_all(outgoing_rows, 'req', split_axis=0, concat_axis=0, tiled=T...  41.2 us
    all_gather x1, waiting for transfers between devices, body(): up_full = lax.all_gather(w_up[0], 'tp', axis=1, tiled=True)  33.9 us
    all_gather x1, waiting for transfers between devices, body(): down_full = lax.all_gather(w_down[0], 'tp', axis=0, tiled=True)  33.7 us
    all_to_all x1, waiting for transfers between devices, body(): lax.all_to_all(expert_out.reshape(src_count, item_count, width_all), 'req...  29.5 us
    reduce_scatter x1, waiting for transfers between devices, body(): moe_part = lax.psum_scatter(moe_full, 'tp', scatter_dimension=1, tiled=True)  29.1 us
    unnamed x8, waiting for transfers between devices  24.8 us
    all_to_all x1, waiting for transfers between devices, body(): lax.all_to_all(outgoing.reshape(req_count, most_pages, 2, half_rows, HD),...  23.6 us
    unnamed x1, blocking collectives  20.5 us
  transfers between devices with their start and end apart: 13, of which 10 were waited for; matrix products, arithmetic and copies ran while one was open for 9% of the time, Pallas kernels for 0%

profile of v2, /device:TPU:1, one launch (start us, length us, event | category | flops | bytes accessed | tf_op | source)
XLA Modules:
  0.0 466.7 jit_solution(9775277659254078058)
XLA Ops:
  6.5 0.7 all-gather.11.cloned.1.call-update
  7.3 0.7 all-gather.15.cloned.1.call-update
  8.1 0.7 all-gather.17.cloned.1.call-update
  9.5 0.6 multiply_reduce_fusion.2
  10.2 3.2 convolution_convert_fusion
  13.3 3.4 copy.115
  16.8 2.9 copy.89
  19.7 11.4 %all-to-all-start = ((bf16[32,4,2,64,128]{4,3,2,1,0:T(8,128)(2,1)}), bf16[32,4,2,64,128]{4,3,2,1,0:T(8,128)(2,1)}, u32[]{:S(2)}, u32[]{:S(2)}) async-start(bf16[32,4,2,64,128]{4,3,2,1,0:T(8,128)(2,1)} %copy.89), calls=%async_computation | async-start | bytes 8388608 | tf_op jit(solution)/shard_map/all_to_all | solution.py:103
  31.2 0.5 all-gather.19.cloned.1.call-update
  31.7 0.6 dynamic_slice.27
  34.6 20.5 %all-gather.4 = f32[4,1,384]{2,1,0:T(1,128)S(1)} all-gather(f32[1,1,384]{2,1,0:T(1,128)S(1)} %reshape.450), channel_id=2, replica_groups=mesh['req'=32,'tp'=4] {'tp'}, dimensions={0}, use_global_device_ids=true | all-gather | bytes 7680 | tf_op args[1]
  55.5 0.8 multiply_cosine_fusion
  56.2 1.9 constant_dynamic-slice_fusion.2
  58.2 1.6 fusion.18
  59.8 2.5 fusion.39
  63.2 0.7 collective-permute-start
  64.4 0.7 fusion.30
  65.2 0.4 fusion.49
  66.1 23.6 %all-to-all-done = bf16[32,4,2,64,128]{4,3,2,1,0:T(8,128)(2,1)} async-done(((bf16[32,4,2,64,128]{4,3,2,1,0:T(8,128)(2,1)}), bf16[32,4,2,64,128]{4,3,2,1,0:T(8,128)(2,1)}, u32[]{:S(2)}, u32[]{:S(2)}) %all-to-all-start) | async-done | bytes 4194336 | tf_op jit(solution)/shard_map/all_to_all | solution.py:103
  89.6 4.4 gather_fusion
  94.0 1.9 broadcast_select_fusion.1
  95.9 1.1 fusion.88
  97.0 12.8 %all-gather.15.cloned.1.call-done = bf16[1,1536,768]{1,2,0:T(8,128)(2,1)} async-done(((bf16[1,1536,192]{1,2,0:T(8,128)(2,1)}), bf16[1,1536,768]{1,2,0:T(8,128)(2,1)}) %all-gather.15.cloned.1.call-update) | async-done | bytes 2359312 | tf_op jit(solution)/shard_map/all_gather | solution.py:163
  109.8 33.9 %all-gather.17.cloned.1.call-done = bf16[1,1536,768]{1,2,0:T(8,128)(2,1)} async-done(((bf16[1,1536,192]{1,2,0:T(8,128)(2,1)}), bf16[1,1536,768]{1,2,0:T(8,128)(2,1)}) %all-gather.17.cloned.1.call-update) | async-done | bytes 2359312 | tf_op jit(solution)/shard_map/all_gather | solution.py:164
  143.7 33.7 %all-gather.19.cloned.1.call-done = bf16[1,768,1536]{2,1,0:T(8,128)(2,1)} async-done(((bf16[1,192,1536]{2,1,0:T(8,128)(2,1)}), bf16[1,768,1536]{2,1,0:T(8,128)(2,1)}) %all-gather.19.cloned.1.call-update) | async-done | bytes 2359312 | tf_op jit(solution)/shard_map/all_gather | solution.py:165
  177.5 55.5 %while.15 = (s32[]{:T(128)}, f32[384,6]{0,1:T(8,128)S(1)}, f32[384,6]{0,1:T(8,128)S(1)}, f32[384,6,128]{2,0,1:T(8,128)S(1)}, bf16[2,2048,128]{2,1,0:T(8,128)(2,1...) while((s32[]{:T(128)}, f32[384,6]{0,1:T(8,128)S(1)}, ...), condition=%wide.region_10.11_spmd.clone, body=%wide.region_7.10_spmd.clone.sunk | while | flops 2454564096 | bytes 60774516 | solution.py:175
  177.5 10.1 %bitcast_reduce_fusion.2 = (f32[384,6]{0,1:T(8,128)S(1)}, f32[2048,384,6]{1,0,2:T(8,128)}) fusion(bf16[384,6,128]{2,0,1:T(8,128)(2,1)S(1)} %get-tuple-element.201, bf16[2,2048,128]{2,1,0:T(8,128)(2,1)} %get-tuple-element.200, s32[]{:T(128)S(6)} %copy.125), kind=kOutput, calls=%fused_computation.4.clone.1 | convolution fusion | flops 1217394432 | bytes 19997700 | tf_op jit(solution)/shard_map/while/body/eval_jaxpr/thd,kd->thk/dot_general | solution.py:144
  187.6 9.4 %fusion.112 = f32[384,6]{0,1:T(8,128)S(1)} fusion(f32[2048,384,6]{1,0,2:T(8,128)} %get-tuple-element.175, f32[384,6]{0,1:T(8,128)S(1)} %select_maximum_fusion.2), kind=kLoop, calls=%fused_computation.7.clone.1 | loop fusion | flops 14153472 | bytes 18892800 | tf_op jit(solution)/shard_map/while/body/eval_jaxpr/reduce_sum | solution.py:150
  197.1 8.2 %fusion.114 = f32[384,6,128]{2,0,1:T(8,128)S(1)} fusion(f32[2048,384,6]{1,0,2:T(8,128)} %get-tuple-element.175, f32[384,6]{0,1:T(8,128)S(1)} %select_maximum_fusion.2, f32[384,6,128]{2,0,1:T(8,128)S(1)} %get-tuple-element.190, f32[384,6]{0,1:T(8,128)S(1)} %get-tuple-element.177, pred[]{:T(512)S(6)} %compare.13, ...), kind=kOutput, calls=%fused_computation.9.clone.1 | convolution fusion | flops 1223000064 | bytes 21782532 | tf_op jit(solution)/shard_map/while/body/eval_jaxpr/thk,kd->thd/dot_general | solution.py:151
  205.3 10.1 %bitcast_reduce_fusion.2 = (f32[384,6]{0,1:T(8,128)S(1)}, f32[2048,384,6]{1,0,2:T(8,128)}) fusion(bf16[384,6,128]{2,0,1:T(8,128)(2,1)S(1)} %get-tuple-element.201, bf16[2,2048,128]{2,1,0:T(8,128)(2,1)} %get-tuple-element.200, s32[]{:T(128)S(6)} %copy.125), kind=kOutput, calls=%fused_computation.4.clone.1 | convolution fusion | flops 1217394432 | bytes 19997700 | tf_op jit(solution)/shard_map/while/body/eval_jaxpr/thd,kd->thk/dot_general | solution.py:144
  215.4 9.4 %fusion.112 = f32[384,6]{0,1:T(8,128)S(1)} fusion(f32[2048,384,6]{1,0,2:T(8,128)} %get-tuple-element.175, f32[384,6]{0,1:T(8,128)S(1)} %select_maximum_fusion.2), kind=kLoop, calls=%fused_computation.7.clone.1 | loop fusion | flops 14153472 | bytes 18892800 | tf_op jit(solution)/shard_map/while/body/eval_jaxpr/reduce_sum | solution.py:150
  224.8 8.2 %fusion.114 = f32[384,6,128]{2,0,1:T(8,128)S(1)} fusion(f32[2048,384,6]{1,0,2:T(8,128)} %get-tuple-element.175, f32[384,6]{0,1:T(8,128)S(1)} %select_maximum_fusion.2, f32[384,6,128]{2,0,1:T(8,128)S(1)} %get-tuple-element.190, f32[384,6]{0,1:T(8,128)S(1)} %get-tuple-element.177, pred[]{:T(512)S(6)} %compare.13, ...), kind=kOutput, calls=%fused_computation.9.clone.1 | convolution fusion | flops 1223000064 | bytes 21782532 | tf_op jit(solution)/shard_map/while/body/eval_jaxpr/thk,kd->thd/dot_general | solution.py:151
  233.6 0.4 copy-done.5
  234.0 0.5 fusion.21
  234.7 0.6 collective-permute-start.1
  236.2 0.7 fusion.37
  236.8 0.6 copy-done.6
  237.4 0.8 convolution_convert_fusion.1
  238.2 1.4 copy.111
  239.7 22.1 %reduce-scatter.7.cloned.1.call-done = bf16[384,384]{1,0:T(8,128)(2,1)} async-done(((bf16[1536,384]{1,0:T(8,128)(2,1)}), bf16[384,384]{1,0:T(8,128)(2,1)}) %reduce-scatter.7.cloned.1.call-update) | async-done | bytes 294928
  261.8 1.2 copy.112
  263.2 5.1 %psum.7 = f32[384]{0:T(512)S(1)} all-reduce(f32[384]{0:T(512)S(1)} %multiply_reduce_fusion.1), channel_id=1, replica_groups=mesh['req'=32,'tp'=4] {'tp'}, use_global_device_ids=true, to_apply=%region_18.19 | all-reduce | flops 384 | bytes 3072 | tf_op jit(solution)/shard_map/psum | solution.py:201
  268.3 0.8 multiply_convert_fusion.1
  269.7 9.1 %reduce-window.19 = s32[32,12,128]{2,1,0:T(8,128)S(1)} reduce-window(s32[32,12,128]{2,1,0:T(8,128)S(1)} %fusion.41, s32[]{:T(128)} %constant.206.clone.1), window={size=1x1x128 pad=0_0x0_0x127_0}, to_apply=%region_13.14 | reduce-window | flops 6242304 | bytes 393220 | tf_op jit(solution)/shard_map/reduce-window.1
  279.5 0.8 select_reduce_fusion
  280.4 12.9 %all-gather.13.cloned.1.call-done = bf16[384,1536]{1,0:T(8,128)(2,1)} async-done(((bf16[384,384]{1,0:T(8,128)(2,1)}), bf16[384,1536]{1,0:T(8,128)(2,1)}) %all-gather.13.cloned.1.call-update) | async-done | bytes 1179664 | tf_op jit(solution)/shard_map/all_gather | solution.py:217
  293.3 6.7 %gather_fusion.1 = bf16[576,1536]{1,0:T(8,128)(2,1)S(1)} fusion(bf16[384,1536]{1,0:T(8,128)(2,1)} %all-gather.13.cloned.1.call-done, s32[1024]{0:T(1024)S(1)} %pad_clamp_fusion.1), kind=kCustom, calls=%fused_computation.1 | custom fusion | bytes 3541248 | tf_op jit(solution)/shard_map/jit(_take)/gather | solution.py:218
  300.0 1.7 gather.18
  301.7 1.9 broadcast_select_fusion
  303.7 41.2 %all_to_all.15 = bf16[32,18,1536]{2,1,0:T(8,128)(2,1)} all-to-all(bf16[32,18,1536]{2,1,0:T(8,128)(2,1)S(1)} %broadcast_select_fusion), channel_id=1, replica_groups=mesh['req'=32,'tp'=4] {'req'}, dimensions={0} | all-to-all | bytes 3538944 | tf_op jit(solution)/shard_map/all_to_all | solution.py:221
  344.9 2.6 reshape.417
  347.5 3.4 fusion.90
  350.9 2.5 multiply_convert_fusion
  353.5 2.2 copy.105
  355.7 4.2 convert_reduce_fusion
  359.9 1.7 reshape.420
  361.6 5.1 %all-to-all-start.2 = ((bf16[32,18,1536]{2,1,0:T(8,128)(2,1)}), bf16[32,18,1536]{2,1,0:T(8,128)(2,1)}, u32[]{:S(2)}, u32[]{:S(2)}) async-start(bf16[32,18,1536]{2,1,0:T(8,128)(2,1)} %reshape.420), calls=%async_computation.2 | async-start | bytes 4718592 | tf_op jit(solution)/shard_map/all_to_all | solution.py:235
  368.5 29.5 %all-to-all-done.2 = bf16[32,18,1536]{2,1,0:T(8,128)(2,1)} async-done(((bf16[32,18,1536]{2,1,0:T(8,128)(2,1)}), bf16[32,18,1536]{2,1,0:T(8,128)(2,1)}, u32[]{:S(2)}, u32[]{:S(2)}) %all-to-all-start.2) | async-done | bytes 1769504 | tf_op jit(solution)/shard_map/all_to_all | solution.py:235
  398.0 2.6 reshape.421
  400.6 6.3 %gather_fusion.2 = bf16[1536,1536]{1,0:T(8,128)(2,1)} fusion(bf16[576,1536]{1,0:T(8,128)(2,1)S(1)} %reshape.421, s32[2048]{0:T(1024)S(1)} %pad_clamp_fusion), kind=kCustom, calls=%fused_computation.2 | custom fusion | bytes 9443328 | tf_op jit(solution)/shard_map/jit(_take)/gather | solution.py:243
  406.9 8.8 %gather.20 = bf16[384,4,1536]{2,1,0:T(4,128)(2,1)} reshape(bf16[1536,1536]{1,0:T(8,128)(2,1)} %gather_fusion.2) | data formatting | bytes 9437184 | tf_op jit(solution)/shard_map/jit(_take)/gather | solution.py:243
  415.8 12.2 %multiply_reduce_fusion = f32[384,1536]{1,0:T(8,128)} fusion(bf16[384,4,1536]{2,1,0:T(4,128)(2,1)} %gather.20, f32[384,4]{1,0:T(8,128)S(1)} %copy.100, pred[384,4]{1,0:T(8,128)(4,1)S(1)} %copy.104), kind=kLoop, calls=%fused_computation.24 | loop fusion | flops 8847360 | bytes 7085568 | tf_op jit(solution)/shard_map/reduce_sum | solution.py:245
  428.6 29.1 %reduce-scatter.5.cloned.1.call-done = f32[384,384]{1,0:T(8,128)} async-done(((f32[384,1536]{1,0:T(8,128)}), f32[384,384]{1,0:T(8,128)}) %reduce-scatter.5.cloned.1.call-update) | async-done | bytes 589840 | tf_op jit(solution)/shard_map/reduce_scatter | solution.py:246
  457.7 1.9 select_convert_fusion
  (134 shorter events, 8.0 us)
Async XLA Ops:
  6.5 2.2 copy-start
  6.5 2.7 copy-start.13
  6.5 3.6 copy-start.17
  6.5 51.6 %all-gather.11.cloned.1.call-start = ((), (), s32[]{:S(2)}) async-start(), calls=%async_computation.5 | async-start | bytes 1474560 | tf_op jit(solution)/shard_map/all_gather | solution.py:63
  7.3 102.6 %all-gather.15.cloned.1.call-start = ((), (), s32[]{:S(2)}) async-start(), calls=%async_computation.8 | async-start | bytes 2949120 | tf_op jit(solution)/shard_map/all_gather | solution.py:163
  8.0 135.7 %all-gather.17.cloned.1.call-start = ((), (), s32[]{:S(2)}) async-start(), calls=%async_computation.9 | async-start | bytes 2949120 | tf_op jit(solution)/shard_map/all_gather | solution.py:164
  19.7 14.9 %copy-start.16 = (f32[384]{0:T(512)S(1)}, f32[384]{0:T(512)}, u32[]{:S(2)}) copy-start(f32[384]{0:T(512)} %param.19) | copy-start | bytes 4612
  19.7 36.5 %copy-start.9 = (bf16[1536,256]{1,0:T(8,128)(2,1)S(1)}, bf16[1536,256]{1,0:T(8,128)(2,1)}, u32[]{:S(2)}) copy-start(bf16[1536,256]{1,0:T(8,128)(2,1)} %param.22) | copy-start | bytes 2359300
  19.7 69.9 %all-to-all-start = ((bf16[32,4,2,64,128]{4,3,2,1,0:T(8,128)(2,1)}), bf16[32,4,2,64,128]{4,3,2,1,0:T(8,128)(2,1)}, u32[]{:S(2)}, u32[]{:S(2)}) async-start(bf16[32,4,2,64,128]{4,3,2,1,0:T(8,128)(2,1)} %copy.89), calls=%async_computation | async-start | bytes 8388608 | tf_op jit(solution)/shard_map/all_to_all | solution.py:103
  31.1 146.4 %all-gather.19.cloned.1.call-start = ((), (), s32[]{:S(2)}) async-start(), calls=%async_computation.10 | async-start | bytes 2949120 | tf_op jit(solution)/shard_map/all_gather | solution.py:165
  31.7 230.1 %reduce-scatter.7.cloned.1.call-start = ((), (), s32[]{:S(2)}) async-start(), calls=%async_computation.11 | async-start | bytes 1474560
  62.8 1.3 copy-start.3
  62.8 1.5 copy-start.7
  62.8 1.6 copy-start.8
  63.2 2.0 copy-start.4
  63.2 2.4 collective-permute-start
  65.1 0.7 copy-start.10
  233.0 1.0 copy-start.5
  233.5 2.7 collective-permute-start.2
  234.0 2.1 copy-start.11
  234.5 1.2 collective-permute-start.3
  234.7 1.4 collective-permute-start.1
  236.1 1.3 copy-start.6
  238.2 24.8 %copy-start.2 = (bf16[384,384]{1,0:T(8,128)(2,1)S(1)}, bf16[384,384]{1,0:T(8,128)(2,1)}, u32[]{:S(2)}) copy-start(bf16[384,384]{1,0:T(8,128)(2,1)} %param.18) | copy-start | bytes 884740
  238.2 30.1 %copy-start.15 = (f32[384]{0:T(512)S(1)}, f32[384]{0:T(512)}, u32[]{:S(2)}) copy-start(f32[384]{0:T(512)} %param.28) | copy-start | bytes 4612
  239.6 29.6 %copy-start.12 = (s32[384,4]{0,1:T(4,128)S(1)}, s32[384,4]{0,1:T(4,128)}, u32[]{:S(2)}) copy-start(s32[384,4]{0,1:T(4,128)} %param.29) | copy-start | bytes 18436
  239.7 53.7 %all-gather.13.cloned.1.call-start = ((), (), s32[]{:S(2)}) async-start(), calls=%async_computation.6 | async-start | bytes 1474560 | tf_op jit(solution)/shard_map/all_gather | solution.py:217
  347.5 3.4 copy-start.18
  361.6 6.5 %copy-start.14 = (f32[384,4]{0,1:T(4,128)S(1)}, f32[384,4]{0,1:T(4,128)}, u32[]{:S(2)}) copy-start(f32[384,4]{0,1:T(4,128)} %param.30) | copy-start | bytes 18436
  361.6 36.4 %all-to-all-start.2 = ((bf16[32,18,1536]{2,1,0:T(8,128)(2,1)}), bf16[32,18,1536]{2,1,0:T(8,128)(2,1)}, u32[]{:S(2)}, u32[]{:S(2)}) async-start(bf16[32,18,1536]{2,1,0:T(8,128)(2,1)} %reshape.420), calls=%async_computation.2 | async-start | bytes 4718592 | tf_op jit(solution)/shard_map/all_to_all | solution.py:235
  366.7 91.0 %reduce-scatter.5.cloned.1.call-start = ((), (), s32[]{:S(2)}) async-start(), calls=%async_computation.7 | async-start | bytes 2949120 | tf_op jit(solution)/shard_map/reduce_scatter | solution.py:246
  415.8 43.8 %copy-start.1 = (bf16[16,2,2,128,128]{4,3,2,1,0:T(8,128)(2,1)S(1)}, bf16[16,2,2,128,128]{4,3,2,1,0:T(8,128)(2,1)}, u32[]{:S(2)}) copy-start(bf16[16,2,2,128,128]{4,3,2,1,0:T(8,128)(2,1)} %param.24) | copy-start | bytes 6291460
Sparse Core Ops, SparseCore 0:
  9.0 26.3 all-gather.10
  37.1 72.6 all-gather.14
  111.5 32.1 all-gather.16
  145.2 32.1 all-gather.18
  239.8 22.0 reduce-scatter.6
  269.3 23.9 all-gather.12
  428.1 29.5 reduce-scatter.4

commit v3 on v2

--- a/solution.py
+++ b/solution.py
@@ -163,8 +163,22 @@
     gate_full = lax.all_gather(w_gate[0], "tp", axis=1, tiled=True)
     up_full = lax.all_gather(w_up[0], "tp", axis=1, tiled=True)
     down_full = lax.all_gather(w_down[0], "tp", axis=0, tiled=True)
-    gate_full, up_full, down_full, block_inputs = lax.optimization_barrier(
-        (gate_full, up_full, down_full, block_inputs)
+    expert_count = w_gate.shape[0] * req_count
+    capacity = 3 * rows_here * TOP // (2 * expert_count)
+    sub = capacity // tp_count
+    onehot_exp = (
+        (expert_ids[:, :, None] == jnp.arange(expert_count)[None, None, :])
+        .astype(jnp.int32)
+        .reshape(rows_here * TOP, expert_count)
+    )
+    pair_rank = jnp.sum(jnp.cumsum(onehot_exp, axis=0) * onehot_exp, axis=1) - 1
+    mine = (pair_rank // sub) == tp_index
+    send_pos = expert_ids.reshape(-1) * sub + pair_rank % sub
+    pair_token = jnp.arange(rows_here * TOP) // TOP
+    slot_match = (send_pos[None, :] == jnp.arange(expert_count * sub)[:, None]) & mine[None, :]
+    slot_token = jnp.sum(jnp.where(slot_match, pair_token[None, :], 0), axis=1)
+    slot_token, send_pos, mine, block_inputs = lax.optimization_barrier(
+        (slot_token, send_pos, mine, block_inputs)
     )
     six = 2 * heads_here
     start_state = (
@@ -173,6 +187,9 @@
         jnp.zeros((rows_here, six, HD), jnp.float32),
     )
     (pre_max, pre_sum, pre_weighted), _ = lax.scan(absorb, start_state, block_inputs)
+    gate_full, up_full, down_full, pre_max, pre_sum, pre_weighted = lax.optimization_barrier(
+        (gate_full, up_full, down_full, pre_max, pre_sum, pre_weighted)
+    )
     back = lax.ppermute(
         (pre_max[:, heads_here:], pre_sum[:, heads_here:], pre_weighted[:, heads_here:]),
         "tp",
@@ -200,20 +217,6 @@
     residual = hidden + attn_slice
     sq_mid = lax.psum(jnp.sum(residual * residual, axis=1), "tp")
     moe_in = (residual * lax.rsqrt(sq_mid / D + EPSILON)[:, None] * norm_moe).astype(jnp.bfloat16)
-    expert_count = w_gate.shape[0] * req_count
-    capacity = 3 * rows_here * TOP // (2 * expert_count)
-    sub = capacity // tp_count
-    onehot_exp = (
-        (expert_ids[:, :, None] == jnp.arange(expert_count)[None, None, :])
-        .astype(jnp.int32)
-        .reshape(rows_here * TOP, expert_count)
-    )
-    pair_rank = jnp.sum(jnp.cumsum(onehot_exp, axis=0) * onehot_exp, axis=1) - 1
-    mine = (pair_rank // sub) == tp_index
-    send_pos = expert_ids.reshape(-1) * sub + pair_rank % sub
-    pair_token = jnp.arange(rows_here * TOP) // TOP
-    slot_match = (send_pos[None, :] == jnp.arange(expert_count * sub)[:, None]) & mine[None, :]
-    slot_token = jnp.sum(jnp.where(slot_match, pair_token[None, :], 0), axis=1)
     full_rows = lax.all_gather(moe_in, "tp", axis=1, tiled=True)
     outgoing_rows = jnp.take(full_rows, slot_token, axis=0).reshape(
         req_count, sub, full_rows.shape[1]

time: 473 us -> 412 us (0.87)
  waiting for transfers between devices: 201 us -> 146 us
    all_gather x1, waiting for transfers between devices: 33.9 us -> 0.02 us  [body(): up_full = lax.all_gather(w_up[0], 'tp', axis=1, tiled=True)]
    all_gather x1, waiting for transfers between devices: 12.8 us -> 0.02 us  [body(): gate_full = lax.all_gather(w_gate[0], 'tp', axis=1, tiled=True)]
    all_gather x1, waiting for transfers between devices: 12.9 us -> 23.9 us  [body(): full_rows = lax.all_gather(moe_in, 'tp', axis=1, tiled=True)]
    all_to_all x1, waiting for transfers between devices: 23.6 us -> 13.2 us  [body(): lax.all_to_all(outgoing.reshape(req_count, most_pages, 2, half_rows, HD),...]
    all_gather x1, waiting for transfers between devices: 33.7 us -> 24.3 us  [body(): down_full = lax.all_gather(w_down[0], 'tp', axis=0, tiled=True)]
  transfers between devices with their start and end apart: 13 -> 13, of which waited for: 10 -> 8; matrix products, arithmetic and copies ran while one was open for 9% -> 24% of each run, Pallas kernels for 0% -> 0%
where the time goes in v3:
time: 412 us; the launch traced here: 410 us
  waiting for transfers between devices  146 us (35%)
  blocking collectives  66.1 us (16%)
  matrix products  55.5 us (13%)
  local copies, waits for them, and re-layouts  54.4 us (13%)
  other arithmetic  53.2 us (13%)
  starting transfers between devices  18.2 us (4%)
  between operations  16.8 us (4%)
    all_to_all x1, blocking collectives, body(): lax.all_to_all(outgoing_rows, 'req', split_axis=0, concat_axis=0, tiled=T...  41.3 us
    all_to_all x1, waiting for transfers between devices, body(): lax.all_to_all(expert_out.reshape(src_count, item_count, width_all), 'req...  30.2 us
    reduce_scatter x1, waiting for transfers between devices, body(): moe_part = lax.psum_scatter(moe_full, 'tp', scatter_dimension=1, tiled=True)  29.1 us
    unnamed x8, waiting for transfers between devices  24.8 us
    all_gather x1, waiting for transfers between devices, body(): down_full = lax.all_gather(w_down[0], 'tp', axis=0, tiled=True)  24.3 us
    all_gather x1, waiting for transfers between devices, body(): full_rows = lax.all_gather(moe_in, 'tp', axis=1, tiled=True)  23.9 us
    dot_general x2, matrix products, absorb(): jnp.einsum('thd,kd->thk', query_six, key_block, preferred_element_type=jn...  20.3 us
    unnamed x1, blocking collectives  19.7 us
  transfers between devices with their start and end apart: 13, of which 8 were waited for; matrix products, arithmetic and copies ran while one was open for 24% of the time, Pallas kernels for 0%

profile of v3, /device:TPU:1, one launch (start us, length us, event | category | flops | bytes accessed | tf_op | source)
XLA Modules:
  0.0 410.4 jit_solution(15709151476179834076)
XLA Ops:
  6.5 0.7 all-gather.11.cloned.1.call-update
  7.3 0.7 all-gather.15.cloned.1.call-update
  8.1 0.7 all-gather.17.cloned.1.call-update
  9.5 0.6 multiply_reduce_fusion.2
  10.2 3.2 convolution_convert_fusion
  13.3 3.4 copy.97
  16.8 2.9 copy.83
  19.7 11.4 %all-to-all-start = ((bf16[32,4,2,64,128]{4,3,2,1,0:T(8,128)(2,1)}), bf16[32,4,2,64,128]{4,3,2,1,0:T(8,128)(2,1)}, u32[]{:S(2)}, u32[]{:S(2)}) async-start(bf16[32,4,2,64,128]{4,3,2,1,0:T(8,128)(2,1)} %copy.83), calls=%async_computation | async-start | bytes 8388608 | tf_op jit(solution)/shard_map/all_to_all | solution.py:103
  31.2 0.5 all-gather.19.cloned.1.call-update
  32.3 0.6 dynamic_slice.27
  35.4 19.7 %all-gather.4 = f32[4,1,384]{2,1,0:T(1,128)S(1)} all-gather(f32[1,1,384]{2,1,0:T(1,128)S(1)} %reshape.380), channel_id=2, replica_groups=mesh['req'=32,'tp'=4] {'tp'}, dimensions={0}, use_global_device_ids=true | all-gather | bytes 7680 | tf_op args[1]
  55.1 9.1 %reduce-window.18 = s32[32,12,128]{2,1,0:T(8,128)S(1)} reduce-window(s32[32,12,128]{2,1,0:T(8,128)S(1)} %fusion.41, s32[]{:T(128)} %constant.206.clone.1), window={size=1x1x128 pad=0_0x0_0x127_0}, to_apply=%region_2.3 | reduce-window | flops 6242304 | bytes 393220 | tf_op jit(solution)/shard_map/reduce-window
  65.0 0.8 select_reduce_fusion
  65.8 0.8 multiply_cosine_fusion
  66.5 2.1 constant_dynamic-slice_fusion.2
  68.6 1.6 fusion.18
  70.2 2.5 fusion.39
  73.6 0.4 collective-permute-start
  74.0 0.5 copy-done.3
  74.8 0.7 fusion.30
  75.6 0.4 fusion.49
  76.5 13.2 %all-to-all-done = bf16[32,4,2,64,128]{4,3,2,1,0:T(8,128)(2,1)} async-done(((bf16[32,4,2,64,128]{4,3,2,1,0:T(8,128)(2,1)}), bf16[32,4,2,64,128]{4,3,2,1,0:T(8,128)(2,1)}, u32[]{:S(2)}, u32[]{:S(2)}) %all-to-all-start) | async-done | bytes 4194336 | tf_op jit(solution)/shard_map/all_to_all | solution.py:103
  89.6 4.4 %gather_fusion = bf16[16,4,2,64,128]{4,3,2,1,0:T(8,128)(2,1)} fusion(bf16[32,4,2,64,128]{4,3,2,1,0:T(8,128)(2,1)} %all-to-all-done, s32[1024]{0:T(1024)S(1)} %pad_clamp_fusion.2), kind=kCustom, calls=%fused_computation | custom fusion | bytes 4194368 | tf_op jit(solution)/shard_map/jit(_take)/gather | solution.py:117
  94.0 1.9 broadcast_select_fusion.1
  95.9 1.1 fusion.83
  97.0 56.1 %while.15 = (s32[]{:T(128)}, f32[384,6]{0,1:T(8,128)S(1)}, f32[384,6]{0,1:T(8,128)S(1)}, f32[384,6,128]{2,0,1:T(8,128)S(1)}, bf16[2,2048,128]{2,1,0:T(8,128)(2,1...) while((s32[]{:T(128)}, f32[384,6]{0,1:T(8,128)S(1)}, ...), condition=%wide.region_14.15_spmd.clone, body=%wide.region_11.14_spmd.clone.sunk | while | flops 2454564096 | bytes 60775016 | solution.py:189
  97.0 10.1 %bitcast_reduce_fusion.2 = (f32[384,6]{0,1:T(8,128)S(1)}, f32[2048,384,6]{1,0,2:T(8,128)}) fusion(bf16[384,6,128]{2,0,1:T(8,128)(2,1)S(1)} %get-tuple-element.209, bf16[2,2048,128]{2,1,0:T(8,128)(2,1)} %get-tuple-element.208, s32[]{:T(128)} %get-tuple-element.195), kind=kOutput, calls=%fused_computation.4.clone.1 | convolution fusion | flops 1217394432 | bytes 19998208 | tf_op jit(solution)/shard_map/while/body/eval_jaxpr/thd,kd->thk/dot_general | solution.py:144
  107.1 9.4 %fusion.107 = f32[384,6]{0,1:T(8,128)S(1)} fusion(f32[2048,384,6]{1,0,2:T(8,128)} %get-tuple-element.183, f32[384,6]{0,1:T(8,128)S(1)} %select_maximum_fusion.2), kind=kLoop, calls=%fused_computation.7.clone.1 | loop fusion | flops 14153472 | bytes 18892800 | tf_op jit(solution)/shard_map/while/body/eval_jaxpr/reduce_sum | solution.py:150
  116.6 8.6 %fusion.109 = f32[384,6,128]{2,0,1:T(8,128)S(1)} fusion(f32[2048,384,6]{1,0,2:T(8,128)} %get-tuple-element.183, f32[384,6]{0,1:T(8,128)S(1)} %select_maximum_fusion.2, f32[384,6,128]{2,0,1:T(8,128)S(1)} %get-tuple-element.198, f32[384,6]{0,1:T(8,128)S(1)} %get-tuple-element.185, pred[]{:T(512)S(6)} %compare.13, ...), kind=kOutput, calls=%fused_computation.9.clone.1 | convolution fusion | flops 1223000064 | bytes 21782532 | tf_op jit(solution)/shard_map/while/body/eval_jaxpr/thk,kd->thd/dot_general | solution.py:151
  125.2 10.1 %bitcast_reduce_fusion.2 = (f32[384,6]{0,1:T(8,128)S(1)}, f32[2048,384,6]{1,0,2:T(8,128)}) fusion(bf16[384,6,128]{2,0,1:T(8,128)(2,1)S(1)} %get-tuple-element.209, bf16[2,2048,128]{2,1,0:T(8,128)(2,1)} %get-tuple-element.208, s32[]{:T(128)} %get-tuple-element.195), kind=kOutput, calls=%fused_computation.4.clone.1 | convolution fusion | flops 1217394432 | bytes 19998208 | tf_op jit(solution)/shard_map/while/body/eval_jaxpr/thd,kd->thk/dot_general | solution.py:144
  135.3 9.5 %fusion.107 = f32[384,6]{0,1:T(8,128)S(1)} fusion(f32[2048,384,6]{1,0,2:T(8,128)} %get-tuple-element.183, f32[384,6]{0,1:T(8,128)S(1)} %select_maximum_fusion.2), kind=kLoop, calls=%fused_computation.7.clone.1 | loop fusion | flops 14153472 | bytes 18892800 | tf_op jit(solution)/shard_map/while/body/eval_jaxpr/reduce_sum | solution.py:150
  144.9 8.2 %fusion.109 = f32[384,6,128]{2,0,1:T(8,128)S(1)} fusion(f32[2048,384,6]{1,0,2:T(8,128)} %get-tuple-element.183, f32[384,6]{0,1:T(8,128)S(1)} %select_maximum_fusion.2, f32[384,6,128]{2,0,1:T(8,128)S(1)} %get-tuple-element.198, f32[384,6]{0,1:T(8,128)S(1)} %get-tuple-element.185, pred[]{:T(512)S(6)} %compare.13, ...), kind=kOutput, calls=%fused_computation.9.clone.1 | convolution fusion | flops 1223000064 | bytes 21782532 | tf_op jit(solution)/shard_map/while/body/eval_jaxpr/thk,kd->thd/dot_general | solution.py:151
  153.1 24.3 %all-gather.19.cloned.1.call-done = bf16[1,768,1536]{2,1,0:T(8,128)(2,1)} async-done(((bf16[1,192,1536]{2,1,0:T(8,128)(2,1)}), bf16[1,768,1536]{2,1,0:T(8,128)(2,1)}) %all-gather.19.cloned.1.call-update) | async-done | bytes 2359312 | tf_op jit(solution)/shard_map/all_gather | solution.py:165
  177.5 0.4 copy.84
  178.0 0.5 fusion.21
  178.5 0.6 collective-permute-start.1
  179.4 0.4 fusion.22
  180.3 0.7 fusion.37
  181.0 0.6 copy-done.6
  181.6 0.8 convolution_convert_fusion.1
  182.4 1.4 copy.92
  183.9 22.1 %reduce-scatter.7.cloned.1.call-done = bf16[384,384]{1,0:T(8,128)(2,1)} async-done(((bf16[1536,384]{1,0:T(8,128)(2,1)}), bf16[384,384]{1,0:T(8,128)(2,1)}) %reduce-scatter.7.cloned.1.call-update) | async-done | bytes 294928
  206.0 1.2 copy.93
  207.4 5.1 %psum.7 = f32[384]{0:T(512)S(1)} all-reduce(f32[384]{0:T(512)S(1)} %multiply_reduce_fusion.1), channel_id=1, replica_groups=mesh['req'=32,'tp'=4] {'tp'}, use_global_device_ids=true, to_apply=%region_18.19 | all-reduce | flops 384 | bytes 3072 | tf_op jit(solution)/shard_map/psum | solution.py:218
  212.5 0.8 multiply_convert_fusion.1
  213.5 23.9 %all-gather.13.cloned.1.call-done = bf16[384,1536]{1,0:T(8,128)(2,1)} async-done(((bf16[384,384]{1,0:T(8,128)(2,1)}), bf16[384,1536]{1,0:T(8,128)(2,1)}) %all-gather.13.cloned.1.call-update) | async-done | bytes 1179664 | tf_op jit(solution)/shard_map/all_gather | solution.py:220
  237.4 6.7 %gather_fusion.1 = bf16[576,1536]{1,0:T(8,128)(2,1)S(1)} fusion(bf16[384,1536]{1,0:T(8,128)(2,1)} %all-gather.13.cloned.1.call-done, s32[1024]{0:T(1024)S(1)} %pad_clamp_fusion.1), kind=kCustom, calls=%fused_computation.1 | custom fusion | bytes 3541248 | tf_op jit(solution)/shard_map/jit(_take)/gather | solution.py:221
  244.1 1.7 gather.18
  245.8 1.9 broadcast_select_fusion
  247.7 41.3 %all_to_all.15 = bf16[32,18,1536]{2,1,0:T(8,128)(2,1)} all-to-all(bf16[32,18,1536]{2,1,0:T(8,128)(2,1)S(1)} %broadcast_select_fusion), channel_id=1, replica_groups=mesh['req'=32,'tp'=4] {'req'}, dimensions={0} | all-to-all | bytes 3538944 | tf_op jit(solution)/shard_map/all_to_all | solution.py:224
  289.0 2.6 reshape.345
  291.7 3.4 fusion.85
  295.0 2.5 multiply_convert_fusion
  297.6 2.2 copy.87
  299.8 4.2 %convert_reduce_fusion = bf16[576,1536]{1,0:T(8,128)(2,1)S(1)} fusion(bf16[576,4,192]{0,2,1:T(8,128)(2,1)} %bitcast.115, bf16[4,192,1536]{2,1,0:T(8,128)(2,1)} %bitcast.123), kind=kOutput, calls=%fused_computation.25 | convolution fusion | flops 1365147648 | bytes 5013504 | tf_op jit(solution)/shard_map/rqf,qfd->qrd/dot_general | solution.py:231
  304.0 1.7 reshape.348
  305.7 4.9 %all-to-all-start.2 = ((bf16[32,18,1536]{2,1,0:T(8,128)(2,1)}), bf16[32,18,1536]{2,1,0:T(8,128)(2,1)}, u32[]{:S(2)}, u32[]{:S(2)}) async-start(bf16[32,18,1536]{2,1,0:T(8,128)(2,1)} %reshape.348), calls=%async_computation.2 | async-start | bytes 4718592 | tf_op jit(solution)/shard_map/all_to_all | solution.py:238
  311.6 30.2 %all-to-all-done.2 = bf16[32,18,1536]{2,1,0:T(8,128)(2,1)} async-done(((bf16[32,18,1536]{2,1,0:T(8,128)(2,1)}), bf16[32,18,1536]{2,1,0:T(8,128)(2,1)}, u32[]{:S(2)}, u32[]{:S(2)}) %all-to-all-start.2) | async-done | bytes 1769504 | tf_op jit(solution)/shard_map/all_to_all | solution.py:238
  341.9 2.6 reshape.349
  344.5 6.3 %gather_fusion.2 = bf16[1536,1536]{1,0:T(8,128)(2,1)} fusion(bf16[576,1536]{1,0:T(8,128)(2,1)S(1)} %reshape.349, s32[2048]{0:T(1024)S(1)} %pad_clamp_fusion), kind=kCustom, calls=%fused_computation.2 | custom fusion | bytes 9443328 | tf_op jit(solution)/shard_map/jit(_take)/gather | solution.py:246
  350.8 8.8 %gather.20 = bf16[384,4,1536]{2,1,0:T(4,128)(2,1)} reshape(bf16[1536,1536]{1,0:T(8,128)(2,1)} %gather_fusion.2) | data formatting | bytes 9437184 | tf_op jit(solution)/shard_map/jit(_take)/gather | solution.py:246
  359.7 12.2 %multiply_reduce_fusion = f32[384,1536]{1,0:T(8,128)} fusion(bf16[384,4,1536]{2,1,0:T(4,128)(2,1)} %gather.20, f32[384,4]{1,0:T(8,128)S(1)} %broadcast_select_fusion.2, pred[384,4]{1,0:T(8,128)(4,1)S(1)} %broadcast_in_dim.159), kind=kLoop, calls=%fused_computation.24 | loop fusion | flops 8847360 | bytes 7085568 | tf_op jit(solution)/shard_map/reduce_sum | solution.py:248
  372.5 29.1 %reduce-scatter.5.cloned.1.call-done = f32[384,384]{1,0:T(8,128)} async-done(((f32[384,1536]{1,0:T(8,128)}), f32[384,384]{1,0:T(8,128)}) %reduce-scatter.5.cloned.1.call-update) | async-done | bytes 589840 | tf_op jit(solution)/shard_map/reduce_scatter | solution.py:249
  401.6 1.9 select_convert_fusion
  (124 shorter events, 6.6 us)
Async XLA Ops:
  6.5 2.2 copy-start
  6.5 2.7 copy-start.11
  6.5 3.6 copy-start.16
  6.5 62.0 %all-gather.11.cloned.1.call-start = ((), (), s32[]{:S(2)}) async-start(), calls=%async_computation.5 | async-start | bytes 1474560 | tf_op jit(solution)/shard_map/all_gather | solution.py:63
  7.3 145.8 %all-gather.15.cloned.1.call-start = ((), (), s32[]{:S(2)}) async-start(), calls=%async_computation.8 | async-start | bytes 2949120 | tf_op jit(solution)/shard_map/all_gather | solution.py:163
  8.0 145.1 %all-gather.17.cloned.1.call-start = ((), (), s32[]{:S(2)}) async-start(), calls=%async_computation.9 | async-start | bytes 2949120 | tf_op jit(solution)/shard_map/all_gather | solution.py:164
  19.7 12.1 %copy-start.12 = (s32[384,4]{0,1:T(4,128)S(1)}, s32[384,4]{0,1:T(4,128)}, u32[]{:S(2)}) copy-start(s32[384,4]{0,1:T(4,128)} %param.29) | copy-start | bytes 18436
  19.7 12.6 %copy-start.15 = (f32[384]{0:T(512)S(1)}, f32[384]{0:T(512)}, u32[]{:S(2)}) copy-start(f32[384]{0:T(512)} %param.19) | copy-start | bytes 4612
  19.7 69.9 %all-to-all-start = ((bf16[32,4,2,64,128]{4,3,2,1,0:T(8,128)(2,1)}), bf16[32,4,2,64,128]{4,3,2,1,0:T(8,128)(2,1)}, u32[]{:S(2)}, u32[]{:S(2)}) async-start(bf16[32,4,2,64,128]{4,3,2,1,0:T(8,128)(2,1)} %copy.83), calls=%async_computation | async-start | bytes 8388608 | tf_op jit(solution)/shard_map/all_to_all | solution.py:103
  31.1 146.4 %all-gather.19.cloned.1.call-start = ((), (), s32[]{:S(2)}) async-start(), calls=%async_computation.10 | async-start | bytes 2949120 | tf_op jit(solution)/shard_map/all_gather | solution.py:165
  31.7 174.3 %reduce-scatter.7.cloned.1.call-start = ((), (), s32[]{:S(2)}) async-start(), calls=%async_computation.11 | async-start | bytes 1474560
  73.2 1.3 copy-start.3
  73.3 1.5 copy-start.7
  73.3 1.6 copy-start.8
  73.6 2.0 copy-start.4
  73.6 2.4 collective-permute-start
  75.6 0.7 copy-start.9
  153.1 24.9 %copy-start.5 = (bf16[384,3,128]{2,0,1:T(8,128)(2,1)S(1)}, bf16[384,3,128]{2,0,1:T(8,128)(2,1)}, u32[]{:S(2)}) copy-start(bf16[384,3,128]{2,0,1:T(8,128)(2,1)} %copy-done.4) | copy-start | bytes 884740
  177.9 2.4 collective-permute-start.2
  178.0 2.3 copy-start.10
  178.5 1.4 collective-permute-start.1
  179.1 1.2 collective-permute-start.3
  180.3 1.3 copy-start.6
  182.4 24.8 %copy-start.2 = (bf16[384,384]{1,0:T(8,128)(2,1)S(1)}, bf16[384,384]{1,0:T(8,128)(2,1)}, u32[]{:S(2)}) copy-start(bf16[384,384]{1,0:T(8,128)(2,1)} %param.18) | copy-start | bytes 884740
  182.4 30.1 %copy-start.14 = (f32[384]{0:T(512)S(1)}, f32[384]{0:T(512)}, u32[]{:S(2)}) copy-start(f32[384]{0:T(512)} %param.28) | copy-start | bytes 4612
  183.9 53.5 %all-gather.13.cloned.1.call-start = ((), (), s32[]{:S(2)}) async-start(), calls=%async_computation.6 | async-start | bytes 1474560 | tf_op jit(solution)/shard_map/all_gather | solution.py:220
  291.6 3.4 copy-start.17
  305.7 5.3 %copy-start.13 = (f32[384,4]{0,1:T(4,128)S(1)}, f32[384,4]{0,1:T(4,128)}, u32[]{:S(2)}) copy-start(f32[384,4]{0,1:T(4,128)} %param.30) | copy-start | bytes 18436
  305.7 36.2 %all-to-all-start.2 = ((bf16[32,18,1536]{2,1,0:T(8,128)(2,1)}), bf16[32,18,1536]{2,1,0:T(8,128)(2,1)}, u32[]{:S(2)}, u32[]{:S(2)}) async-start(bf16[32,18,1536]{2,1,0:T(8,128)(2,1)} %reshape.348), calls=%async_computation.2 | async-start | bytes 4718592 | tf_op jit(solution)/shard_map/all_to_all | solution.py:238
  310.6 91.0 %reduce-scatter.5.cloned.1.call-start = ((), (), s32[]{:S(2)}) async-start(), calls=%async_computation.7 | async-start | bytes 2949120 | tf_op jit(solution)/shard_map/reduce_scatter | solution.py:249
  359.7 43.9 %copy-start.1 = (bf16[16,2,2,128,128]{4,3,2,1,0:T(8,128)(2,1)S(1)}, bf16[16,2,2,128,128]{4,3,2,1,0:T(8,128)(2,1)}, u32[]{:S(2)}) copy-start(bf16[16,2,2,128,128]{4,3,2,1,0:T(8,128)(2,1)} %param.24) | copy-start | bytes 6291460
Sparse Core Ops, SparseCore 0:
  9.0 26.3 all-gather.10
  37.1 72.6 all-gather.14
  111.5 32.1 all-gather.16
  145.2 32.1 all-gather.18
  184.0 22.0 reduce-scatter.6
  213.5 23.8 all-gather.12
  372.0 29.6 reduce-scatter.4

commit v4 on v3

--- a/solution.py
+++ b/solution.py
@@ -211,13 +211,13 @@
         (weighted / row_sum[:, :, None]).astype(jnp.bfloat16).reshape(rows_here, heads_here * HD)
     )
     proj_part = jnp.dot(attention, w_out, preferred_element_type=jnp.float32)
-    attn_slice = lax.psum_scatter(
-        proj_part.astype(jnp.bfloat16), "tp", scatter_dimension=1, tiled=True
-    ).astype(jnp.float32)
-    residual = hidden + attn_slice
-    sq_mid = lax.psum(jnp.sum(residual * residual, axis=1), "tp")
-    moe_in = (residual * lax.rsqrt(sq_mid / D + EPSILON)[:, None] * norm_moe).astype(jnp.bfloat16)
-    full_rows = lax.all_gather(moe_in, "tp", axis=1, tiled=True)
+    attn_full = lax.psum(proj_part.astype(jnp.bfloat16), "tp").astype(jnp.float32)
+    residual_full = full_in + attn_full
+    sq_mid = jnp.sum(residual_full * residual_full, axis=1)
+    full_rows = (residual_full * lax.rsqrt(sq_mid / D + EPSILON)[:, None] * norm_moe).astype(
+        jnp.bfloat16
+    )
+    residual = lax.dynamic_slice_in_dim(residual_full, tp_index * feature_cols, feature_cols, 1)
     outgoing_rows = jnp.take(full_rows, slot_token, axis=0).reshape(
         req_count, sub, full_rows.shape[1]
     )
@@ -243,9 +243,15 @@
         tiled=True,
     )
     flat_back = returned.reshape(-1, width_all)
-    picked = jnp.take(flat_back, send_pos, axis=0).reshape(rows_here, TOP, width_all)
     pick_weight = jnp.where(mine.reshape(rows_here, TOP), expert_weights, 0.0)
-    moe_full = jnp.sum(pick_weight[:, :, None] * picked.astype(jnp.float32), axis=1)
+    slot_hit = send_pos.reshape(rows_here, TOP)[:, :, None] == jnp.arange(flat_back.shape[0])
+    combine = jnp.sum(jnp.where(slot_hit, pick_weight[:, :, None], 0.0), axis=1)
+    moe_full = jnp.dot(
+        combine,
+        flat_back.astype(jnp.float32),
+        precision=lax.Precision.HIGHEST,
+        preferred_element_type=jnp.float32,
+    )
     moe_part = lax.psum_scatter(moe_full, "tp", scatter_dimension=1, tiled=True)
     layer_out = residual + moe_part
     live_rows = jnp.arange(rows_here) < suffix_len[0]
@@ -264,7 +270,7 @@
         P(),
         P(),
         P("req"),
-        P("tp"),
+        P(),
         P("req", None),
         P("req", None),
         P("req", None, "tp"),

time: 412 us -> 380 us (0.922)
  local copies, waits for them, and re-layouts: 54.4 us -> 35.4 us
  waiting for transfers between devices: 146 us -> 136 us
  other arithmetic: 53.2 us -> 46.4 us
  matrix products: 55.5 us -> 60.5 us
    psum x0 -> x1, waiting for transfers between devices: none -> 38.4 us  [body(): lax.psum(proj_part.astype(jnp.bfloat16), 'tp').astype(jnp.float32)]
    all_gather x1 -> x0, waiting for transfers between devices: 23.9 us -> none  [body(): full_rows = lax.all_gather(moe_in, 'tp', axis=1, tiled=True)]
    unnamed x8 -> x6, waiting for transfers between devices: 24.8 us -> 2.64 us
    gather x2 -> x0, local copies, waits for them, and re-layouts: 15.2 us -> none  [body(): jnp.take(flat_back, send_pos, axis=0).reshape(rows_here, TOP, width_all)]
    reduce_sum x2 -> x1, other arithmetic: 12.3 us -> 0.57 us  [body(): combine = jnp.sum(jnp.where(slot_hit, pick_weight[:, :, None], 0.0), axis=1)]
    unnamed x1 -> x2, blocking collectives: 19.7 us -> 24.9 us
    psum x1 -> x0, blocking collectives: 5.11 us -> none  [body(): sq_mid = lax.psum(jnp.sum(residual * residual, axis=1), 'tp')]
    dot_general x0 -> x1, matrix products: none -> 4.35 us  [body(): jnp.dot(combine, flat_back.astype(jnp.float32), precision=lax.Precision.H...]
  transfers between devices with their start and end apart: 13 -> 12, of which waited for: 8 -> 8; matrix products, arithmetic and copies ran while one was open for 24% -> 27% of each run, Pallas kernels for 0% -> 0%
where the time goes in v4:
time: 380 us; the launch traced here: 379 us
  waiting for transfers between devices  136 us (36%)
  blocking collectives  66.1 us (17%)
  matrix products  60.5 us (16%)
  other arithmetic  46.4 us (12%)
  local copies, waits for them, and re-layouts  35.4 us (9%)
  starting transfers between devices  17.9 us (5%)
  between operations  16.9 us (4%)
    all_to_all x1, blocking collectives, body(): lax.all_to_all(outgoing_rows, 'req', split_axis=0, concat_axis=0, tiled=T...  41.2 us
    psum x1, waiting for transfers between devices, body(): lax.psum(proj_part.astype(jnp.bfloat16), 'tp').astype(jnp.float32)  38.4 us
    all_to_all x1, waiting for transfers between devices, body(): lax.all_to_all(expert_out.reshape(src_count, item_count, width_all), 'req...  29.6 us
    reduce_scatter x1, waiting for transfers between devices, body(): moe_part = lax.psum_scatter(moe_full, 'tp', scatter_dimension=1, tiled=True)  29 us
    unnamed x2, blocking collectives  24.9 us
    all_gather x1, waiting for transfers between devices, body(): down_full = lax.all_gather(w_down[0], 'tp', axis=0, tiled=True)  24.4 us
    dot_general x2, matrix products, absorb(): jnp.einsum('thd,kd->thk', query_six, key_block, preferred_element_type=jn...  20.3 us
    reduce_sum x2, other arithmetic, absorb(): new_sum = old_sum * rescale + jnp.sum(block_weights, axis=2)  18.9 us
  transfers between devices with their start and end apart: 12, of which 8 were waited for; matrix products, arithmetic and copies ran while one was open for 27% of the time, Pallas kernels for 0%

profile of v4, /device:TPU:1, one launch (start us, length us, event | category | flops | bytes accessed | tf_op | source)
XLA Modules:
  0.0 379.1 jit_solution(11697861805309552809)
XLA Ops:
  6.5 0.7 all-gather.12.cloned.1.call-update
  7.3 0.7 all-gather.14.cloned.1.call-update
  8.1 0.7 all-gather.16.cloned.1.call-update
  9.5 0.6 multiply_reduce_fusion.1
  10.2 3.2 convolution_convert_fusion
  13.3 3.4 copy.99
  16.7 2.9 copy.85
  19.7 11.4 %all-to-all-start = ((bf16[32,4,2,64,128]{4,3,2,1,0:T(8,128)(2,1)}), bf16[32,4,2,64,128]{4,3,2,1,0:T(8,128)(2,1)}, u32[]{:S(2)}, u32[]{:S(2)}) async-start(bf16[32,4,2,64,128]{4,3,2,1,0:T(8,128)(2,1)} %copy.85), calls=%async_computation | async-start | bytes 8388608 | tf_op jit(solution)/shard_map/all_to_all | solution.py:103
  31.2 0.5 all-gather.18.cloned.1.call-update
  32.3 0.6 dynamic_slice.30
  35.4 19.7 %all-gather.5 = f32[4,1,384]{2,1,0:T(1,128)S(1)} all-gather(f32[1,1,384]{2,1,0:T(1,128)S(1)} %reshape.364), channel_id=2, replica_groups=mesh['req'=32,'tp'=4] {'tp'}, dimensions={0}, use_global_device_ids=true | all-gather | bytes 7680 | tf_op args[1]
  55.1 9.1 %reduce-window.18 = s32[32,12,128]{2,1,0:T(8,128)S(1)} reduce-window(s32[32,12,128]{2,1,0:T(8,128)S(1)} %fusion.41, s32[]{:T(128)} %constant.196.clone.1), window={size=1x1x128 pad=0_0x0_0x127_0}, to_apply=%region_2.3 | reduce-window | flops 6242304 | bytes 393220 | tf_op jit(solution)/shard_map/reduce-window
  65.0 0.8 select_reduce_fusion.1
  65.8 1.5 multiply_cosine_fusion
  67.3 2.0 constant_dynamic-slice_fusion.2
  69.3 1.6 fusion.18
  70.9 2.5 fusion.39
  73.7 1.1 copy.97
  74.8 1.4 subtract_convert_fusion
  76.4 0.4 collective-permute-start
  76.8 0.7 fusion.30
  77.6 0.4 fusion.49
  78.5 11.1 %all-to-all-done = bf16[32,4,2,64,128]{4,3,2,1,0:T(8,128)(2,1)} async-done(((bf16[32,4,2,64,128]{4,3,2,1,0:T(8,128)(2,1)}), bf16[32,4,2,64,128]{4,3,2,1,0:T(8,128)(2,1)}, u32[]{:S(2)}, u32[]{:S(2)}) %all-to-all-start) | async-done | bytes 4194336 | tf_op jit(solution)/shard_map/all_to_all | solution.py:103
  89.6 4.4 %gather_fusion = bf16[16,4,2,64,128]{4,3,2,1,0:T(8,128)(2,1)} fusion(bf16[32,4,2,64,128]{4,3,2,1,0:T(8,128)(2,1)} %all-to-all-done, s32[1024]{0:T(1024)S(1)} %pad_clamp_fusion.1), kind=kCustom, calls=%fused_computation | custom fusion | bytes 4194368 | tf_op jit(solution)/shard_map/jit(_take)/gather | solution.py:117
  94.0 1.9 broadcast_select_fusion.1
  95.8 1.1 fusion.83
  97.0 56.1 %while.15 = (s32[]{:T(128)}, f32[384,6]{0,1:T(8,128)S(1)}, f32[384,6]{0,1:T(8,128)S(1)}, f32[384,6,128]{2,0,1:T(8,128)S(1)}, bf16[2,2048,128]{2,1,0:T(8,128)(2,1...) while((s32[]{:T(128)}, f32[384,6]{0,1:T(8,128)S(1)}, ...), condition=%wide.region_14.15_spmd.clone, body=%wide.region_11.14_spmd.clone.sunk | while | flops 2454564096 | bytes 60775016 | solution.py:189
  97.0 10.1 %bitcast_reduce_fusion.2 = (f32[384,6]{0,1:T(8,128)S(1)}, f32[2048,384,6]{1,0,2:T(8,128)}) fusion(bf16[384,6,128]{2,0,1:T(8,128)(2,1)S(1)} %get-tuple-element.211, bf16[2,2048,128]{2,1,0:T(8,128)(2,1)} %get-tuple-element.210, s32[]{:T(128)} %get-tuple-element.197), kind=kOutput, calls=%fused_computation.3.clone.1 | convolution fusion | flops 1217394432 | bytes 19998208 | tf_op jit(solution)/shard_map/while/body/eval_jaxpr/thd,kd->thk/dot_general | solution.py:144
  107.1 9.4 %fusion.110 = f32[384,6]{0,1:T(8,128)S(1)} fusion(f32[2048,384,6]{1,0,2:T(8,128)} %get-tuple-element.185, f32[384,6]{0,1:T(8,128)S(1)} %select_maximum_fusion.2), kind=kLoop, calls=%fused_computation.6.clone.1 | loop fusion | flops 14153472 | bytes 18892800 | tf_op jit(solution)/shard_map/while/body/eval_jaxpr/reduce_sum | solution.py:150
  116.6 8.6 %fusion.112 = f32[384,6,128]{2,0,1:T(8,128)S(1)} fusion(f32[2048,384,6]{1,0,2:T(8,128)} %get-tuple-element.185, f32[384,6]{0,1:T(8,128)S(1)} %select_maximum_fusion.2, f32[384,6,128]{2,0,1:T(8,128)S(1)} %get-tuple-element.200, f32[384,6]{0,1:T(8,128)S(1)} %get-tuple-element.187, pred[]{:T(512)S(6)} %compare.13, ...), kind=kOutput, calls=%fused_computation.8.clone.1 | convolution fusion | flops 1223000064 | bytes 21782532 | tf_op jit(solution)/shard_map/while/body/eval_jaxpr/thk,kd->thd/dot_general | solution.py:151
  125.2 10.1 %bitcast_reduce_fusion.2 = (f32[384,6]{0,1:T(8,128)S(1)}, f32[2048,384,6]{1,0,2:T(8,128)}) fusion(bf16[384,6,128]{2,0,1:T(8,128)(2,1)S(1)} %get-tuple-element.211, bf16[2,2048,128]{2,1,0:T(8,128)(2,1)} %get-tuple-element.210, s32[]{:T(128)} %get-tuple-element.197), kind=kOutput, calls=%fused_computation.3.clone.1 | convolution fusion | flops 1217394432 | bytes 19998208 | tf_op jit(solution)/shard_map/while/body/eval_jaxpr/thd,kd->thk/dot_general | solution.py:144
  135.3 9.5 %fusion.110 = f32[384,6]{0,1:T(8,128)S(1)} fusion(f32[2048,384,6]{1,0,2:T(8,128)} %get-tuple-element.185, f32[384,6]{0,1:T(8,128)S(1)} %select_maximum_fusion.2), kind=kLoop, calls=%fused_computation.6.clone.1 | loop fusion | flops 14153472 | bytes 18892800 | tf_op jit(solution)/shard_map/while/body/eval_jaxpr/reduce_sum | solution.py:150
  144.9 8.2 %fusion.112 = f32[384,6,128]{2,0,1:T(8,128)S(1)} fusion(f32[2048,384,6]{1,0,2:T(8,128)} %get-tuple-element.185, f32[384,6]{0,1:T(8,128)S(1)} %select_maximum_fusion.2, f32[384,6,128]{2,0,1:T(8,128)S(1)} %get-tuple-element.200, f32[384,6]{0,1:T(8,128)S(1)} %get-tuple-element.187, pred[]{:T(512)S(6)} %compare.13, ...), kind=kOutput, calls=%fused_computation.8.clone.1 | convolution fusion | flops 1223000064 | bytes 21782532 | tf_op jit(solution)/shard_map/while/body/eval_jaxpr/thk,kd->thd/dot_general | solution.py:151
  153.1 24.4 %all-gather.18.cloned.1.call-done = bf16[1,768,1536]{2,1,0:T(8,128)(2,1)} async-done(((bf16[1,192,1536]{2,1,0:T(8,128)(2,1)}), bf16[1,768,1536]{2,1,0:T(8,128)(2,1)}) %all-gather.18.cloned.1.call-update) | async-done | bytes 2359312 | tf_op jit(solution)/shard_map/all_gather | solution.py:165
  177.5 0.4 copy.86
  178.0 0.4 copy-done.6
  178.4 0.5 fusion.21
  179.1 0.5 collective-permute-start.3
  179.6 0.4 fusion.22
  180.2 0.3 collective-permute-done.3
  180.6 0.6 fusion.37
  181.2 0.6 copy-done.7
  181.9 1.8 convolution_convert_fusion.1
  183.7 5.2 %all-gather.6 = f32[4,1,384]{2,1,0:T(1,128)S(1)} all-gather(f32[1,1,384]{2,1,0:T(1,128)S(1)} %reshape.366), channel_id=3, replica_groups=mesh['req'=32,'tp'=4] {'tp'}, dimensions={0}, use_global_device_ids=true | all-gather | bytes 7680 | tf_op args[10]
  189.1 38.4 %all-reduce.2.cloned.1.call-done = bf16[384,1536]{1,0:T(8,128)(2,1)} async-done(((bf16[384,1536]{1,0:T(8,128)(2,1)}), bf16[384,1536]{1,0:T(8,128)(2,1)}) %all-reduce.2.cloned.1.call-update) | async-done | bytes 1179664 | tf_op jit(solution)/shard_map/psum | solution.py:214
  227.5 3.2 convert_add_fusion
  230.7 0.4 multiply_convert_fusion
  231.1 3.6 gather_fusion.1
  234.8 3.6 gather.12
  238.3 1.9 broadcast_select_fusion
  240.3 41.2 %all_to_all.15 = bf16[32,18,1536]{2,1,0:T(8,128)(2,1)} all-to-all(bf16[32,18,1536]{2,1,0:T(8,128)(2,1)S(1)} %broadcast_select_fusion), channel_id=1, replica_groups=mesh['req'=32,'tp'=4] {'req'}, dimensions={0} | all-to-all | bytes 3538944 | tf_op jit(solution)/shard_map/all_to_all | solution.py:224
  281.5 2.6 reshape.338
  284.2 3.4 fusion.85
  287.6 2.5 multiply_convert_fusion.1
  290.1 1.5 copy.91
  291.6 3.9 %convert_reduce_fusion = bf16[576,1536]{1,0:T(8,128)(2,1)S(1)} fusion(bf16[576,4,192]{0,2,1:T(8,128)(2,1)S(1)} %bitcast.114, bf16[4,192,1536]{2,1,0:T(8,128)(2,1)} %bitcast.121), kind=kOutput, calls=%fused_computation.23 | convolution fusion | flops 1365147648 | bytes 5013504 | tf_op jit(solution)/shard_map/rqf,qfd->qrd/dot_general | solution.py:231
  295.5 1.7 reshape.341
  297.2 4.9 %all-to-all-start.2 = ((bf16[32,18,1536]{2,1,0:T(8,128)(2,1)}), bf16[32,18,1536]{2,1,0:T(8,128)(2,1)}, u32[]{:S(2)}, u32[]{:S(2)}) async-start(bf16[32,18,1536]{2,1,0:T(8,128)(2,1)} %reshape.341), calls=%async_computation.2 | async-start | bytes 4718592 | tf_op jit(solution)/shard_map/all_to_all | solution.py:238
  303.3 0.6 select_reduce_fusion
  303.9 29.6 %all-to-all-done.2 = bf16[32,18,1536]{2,1,0:T(8,128)(2,1)} async-done(((bf16[32,18,1536]{2,1,0:T(8,128)(2,1)}), bf16[32,18,1536]{2,1,0:T(8,128)(2,1)}, u32[]{:S(2)}, u32[]{:S(2)}) %all-to-all-start.2) | async-done | bytes 1769504 | tf_op jit(solution)/shard_map/all_to_all | solution.py:238
  333.4 2.6 reshape.342
  336.1 4.3 %fusion.86 = f32[384,1536]{1,0:T(8,128)} fusion(f32[384,576]{0,1:T(8,128)S(1)} %select_reduce_fusion, bf16[576,1536]{1,0:T(8,128)(2,1)S(1)} %reshape.342), kind=kOutput, calls=%fused_computation.166 | convolution fusion | flops 4076863488 | bytes 5013504 | tf_op jit(solution)/shard_map/dot_general | solution.py:249
  341.2 29.0 %reduce-scatter.2.cloned.1.call-done = f32[384,384]{1,0:T(8,128)} async-done(((f32[384,1536]{1,0:T(8,128)}), f32[384,384]{1,0:T(8,128)}) %reduce-scatter.2.cloned.1.call-update) | async-done | bytes 589840 | tf_op jit(solution)/shard_map/reduce_scatter | solution.py:255
  370.2 2.1 select_convert_fusion
  (124 shorter events, 5.5 us)
Async XLA Ops:
  6.5 2.3 copy-start
  6.5 2.7 copy-start.13
  6.5 62.7 %all-gather.12.cloned.1.call-start = ((), (), s32[]{:S(2)}) async-start(), calls=%async_computation.4 | async-start | bytes 1474560 | tf_op jit(solution)/shard_map/all_gather | solution.py:63
  7.3 2.9 copy-start.18
  7.3 145.8 %all-gather.14.cloned.1.call-start = ((), (), s32[]{:S(2)}) async-start(), calls=%async_computation.7 | async-start | bytes 2949120 | tf_op jit(solution)/shard_map/all_gather | solution.py:163
  8.0 145.1 %all-gather.16.cloned.1.call-start = ((), (), s32[]{:S(2)}) async-start(), calls=%async_computation.8 | async-start | bytes 2949120 | tf_op jit(solution)/shard_map/all_gather | solution.py:164
  19.7 12.1 %copy-start.14 = (s32[384,4]{0,1:T(4,128)S(1)}, s32[384,4]{0,1:T(4,128)}, u32[]{:S(2)}) copy-start(s32[384,4]{0,1:T(4,128)} %param.29) | copy-start | bytes 18436
  19.7 12.6 %copy-start.16 = (f32[384]{0:T(512)S(1)}, f32[384]{0:T(512)}, u32[]{:S(2)}) copy-start(f32[384]{0:T(512)} %param.19) | copy-start | bytes 4612
  19.7 69.9 %all-to-all-start = ((bf16[32,4,2,64,128]{4,3,2,1,0:T(8,128)(2,1)}), bf16[32,4,2,64,128]{4,3,2,1,0:T(8,128)(2,1)}, u32[]{:S(2)}, u32[]{:S(2)}) async-start(bf16[32,4,2,64,128]{4,3,2,1,0:T(8,128)(2,1)} %copy.85), calls=%async_computation | async-start | bytes 8388608 | tf_op jit(solution)/shard_map/all_to_all | solution.py:103
  31.1 146.3 %all-gather.18.cloned.1.call-start = ((), (), s32[]{:S(2)}) async-start(), calls=%async_computation.9 | async-start | bytes 2949120 | tf_op jit(solution)/shard_map/all_gather | solution.py:165
  31.7 195.8 %all-reduce.2.cloned.1.call-start = ((), (), s32[]{:S(2)}) async-start(), calls=%async_computation.5 | async-start | bytes 2359296 | tf_op jit(solution)/shard_map/psum | solution.py:214
  31.9 35.3 %copy-start.10 = (bf16[1536,256]{1,0:T(8,128)(2,1)S(1)}, bf16[1536,256]{1,0:T(8,128)(2,1)}, u32[]{:S(2)}) copy-start(bf16[1536,256]{1,0:T(8,128)(2,1)} %param.22) | copy-start | bytes 2359300
  73.7 3.2 copy-start.2
  74.8 2.1 copy-start.8
  74.8 2.1 copy-start.9
  76.4 1.2 copy-start.5
  76.4 1.8 collective-permute-start
  77.6 0.7 copy-start.11
  177.5 1.0 copy-start.6
  177.9 2.7 collective-permute-start.2
  178.4 2.1 copy-start.12
  179.0 1.2 collective-permute-start.1
  179.1 1.4 collective-permute-start.3
  180.6 1.3 copy-start.7
  181.9 1.8 copy-start.17
  181.9 45.7 %copy-start.3 = (bf16[384,1536]{1,0:T(8,128)(2,1)S(1)}, bf16[384,1536]{1,0:T(8,128)(2,1)}, u32[]{:S(2)}) copy-start(bf16[384,1536]{1,0:T(8,128)(2,1)} %all-gather.12.cloned.1.call-done) | copy-start | bytes 3538948
  227.5 3.2 copy-start.4
  284.2 3.4 copy-start.19
  297.2 5.2 %copy-start.15 = (f32[384,4]{0,1:T(4,128)S(1)}, f32[384,4]{0,1:T(4,128)}, u32[]{:S(2)}) copy-start(f32[384,4]{0,1:T(4,128)} %param.30) | copy-start | bytes 18436
  297.2 36.2 %all-to-all-start.2 = ((bf16[32,18,1536]{2,1,0:T(8,128)(2,1)}), bf16[32,18,1536]{2,1,0:T(8,128)(2,1)}, u32[]{:S(2)}, u32[]{:S(2)}) async-start(bf16[32,18,1536]{2,1,0:T(8,128)(2,1)} %reshape.341), calls=%async_computation.2 | async-start | bytes 4718592 | tf_op jit(solution)/shard_map/all_to_all | solution.py:238
  302.2 68.0 %reduce-scatter.2.cloned.1.call-start = ((), (), s32[]{:S(2)}) async-start(), calls=%async_computation.6 | async-start | bytes 2949120 | tf_op jit(solution)/shard_map/reduce_scatter | solution.py:255
  340.4 31.9 %copy-start.1 = (bf16[16,2,2,128,128]{4,3,2,1,0:T(8,128)(2,1)S(1)}, bf16[16,2,2,128,128]{4,3,2,1,0:T(8,128)(2,1)}, u32[]{:S(2)}) copy-start(bf16[16,2,2,128,128]{4,3,2,1,0:T(8,128)(2,1)} %param.24) | copy-start | bytes 6291460
Sparse Core Ops, SparseCore 0:
  9.0 26.3 all-gather.11
  37.1 72.6 all-gather.13
  111.5 32.1 all-gather.15
  145.2 32.1 all-gather.17
  183.8 43.6 all-reduce.1
  340.5 29.6 reduce-scatter.1

commit v5 on v4

--- a/solution.py
+++ b/solution.py
@@ -162,7 +162,6 @@
     )
     gate_full = lax.all_gather(w_gate[0], "tp", axis=1, tiled=True)
     up_full = lax.all_gather(w_up[0], "tp", axis=1, tiled=True)
-    down_full = lax.all_gather(w_down[0], "tp", axis=0, tiled=True)
     expert_count = w_gate.shape[0] * req_count
     capacity = 3 * rows_here * TOP // (2 * expert_count)
     sub = capacity // tp_count
@@ -177,8 +176,8 @@
     pair_token = jnp.arange(rows_here * TOP) // TOP
     slot_match = (send_pos[None, :] == jnp.arange(expert_count * sub)[:, None]) & mine[None, :]
     slot_token = jnp.sum(jnp.where(slot_match, pair_token[None, :], 0), axis=1)
-    slot_token, send_pos, mine, block_inputs = lax.optimization_barrier(
-        (slot_token, send_pos, mine, block_inputs)
+    slot_token, send_pos, mine, norm_moe, block_inputs = lax.optimization_barrier(
+        (slot_token, send_pos, mine, norm_moe, block_inputs)
     )
     six = 2 * heads_here
     start_state = (
@@ -187,8 +186,8 @@
         jnp.zeros((rows_here, six, HD), jnp.float32),
     )
     (pre_max, pre_sum, pre_weighted), _ = lax.scan(absorb, start_state, block_inputs)
-    gate_full, up_full, down_full, pre_max, pre_sum, pre_weighted = lax.optimization_barrier(
-        (gate_full, up_full, down_full, pre_max, pre_sum, pre_weighted)
+    gate_full, up_full, pre_max, pre_sum, pre_weighted = lax.optimization_barrier(
+        (gate_full, up_full, pre_max, pre_sum, pre_weighted)
     )
     back = lax.ppermute(
         (pre_max[:, heads_here:], pre_sum[:, heads_here:], pre_weighted[:, heads_here:]),
@@ -211,7 +210,10 @@
         (weighted / row_sum[:, :, None]).astype(jnp.bfloat16).reshape(rows_here, heads_here * HD)
     )
     proj_part = jnp.dot(attention, w_out, preferred_element_type=jnp.float32)
-    attn_full = lax.psum(proj_part.astype(jnp.bfloat16), "tp").astype(jnp.float32)
+    attn_sum = lax.psum(proj_part.astype(jnp.bfloat16), "tp")
+    down_local, attn_sum = lax.optimization_barrier((w_down[0], attn_sum))
+    down_full = lax.all_gather(down_local, "tp", axis=0, tiled=True)
+    attn_full = attn_sum.astype(jnp.float32)
     residual_full = full_in + attn_full
     sq_mid = jnp.sum(residual_full * residual_full, axis=1)
     full_rows = (residual_full * lax.rsqrt(sq_mid / D + EPSILON)[:, None] * norm_moe).astype(

time: 380 us -> 381 us (level)
  waiting for transfers between devices: 136 us -> 126 us
  starting transfers between devices: 17.9 us -> 22.2 us
    all_gather x1, waiting for transfers between devices: 24.4 us -> 0.02 us  [body(): down_full = lax.all_gather(down_local, 'tp', axis=0, tiled=True)]
    psum x1, waiting for transfers between devices: 38.4 us -> 62.5 us  [body(): attn_sum = lax.psum(proj_part.astype(jnp.bfloat16), 'tp')]
    all_to_all x1, waiting for transfers between devices: 11.1 us -> 1.47 us  [body(): lax.all_to_all(outgoing.reshape(req_count, most_pages, 2, half_rows, HD),...]
  transfers between devices with their start and end apart: 12 -> 12, of which waited for: 8 -> 7; matrix products, arithmetic and copies ran while one was open for 27% -> 32% of each run, Pallas kernels for 0% -> 0%
where the time goes in v5:
time: 381 us; the launch traced here: 379 us
  waiting for transfers between devices  126 us (33%)
  blocking collectives  69.9 us (18%)
  matrix products  60.4 us (16%)
  other arithmetic  48.4 us (13%)
  local copies, waits for them, and re-layouts  35.5 us (9%)
  starting transfers between devices  22.2 us (6%)
  between operations  16.9 us (4%)
    psum x1, waiting for transfers between devices, body(): attn_sum = lax.psum(proj_part.astype(jnp.bfloat16), 'tp')  62.5 us
    all_to_all x1, blocking collectives, body(): lax.all_to_all(outgoing_rows, 'req', split_axis=0, concat_axis=0, tiled=T...  41.3 us
    all_to_all x1, waiting for transfers between devices, body(): lax.all_to_all(expert_out.reshape(src_count, item_count, width_all), 'req...  29.6 us
    reduce_scatter x1, waiting for transfers between devices, body(): moe_part = lax.psum_scatter(moe_full, 'tp', scatter_dimension=1, tiled=True)  29.6 us
    unnamed x2, blocking collectives  28.6 us
    dot_general x2, matrix products, absorb(): jnp.einsum('thd,kd->thk', query_six, key_block, preferred_element_type=jn...  20.2 us
    reduce_sum x2, other arithmetic, absorb(): new_sum = old_sum * rescale + jnp.sum(block_weights, axis=2)  19 us
    dot_general x2, matrix products, absorb(): jnp.einsum('thk,kd->thd', block_weights.astype(jnp.bfloat16), value_block...  16.6 us
  transfers between devices with their start and end apart: 12, of which 7 were waited for; matrix products, arithmetic and copies ran while one was open for 32% of the time, Pallas kernels for 0%

profile of v5, /device:TPU:1, one launch (start us, length us, event | category | flops | bytes accessed | tf_op | source)
XLA Modules:
  0.0 379.4 jit_solution(7866241295667477446)
XLA Ops:
  6.5 0.7 all-gather.11.cloned.1.call-update
  7.3 0.7 all-gather.15.cloned.1.call-update
  8.9 0.6 multiply_reduce_fusion.1
  9.5 3.1 convolution_convert_fusion
  12.6 3.4 copy.99
  16.1 2.9 copy.85
  19.0 11.4 %all-to-all-start = ((bf16[32,4,2,64,128]{4,3,2,1,0:T(8,128)(2,1)}), bf16[32,4,2,64,128]{4,3,2,1,0:T(8,128)(2,1)}, u32[]{:S(2)}, u32[]{:S(2)}) async-start(bf16[32,4,2,64,128]{4,3,2,1,0:T(8,128)(2,1)} %copy.85), calls=%async_computation | async-start | bytes 8388608 | tf_op jit(solution)/shard_map/all_to_all | solution.py:103
  30.5 0.7 all-gather.17.cloned.1.call-update
  31.8 23.3 %all-gather.4 = f32[4,1,384]{2,1,0:T(1,128)S(1)} all-gather(f32[1,1,384]{2,1,0:T(1,128)S(1)} %reshape.363), channel_id=2, replica_groups=mesh['req'=32,'tp'=4] {'tp'}, dimensions={0}, use_global_device_ids=true | all-gather | bytes 7680 | tf_op args[1]
  55.1 0.6 dynamic_slice.30
  58.2 0.6 pad_clamp_fusion.1
  58.8 9.1 %reduce-window.18 = s32[32,12,128]{2,1,0:T(8,128)S(1)} reduce-window(s32[32,12,128]{2,1,0:T(8,128)S(1)} %fusion.41, s32[]{:T(128)} %constant.196.clone.1), window={size=1x1x128 pad=0_0x0_0x127_0}, to_apply=%region_2.3 | reduce-window | flops 6242304 | bytes 393220 | tf_op jit(solution)/shard_map/reduce-window
  68.3 5.3 %all-gather.5 = f32[4,1,384]{2,1,0:T(1,128)S(1)} all-gather(f32[1,1,384]{2,1,0:T(1,128)S(1)} %reshape.365), channel_id=3, replica_groups=mesh['req'=32,'tp'=4] {'tp'}, dimensions={0}, use_global_device_ids=true | all-gather | bytes 7680 | tf_op args[10]
  74.0 0.8 select_reduce_fusion.1
  74.8 1.5 multiply_cosine_fusion
  76.3 2.0 constant_dynamic-slice_fusion.2
  78.3 1.6 fusion.18
  79.9 2.5 fusion.39
  82.7 1.1 copy.97
  83.8 1.4 subtract_convert_fusion
  85.4 0.4 collective-permute-start
  85.9 0.7 fusion.30
  86.6 0.4 fusion.49
  87.6 1.5 all-to-all-done
  89.0 4.6 %gather_fusion = bf16[16,4,2,64,128]{4,3,2,1,0:T(8,128)(2,1)} fusion(bf16[32,4,2,64,128]{4,3,2,1,0:T(8,128)(2,1)} %all-to-all-done, s32[1024]{0:T(1024)} %pad_clamp_fusion.1), kind=kCustom, calls=%fused_computation | custom fusion | bytes 4194368 | tf_op jit(solution)/shard_map/jit(_take)/gather | solution.py:117
  93.7 1.9 broadcast_select_fusion.1
  95.6 1.3 fusion.83
  96.8 56.0 %while.15 = (s32[]{:T(128)}, f32[384,6]{0,1:T(8,128)S(1)}, f32[384,6]{0,1:T(8,128)S(1)}, f32[384,6,128]{2,0,1:T(8,128)S(1)}, bf16[2,2048,128]{2,1,0:T(8,128)(2,1...) while((s32[]{:T(128)}, f32[384,6]{0,1:T(8,128)S(1)}, ...), condition=%wide.region_14.15_spmd.clone, body=%wide.region_11.14_spmd.clone.sunk | while | flops 2454564096 | bytes 60775016 | solution.py:188
  96.8 10.1 %bitcast_reduce_fusion.2 = (f32[384,6]{0,1:T(8,128)S(1)}, f32[2048,384,6]{1,0,2:T(8,128)}) fusion(bf16[384,6,128]{2,0,1:T(8,128)(2,1)S(1)} %get-tuple-element.215, bf16[2,2048,128]{2,1,0:T(8,128)(2,1)} %get-tuple-element.214, s32[]{:T(128)} %get-tuple-element.201), kind=kOutput, calls=%fused_computation.3.clone.1 | convolution fusion | flops 1217394432 | bytes 19998208 | tf_op jit(solution)/shard_map/while/body/eval_jaxpr/thd,kd->thk/dot_general | solution.py:144
  107.0 9.4 %fusion.110 = f32[384,6]{0,1:T(8,128)S(1)} fusion(f32[2048,384,6]{1,0,2:T(8,128)} %get-tuple-element.189, f32[384,6]{0,1:T(8,128)S(1)} %select_maximum_fusion.2), kind=kLoop, calls=%fused_computation.6.clone.1 | loop fusion | flops 14153472 | bytes 18892800 | tf_op jit(solution)/shard_map/while/body/eval_jaxpr/reduce_sum | solution.py:150
  116.4 8.5 %fusion.112 = f32[384,6,128]{2,0,1:T(8,128)S(1)} fusion(f32[2048,384,6]{1,0,2:T(8,128)} %get-tuple-element.189, f32[384,6]{0,1:T(8,128)S(1)} %select_maximum_fusion.2, f32[384,6,128]{2,0,1:T(8,128)S(1)} %get-tuple-element.204, f32[384,6]{0,1:T(8,128)S(1)} %get-tuple-element.191, pred[]{:T(512)S(6)} %compare.13, ...), kind=kOutput, calls=%fused_computation.8.clone.1 | convolution fusion | flops 1223000064 | bytes 21782532 | tf_op jit(solution)/shard_map/while/body/eval_jaxpr/thk,kd->thd/dot_general | solution.py:151
  124.9 10.1 %bitcast_reduce_fusion.2 = (f32[384,6]{0,1:T(8,128)S(1)}, f32[2048,384,6]{1,0,2:T(8,128)}) fusion(bf16[384,6,128]{2,0,1:T(8,128)(2,1)S(1)} %get-tuple-element.215, bf16[2,2048,128]{2,1,0:T(8,128)(2,1)} %get-tuple-element.214, s32[]{:T(128)} %get-tuple-element.201), kind=kOutput, calls=%fused_computation.3.clone.1 | convolution fusion | flops 1217394432 | bytes 19998208 | tf_op jit(solution)/shard_map/while/body/eval_jaxpr/thd,kd->thk/dot_general | solution.py:144
  135.0 9.6 %fusion.110 = f32[384,6]{0,1:T(8,128)S(1)} fusion(f32[2048,384,6]{1,0,2:T(8,128)} %get-tuple-element.189, f32[384,6]{0,1:T(8,128)S(1)} %select_maximum_fusion.2), kind=kLoop, calls=%fused_computation.6.clone.1 | loop fusion | flops 14153472 | bytes 18892800 | tf_op jit(solution)/shard_map/while/body/eval_jaxpr/reduce_sum | solution.py:150
  144.6 8.2 %fusion.112 = f32[384,6,128]{2,0,1:T(8,128)S(1)} fusion(f32[2048,384,6]{1,0,2:T(8,128)} %get-tuple-element.189, f32[384,6]{0,1:T(8,128)S(1)} %select_maximum_fusion.2, f32[384,6,128]{2,0,1:T(8,128)S(1)} %get-tuple-element.204, f32[384,6]{0,1:T(8,128)S(1)} %get-tuple-element.191, pred[]{:T(512)S(6)} %compare.13, ...), kind=kOutput, calls=%fused_computation.8.clone.1 | convolution fusion | flops 1223000064 | bytes 21782532 | tf_op jit(solution)/shard_map/while/body/eval_jaxpr/thk,kd->thd/dot_general | solution.py:151
  152.9 0.4 copy.86
  153.3 3.3 collective-permute-start.2
  156.6 0.5 fusion.21
  157.1 0.5 collective-permute-start.1
  157.6 0.3 collective-permute-start.3
  158.0 0.4 fusion.22
  158.5 0.3 collective-permute-done.3
  158.9 0.6 fusion.37
  159.5 0.6 copy-done.6
  160.1 1.8 convolution_convert_fusion.1
  162.2 62.5 %all-reduce.2.cloned.1.call-done = bf16[384,1536]{1,0:T(8,128)(2,1)} async-done(((bf16[384,1536]{1,0:T(8,128)(2,1)}), bf16[384,1536]{1,0:T(8,128)(2,1)}) %all-reduce.2.cloned.1.call-update) | async-done | bytes 1179664 | tf_op jit(solution)/shard_map/psum | solution.py:213
  224.7 3.1 convert_add_fusion
  227.8 1.7 multiply_convert_fusion
  229.5 3.6 gather_fusion.1
  233.1 3.6 gather.12
  236.7 2.1 broadcast_select_fusion
  238.8 41.3 %all_to_all.15 = bf16[32,18,1536]{2,1,0:T(8,128)(2,1)} all-to-all(bf16[32,18,1536]{2,1,0:T(8,128)(2,1)S(1)} %broadcast_select_fusion), channel_id=1, replica_groups=mesh['req'=32,'tp'=4] {'req'}, dimensions={0} | all-to-all | bytes 3538944 | tf_op jit(solution)/shard_map/all_to_all | solution.py:226
  280.1 2.6 reshape.338
  282.7 3.4 fusion.85
  286.1 2.5 multiply_convert_fusion.1
  288.7 1.5 copy.91
  290.2 3.9 %convert_reduce_fusion = bf16[576,1536]{1,0:T(8,128)(2,1)S(1)} fusion(bf16[576,4,192]{0,2,1:T(8,128)(2,1)S(1)} %bitcast.114, bf16[4,192,1536]{2,1,0:T(8,128)(2,1)} %bitcast.122), kind=kOutput, calls=%fused_computation.23 | convolution fusion | flops 1365147648 | bytes 5013504 | tf_op jit(solution)/shard_map/rqf,qfd->qrd/dot_general | solution.py:233
  294.1 1.7 reshape.341
  295.8 5.8 %all-to-all-start.2 = ((bf16[32,18,1536]{2,1,0:T(8,128)(2,1)}), bf16[32,18,1536]{2,1,0:T(8,128)(2,1)}, u32[]{:S(2)}, u32[]{:S(2)}) async-start(bf16[32,18,1536]{2,1,0:T(8,128)(2,1)} %reshape.341), calls=%async_computation.2 | async-start | bytes 4718592 | tf_op jit(solution)/shard_map/all_to_all | solution.py:240
  302.8 0.6 select_reduce_fusion
  303.3 29.6 %all-to-all-done.2 = bf16[32,18,1536]{2,1,0:T(8,128)(2,1)} async-done(((bf16[32,18,1536]{2,1,0:T(8,128)(2,1)}), bf16[32,18,1536]{2,1,0:T(8,128)(2,1)}, u32[]{:S(2)}, u32[]{:S(2)}) %all-to-all-start.2) | async-done | bytes 1769504 | tf_op jit(solution)/shard_map/all_to_all | solution.py:240
  333.0 2.6 reshape.342
  335.6 4.3 %fusion.86 = f32[384,1536]{1,0:T(8,128)} fusion(f32[384,576]{0,1:T(8,128)S(1)} %select_reduce_fusion, bf16[576,1536]{1,0:T(8,128)(2,1)S(1)} %reshape.342), kind=kOutput, calls=%fused_computation.166 | convolution fusion | flops 4076863488 | bytes 5013504 | tf_op jit(solution)/shard_map/dot_general | solution.py:251
  340.8 29.6 %reduce-scatter.2.cloned.1.call-done = f32[384,384]{1,0:T(8,128)} async-done(((f32[384,1536]{1,0:T(8,128)}), f32[384,384]{1,0:T(8,128)}) %reduce-scatter.2.cloned.1.call-update) | async-done | bytes 589840 | tf_op jit(solution)/shard_map/reduce_scatter | solution.py:257
  370.4 2.1 select_convert_fusion
  (126 shorter events, 5.3 us)
Async XLA Ops:
  6.5 1.6 copy-start
  6.5 2.0 copy-start.12
  6.5 2.9 copy-start.19
  6.5 71.8 %all-gather.11.cloned.1.call-start = ((), (), s32[]{:S(2)}) async-start(), calls=%async_computation.4 | async-start | bytes 1474560 | tf_op jit(solution)/shard_map/all_gather | solution.py:63
  7.3 145.6 %all-gather.15.cloned.1.call-start = ((), (), s32[]{:S(2)}) async-start(), calls=%async_computation.8 | async-start | bytes 2949120 | tf_op jit(solution)/shard_map/all_gather | solution.py:163
  19.0 12.3 %copy-start.13 = (s32[384,4]{0,1:T(4,128)S(1)}, s32[384,4]{0,1:T(4,128)}, u32[]{:S(2)}) copy-start(s32[384,4]{0,1:T(4,128)} %param.29) | copy-start | bytes 18436
  19.0 12.8 %copy-start.17 = (f32[384]{0:T(512)S(1)}, f32[384]{0:T(512)}, u32[]{:S(2)}) copy-start(f32[384]{0:T(512)} %param.19) | copy-start | bytes 4612
  19.0 70.0 %all-to-all-start = ((bf16[32,4,2,64,128]{4,3,2,1,0:T(8,128)(2,1)}), bf16[32,4,2,64,128]{4,3,2,1,0:T(8,128)(2,1)}, u32[]{:S(2)}, u32[]{:S(2)}) async-start(bf16[32,4,2,64,128]{4,3,2,1,0:T(8,128)(2,1)} %copy.85), calls=%async_computation | async-start | bytes 8388608 | tf_op jit(solution)/shard_map/all_to_all | solution.py:103
  30.4 37.9 %copy-start.18 = (f32[384]{0:T(512)S(1)}, f32[384]{0:T(512)}, u32[]{:S(2)}) copy-start(f32[384]{0:T(512)} %param.28) | copy-start | bytes 4612
  30.5 122.4 %all-gather.17.cloned.1.call-start = ((), (), s32[]{:S(2)}) async-start(), calls=%async_computation.9 | async-start | bytes 2949120 | tf_op jit(solution)/shard_map/all_gather | solution.py:164
  31.2 193.5 %all-reduce.2.cloned.1.call-start = ((), (), s32[]{:S(2)}) async-start(), calls=%async_computation.5 | async-start | bytes 2359296 | tf_op jit(solution)/shard_map/psum | solution.py:213
  31.3 45.0 %copy-start.15 = (f32[64]{0:T(128)}, f32[64]{0:T(128)S(1)}, u32[]{:S(2)}) copy-start(f32[64]{0:T(128)S(1)} %multiply_power_fusion) | copy-start | bytes 772
  31.6 44.7 %copy-start.9 = (bf16[1536,256]{1,0:T(8,128)(2,1)S(1)}, bf16[1536,256]{1,0:T(8,128)(2,1)}, u32[]{:S(2)}) copy-start(bf16[1536,256]{1,0:T(8,128)(2,1)} %param.22) | copy-start | bytes 2359300
  82.7 3.1 copy-start.2
  83.8 2.0 copy-start.7
  83.8 2.0 copy-start.8
  85.4 1.2 copy-start.4
  85.4 1.8 collective-permute-start
  85.9 0.8 copy-start.16
  86.6 0.8 copy-start.10
  152.9 3.7 copy-start.5
  153.3 5.5 %collective-permute-start.2 = (f32[384,3,128]{0,2,1:T(8,128)S(1)}, f32[384,3,128]{0,2,1:T(8,128)S(1)}, u32[]{:S(2)}, u32[]{:S(2)}) collective-permute-start(f32[384,3,128]{0,2,1:T(8,128)S(1)} %slice.80), channel_id=1, source_target_pairs={{0,1},{1,0},{2,3},{3,2},{4,5},{5,4},{6,7},{7,6},{8,9},{9,8},{10,11... | collective-permute-start | bytes 1769480 | tf_op jit(solution)/shard_map/ppermute | solution.py:192
  156.6 2.3 copy-start.11
  157.1 1.4 collective-permute-start.1
  157.6 1.2 collective-permute-start.3
  158.9 1.3 copy-start.6
  160.1 64.5 %copy-start.3 = (bf16[384,1536]{1,0:T(8,128)(2,1)S(1)}, bf16[384,1536]{1,0:T(8,128)(2,1)}, u32[]{:S(2)}) copy-start(bf16[384,1536]{1,0:T(8,128)(2,1)} %all-gather.11.cloned.1.call-done) | copy-start | bytes 3538948
  162.0 128.3 %all-gather.13.cloned.1.call-start = ((), (), s32[]{:S(2)}) async-start(), calls=%async_computation.6 | async-start | bytes 2949120 | tf_op jit(solution)/shard_map/all_gather | solution.py:215
  282.7 3.4 copy-start.20
  295.8 6.1 %copy-start.14 = (f32[384,4]{0,1:T(4,128)S(1)}, f32[384,4]{0,1:T(4,128)}, u32[]{:S(2)}) copy-start(f32[384,4]{0,1:T(4,128)} %param.30) | copy-start | bytes 18436
  295.8 37.1 %all-to-all-start.2 = ((bf16[32,18,1536]{2,1,0:T(8,128)(2,1)}), bf16[32,18,1536]{2,1,0:T(8,128)(2,1)}, u32[]{:S(2)}, u32[]{:S(2)}) async-start(bf16[32,18,1536]{2,1,0:T(8,128)(2,1)} %reshape.341), calls=%async_computation.2 | async-start | bytes 4718592 | tf_op jit(solution)/shard_map/all_to_all | solution.py:240
  301.6 68.8 %reduce-scatter.2.cloned.1.call-start = ((), (), s32[]{:S(2)}) async-start(), calls=%async_computation.7 | async-start | bytes 2949120 | tf_op jit(solution)/shard_map/reduce_scatter | solution.py:257
  340.0 32.5 %copy-start.1 = (bf16[16,2,2,128,128]{4,3,2,1,0:T(8,128)(2,1)S(1)}, bf16[16,2,2,128,128]{4,3,2,1,0:T(8,128)(2,1)}, u32[]{:S(2)}) copy-start(bf16[16,2,2,128,128]{4,3,2,1,0:T(8,128)(2,1)} %param.24) | copy-start | bytes 6291460
Sparse Core Ops, SparseCore 0:
  9.0 44.2 all-gather.10
  55.0 55.5 all-gather.14
  112.2 32.2 all-gather.16
  162.1 62.5 all-reduce.1
  227.9 57.5 all-gather.12
  340.1 30.2 reduce-scatter.1

commit v6 on v5

--- a/solution.py
+++ b/solution.py
@@ -186,8 +186,9 @@
         jnp.zeros((rows_here, six, HD), jnp.float32),
     )
     (pre_max, pre_sum, pre_weighted), _ = lax.scan(absorb, start_state, block_inputs)
-    gate_full, up_full, pre_max, pre_sum, pre_weighted = lax.optimization_barrier(
-        (gate_full, up_full, pre_max, pre_sum, pre_weighted)
+    out_full = lax.all_gather(w_out, "tp", axis=0, tiled=True)
+    gate_full, up_full, out_full, pre_max, pre_sum, pre_weighted = lax.optimization_barrier(
+        (gate_full, up_full, out_full, pre_max, pre_sum, pre_weighted)
     )
     back = lax.ppermute(
         (pre_max[:, heads_here:], pre_sum[:, heads_here:], pre_weighted[:, heads_here:]),
@@ -209,11 +210,10 @@
     attention = (
         (weighted / row_sum[:, :, None]).astype(jnp.bfloat16).reshape(rows_here, heads_here * HD)
     )
-    proj_part = jnp.dot(attention, w_out, preferred_element_type=jnp.float32)
-    attn_sum = lax.psum(proj_part.astype(jnp.bfloat16), "tp")
-    down_local, attn_sum = lax.optimization_barrier((w_down[0], attn_sum))
+    attention_all = lax.all_gather(attention, "tp", axis=1, tiled=True)
+    down_local, attention_all = lax.optimization_barrier((w_down[0], attention_all))
     down_full = lax.all_gather(down_local, "tp", axis=0, tiled=True)
-    attn_full = attn_sum.astype(jnp.float32)
+    attn_full = jnp.dot(attention_all, out_full, preferred_element_type=jnp.float32)
     residual_full = full_in + attn_full
     sq_mid = jnp.sum(residual_full * residual_full, axis=1)
     full_rows = (residual_full * lax.rsqrt(sq_mid / D + EPSILON)[:, None] * norm_moe).astype(

time: 381 us -> 387 us (1.016)
  matrix products: 60.4 us -> 68.6 us
  waiting for transfers between devices: 126 us -> 131 us
    all_gather x0 -> x2, waiting for transfers between devices: none -> 66.2 us  [the longest x1 43.6 us: body(): out_full = lax.all_gather(w_out, 'tp', axis=0, tiled=True)]
    psum x1 -> x0, waiting for transfers between devices: 62.5 us -> none  [body(): attn_sum = lax.psum(proj_part.astype(jnp.bfloat16), 'tp')]
    dot_general x1, matrix products: 1.81 us -> 6.22 us  [body(): jnp.dot(attention_all, out_full, preferred_element_type=jnp.float32)]
  transfers between devices with their start and end apart: 12 -> 13, of which waited for: 7 -> 8; matrix products, arithmetic and copies ran while one was open for 32% -> 32% of each run, Pallas kernels for 0% -> 0%
where the time goes in v6:
time: 387 us; the launch traced here: 386 us
  waiting for transfers between devices  131 us (34%)
  blocking collectives  69.3 us (18%)
  matrix products  68.6 us (18%)
  other arithmetic  45.5 us (12%)
  local copies, waits for them, and re-layouts  35.7 us (9%)
  starting transfers between devices  19.2 us (5%)
  between operations  16.8 us (4%)
    all_gather x1, waiting for transfers between devices, body(): out_full = lax.all_gather(w_out, 'tp', axis=0, tiled=True)  43.6 us
    all_to_all x1, blocking collectives, body(): lax.all_to_all(outgoing_rows, 'req', split_axis=0, concat_axis=0, tiled=T...  41.3 us
    reduce_scatter x1, waiting for transfers between devices, body(): moe_part = lax.psum_scatter(moe_full, 'tp', scatter_dimension=1, tiled=True)  29.8 us
    all_to_all x1, waiting for transfers between devices, body(): lax.all_to_all(expert_out.reshape(src_count, item_count, width_all), 'req...  29.7 us
    unnamed x2, blocking collectives  28 us
    all_gather x1, waiting for transfers between devices, body(): attention_all = lax.all_gather(attention, 'tp', axis=1, tiled=True)  22.6 us
    dot_general x2, matrix products, absorb(): jnp.einsum('thd,kd->thk', query_six, key_block, preferred_element_type=jn...  20.2 us
    reduce_sum x2, other arithmetic, absorb(): new_sum = old_sum * rescale + jnp.sum(block_weights, axis=2)  18.9 us
  transfers between devices with their start and end apart: 13, of which 8 were waited for; matrix products, arithmetic and copies ran while one was open for 32% of the time, Pallas kernels for 0%

profile of v6, /device:TPU:1, one launch (start us, length us, event | category | flops | bytes accessed | tf_op | source)
XLA Modules:
  0.0 386.2 jit_solution(3322377746028752989)
XLA Ops:
  6.5 0.7 all-gather.13.cloned.1.call-update
  7.3 0.7 all-gather.21.cloned.1.call-update
  8.1 0.7 all-gather.23.cloned.1.call-update
  9.5 0.6 multiply_reduce_fusion.1
  10.2 3.2 convolution_convert_fusion
  13.3 3.4 copy.99
  16.8 2.9 copy.85
  19.7 11.4 %all-to-all-start = ((bf16[32,4,2,64,128]{4,3,2,1,0:T(8,128)(2,1)}), bf16[32,4,2,64,128]{4,3,2,1,0:T(8,128)(2,1)}, u32[]{:S(2)}, u32[]{:S(2)}) async-start(bf16[32,4,2,64,128]{4,3,2,1,0:T(8,128)(2,1)} %copy.85), calls=%async_computation | async-start | bytes 8388608 | tf_op jit(solution)/shard_map/all_to_all | solution.py:103
  31.2 0.5 all-gather.15.cloned.1.call-update
  32.3 22.8 %all-gather.4 = f32[4,1,384]{2,1,0:T(1,128)S(1)} all-gather(f32[1,1,384]{2,1,0:T(1,128)S(1)} %reshape.363), channel_id=2, replica_groups=mesh['req'=32,'tp'=4] {'tp'}, dimensions={0}, use_global_device_ids=true | all-gather | bytes 7680 | tf_op args[1]
  55.1 0.6 dynamic_slice.30
  58.2 0.6 pad_clamp_fusion.1
  58.8 9.1 %reduce-window.18 = s32[32,12,128]{2,1,0:T(8,128)S(1)} reduce-window(s32[32,12,128]{2,1,0:T(8,128)S(1)} %fusion.41, s32[]{:T(128)} %constant.196.clone.1), window={size=1x1x128 pad=0_0x0_0x127_0}, to_apply=%region_2.3 | reduce-window | flops 6242304 | bytes 393220 | tf_op jit(solution)/shard_map/reduce-window
  68.3 5.3 %all-gather.5 = f32[4,1,384]{2,1,0:T(1,128)S(1)} all-gather(f32[1,1,384]{2,1,0:T(1,128)S(1)} %reshape.365), channel_id=3, replica_groups=mesh['req'=32,'tp'=4] {'tp'}, dimensions={0}, use_global_device_ids=true | all-gather | bytes 7680 | tf_op args[10]
  74.0 0.8 select_reduce_fusion.1
  74.8 1.5 multiply_cosine_fusion
  76.3 2.0 constant_dynamic-slice_fusion.2
  78.3 1.6 fusion.18
  79.9 2.5 fusion.39
  82.7 1.1 copy.97
  83.8 1.4 subtract_convert_fusion
  85.4 0.4 collective-permute-start
  85.9 0.7 fusion.30
  86.7 0.4 fusion.49
  87.5 2.2 all-to-all-done
  89.7 4.5 %gather_fusion = bf16[16,4,2,64,128]{4,3,2,1,0:T(8,128)(2,1)} fusion(bf16[32,4,2,64,128]{4,3,2,1,0:T(8,128)(2,1)} %all-to-all-done, s32[1024]{0:T(1024)} %pad_clamp_fusion.1), kind=kCustom, calls=%fused_computation | custom fusion | bytes 4194368 | tf_op jit(solution)/shard_map/jit(_take)/gather | solution.py:117
  94.2 1.9 broadcast_select_fusion.1
  96.1 1.2 fusion.83
  97.3 56.2 %while.15 = (s32[]{:T(128)}, f32[384,6]{0,1:T(8,128)S(1)}, f32[384,6]{0,1:T(8,128)S(1)}, f32[384,6,128]{2,0,1:T(8,128)S(1)}, bf16[2,2048,128]{2,1,0:T(8,128)(2,1...) while((s32[]{:T(128)}, f32[384,6]{0,1:T(8,128)S(1)}, ...), condition=%wide.region_14.15_spmd.clone, body=%wide.region_11.14_spmd.clone.sunk | while | flops 2454564096 | bytes 60775016 | solution.py:188
  97.3 10.1 %bitcast_reduce_fusion.2 = (f32[384,6]{0,1:T(8,128)S(1)}, f32[2048,384,6]{1,0,2:T(8,128)}) fusion(bf16[384,6,128]{2,0,1:T(8,128)(2,1)S(1)} %get-tuple-element.217, bf16[2,2048,128]{2,1,0:T(8,128)(2,1)} %get-tuple-element.216, s32[]{:T(128)} %get-tuple-element.203), kind=kOutput, calls=%fused_computation.3.clone.1 | convolution fusion | flops 1217394432 | bytes 19998208 | tf_op jit(solution)/shard_map/while/body/eval_jaxpr/thd,kd->thk/dot_general | solution.py:144
  107.4 9.4 %fusion.110 = f32[384,6]{0,1:T(8,128)S(1)} fusion(f32[2048,384,6]{1,0,2:T(8,128)} %get-tuple-element.191, f32[384,6]{0,1:T(8,128)S(1)} %select_maximum_fusion.2), kind=kLoop, calls=%fused_computation.6.clone.1 | loop fusion | flops 14153472 | bytes 18892800 | tf_op jit(solution)/shard_map/while/body/eval_jaxpr/reduce_sum | solution.py:150
  116.8 8.7 %fusion.112 = f32[384,6,128]{2,0,1:T(8,128)S(1)} fusion(f32[2048,384,6]{1,0,2:T(8,128)} %get-tuple-element.191, f32[384,6]{0,1:T(8,128)S(1)} %select_maximum_fusion.2, f32[384,6,128]{2,0,1:T(8,128)S(1)} %get-tuple-element.206, f32[384,6]{0,1:T(8,128)S(1)} %get-tuple-element.193, pred[]{:T(512)S(6)} %compare.13, ...), kind=kOutput, calls=%fused_computation.8.clone.1 | convolution fusion | flops 1223000064 | bytes 21782532 | tf_op jit(solution)/shard_map/while/body/eval_jaxpr/thk,kd->thd/dot_general | solution.py:151
  125.6 10.1 %bitcast_reduce_fusion.2 = (f32[384,6]{0,1:T(8,128)S(1)}, f32[2048,384,6]{1,0,2:T(8,128)}) fusion(bf16[384,6,128]{2,0,1:T(8,128)(2,1)S(1)} %get-tuple-element.217, bf16[2,2048,128]{2,1,0:T(8,128)(2,1)} %get-tuple-element.216, s32[]{:T(128)} %get-tuple-element.203), kind=kOutput, calls=%fused_computation.3.clone.1 | convolution fusion | flops 1217394432 | bytes 19998208 | tf_op jit(solution)/shard_map/while/body/eval_jaxpr/thd,kd->thk/dot_general | solution.py:144
  135.7 9.5 %fusion.110 = f32[384,6]{0,1:T(8,128)S(1)} fusion(f32[2048,384,6]{1,0,2:T(8,128)} %get-tuple-element.191, f32[384,6]{0,1:T(8,128)S(1)} %select_maximum_fusion.2), kind=kLoop, calls=%fused_computation.6.clone.1 | loop fusion | flops 14153472 | bytes 18892800 | tf_op jit(solution)/shard_map/while/body/eval_jaxpr/reduce_sum | solution.py:150
  145.3 8.2 %fusion.112 = f32[384,6,128]{2,0,1:T(8,128)S(1)} fusion(f32[2048,384,6]{1,0,2:T(8,128)} %get-tuple-element.191, f32[384,6]{0,1:T(8,128)S(1)} %select_maximum_fusion.2, f32[384,6,128]{2,0,1:T(8,128)S(1)} %get-tuple-element.206, f32[384,6]{0,1:T(8,128)S(1)} %get-tuple-element.193, pred[]{:T(512)S(6)} %compare.13, ...), kind=kOutput, calls=%fused_computation.8.clone.1 | convolution fusion | flops 1223000064 | bytes 21782532 | tf_op jit(solution)/shard_map/while/body/eval_jaxpr/thk,kd->thd/dot_general | solution.py:151
  153.5 43.6 %all-gather.15.cloned.1.call-done = bf16[1536,1536]{1,0:T(8,128)(2,1)} async-done(((bf16[384,1536]{1,0:T(8,128)(2,1)}), bf16[1536,1536]{1,0:T(8,128)(2,1)}) %all-gather.15.cloned.1.call-update) | async-done | bytes 4718608 | tf_op jit(solution)/shard_map/all_gather | solution.py:189
  197.1 0.4 copy.86
  197.6 0.5 fusion.21
  198.2 0.6 collective-permute-start.1
  198.7 0.3 collective-permute-start.3
  199.1 0.4 fusion.22
  199.6 0.3 collective-permute-done.3
  200.0 2.5 fusion.37
  202.7 22.6 %all-gather.17.cloned.1.call-done = bf16[384,1536]{0,1:T(8,128)(2,1)} async-done(((bf16[384,384]{0,1:T(8,128)(2,1)}), bf16[384,1536]{0,1:T(8,128)(2,1)}) %all-gather.17.cloned.1.call-update) | async-done | bytes 1179664 | tf_op jit(solution)/shard_map/all_gather | solution.py:213
  225.3 6.2 %multiply_reduce_fusion = (f32[384]{0:T(512)S(1)}, f32[384,1536]{1,0:T(8,128)}) fusion(bf16[384,1536]{0,1:T(8,128)(2,1)} %all-gather.17.cloned.1.call-done, bf16[1536,1536]{1,0:T(8,128)(2,1)} %all-gather.15.cloned.1.call-done, bf16[384,1536]{1,0:T(8,128)(2,1)S(1)} %copy-done.3), kind=kOutput, calls=%fused_computation.36 | convolution fusion | flops 1814298240 | bytes 9438720 | tf_op jit(solution)/shard_map/dot_general | solution.py:216
  231.6 1.9 multiply_convert_fusion
  233.5 3.6 gather_fusion.1
  237.1 3.6 gather.12
  240.7 2.1 broadcast_select_fusion
  242.8 41.3 %all_to_all.15 = bf16[32,18,1536]{2,1,0:T(8,128)(2,1)} all-to-all(bf16[32,18,1536]{2,1,0:T(8,128)(2,1)S(1)} %broadcast_select_fusion), channel_id=1, replica_groups=mesh['req'=32,'tp'=4] {'req'}, dimensions={0} | all-to-all | bytes 3538944 | tf_op jit(solution)/shard_map/all_to_all | solution.py:226
  284.1 2.6 reshape.338
  286.7 3.4 fusion.85
  290.1 2.6 multiply_convert_fusion.1
  292.7 1.5 copy.91
  294.2 3.9 %convert_reduce_fusion = bf16[576,1536]{1,0:T(8,128)(2,1)S(1)} fusion(bf16[576,4,192]{0,2,1:T(8,128)(2,1)S(1)} %bitcast.114, bf16[4,192,1536]{2,1,0:T(8,128)(2,1)} %bitcast.122), kind=kOutput, calls=%fused_computation.23 | convolution fusion | flops 1365147648 | bytes 5013504 | tf_op jit(solution)/shard_map/rqf,qfd->qrd/dot_general | solution.py:233
  298.1 1.7 reshape.341
  299.8 5.8 %all-to-all-start.2 = ((bf16[32,18,1536]{2,1,0:T(8,128)(2,1)}), bf16[32,18,1536]{2,1,0:T(8,128)(2,1)}, u32[]{:S(2)}, u32[]{:S(2)}) async-start(bf16[32,18,1536]{2,1,0:T(8,128)(2,1)} %reshape.341), calls=%async_computation.2 | async-start | bytes 4718592 | tf_op jit(solution)/shard_map/all_to_all | solution.py:240
  305.7 0.3 reduce-scatter.2.cloned.1.call-start
  306.8 0.6 select_reduce_fusion
  307.4 29.7 %all-to-all-done.2 = bf16[32,18,1536]{2,1,0:T(8,128)(2,1)} async-done(((bf16[32,18,1536]{2,1,0:T(8,128)(2,1)}), bf16[32,18,1536]{2,1,0:T(8,128)(2,1)}, u32[]{:S(2)}, u32[]{:S(2)}) %all-to-all-start.2) | async-done | bytes 1769504 | tf_op jit(solution)/shard_map/all_to_all | solution.py:240
  337.0 3.8 reshape.342
  340.9 6.0 %fusion.86 = f32[384,1536]{1,0:T(8,128)} fusion(f32[384,576]{0,1:T(8,128)S(1)} %select_reduce_fusion, bf16[576,1536]{1,0:T(8,128)(2,1)} %reshape.342), kind=kOutput, calls=%fused_computation.165 | convolution fusion | flops 4076863488 | bytes 5013504 | tf_op jit(solution)/shard_map/dot_general | solution.py:251
  347.6 29.8 %reduce-scatter.2.cloned.1.call-done = f32[384,384]{1,0:T(8,128)} async-done(((f32[384,1536]{1,0:T(8,128)}), f32[384,384]{1,0:T(8,128)}) %reduce-scatter.2.cloned.1.call-update) | async-done | bytes 589840 | tf_op jit(solution)/shard_map/reduce_scatter | solution.py:257
  377.3 2.1 select_convert_fusion
  (128 shorter events, 5.0 us)
Async XLA Ops:
  6.5 2.2 copy-start
  6.5 2.7 copy-start.12
  6.5 3.6 copy-start.19
  6.5 71.8 %all-gather.13.cloned.1.call-start = ((), (), s32[]{:S(2)}) async-start(), calls=%async_computation.4 | async-start | bytes 1474560 | tf_op jit(solution)/shard_map/all_gather | solution.py:63
  7.3 146.2 %all-gather.21.cloned.1.call-start = ((), (), s32[]{:S(2)}) async-start(), calls=%async_computation.9 | async-start | bytes 2949120 | tf_op jit(solution)/shard_map/all_gather | solution.py:163
  8.0 145.5 %all-gather.23.cloned.1.call-start = ((), (), s32[]{:S(2)}) async-start(), calls=%async_computation.10 | async-start | bytes 2949120 | tf_op jit(solution)/shard_map/all_gather | solution.py:164
  19.7 12.1 %copy-start.13 = (s32[384,4]{0,1:T(4,128)S(1)}, s32[384,4]{0,1:T(4,128)}, u32[]{:S(2)}) copy-start(s32[384,4]{0,1:T(4,128)} %param.29) | copy-start | bytes 18436
  19.7 12.6 %copy-start.17 = (f32[384]{0:T(512)S(1)}, f32[384]{0:T(512)}, u32[]{:S(2)}) copy-start(f32[384]{0:T(512)} %param.19) | copy-start | bytes 4612
  19.7 70.0 %all-to-all-start = ((bf16[32,4,2,64,128]{4,3,2,1,0:T(8,128)(2,1)}), bf16[32,4,2,64,128]{4,3,2,1,0:T(8,128)(2,1)}, u32[]{:S(2)}, u32[]{:S(2)}) async-start(bf16[32,4,2,64,128]{4,3,2,1,0:T(8,128)(2,1)} %copy.85), calls=%async_computation | async-start | bytes 8388608 | tf_op jit(solution)/shard_map/all_to_all | solution.py:103
  31.1 37.2 %copy-start.18 = (f32[384]{0:T(512)S(1)}, f32[384]{0:T(512)}, u32[]{:S(2)}) copy-start(f32[384]{0:T(512)} %param.28) | copy-start | bytes 4612
  31.2 166.0 %all-gather.15.cloned.1.call-start = ((), (), s32[]{:S(2)}) async-start(), calls=%async_computation.5 | async-start | bytes 5898240 | tf_op jit(solution)/shard_map/all_gather | solution.py:189
  31.7 44.6 %copy-start.9 = (bf16[1536,256]{1,0:T(8,128)(2,1)S(1)}, bf16[1536,256]{1,0:T(8,128)(2,1)}, u32[]{:S(2)}) copy-start(bf16[1536,256]{1,0:T(8,128)(2,1)} %param.22) | copy-start | bytes 2359300
  31.7 193.6 %all-gather.17.cloned.1.call-start = ((), (), s32[]{:S(2)}) async-start(), calls=%async_computation.6 | async-start | bytes 1474560 | tf_op jit(solution)/shard_map/all_gather | solution.py:213
  31.8 46.5 %copy-start.15 = (f32[64]{0:T(128)}, f32[64]{0:T(128)S(1)}, u32[]{:S(2)}) copy-start(f32[64]{0:T(128)S(1)} %multiply_power_fusion) | copy-start | bytes 772
  82.7 3.2 copy-start.2
  83.8 2.0 copy-start.7
  83.8 2.1 copy-start.8
  85.4 1.2 copy-start.5
  85.4 1.8 collective-permute-start
  85.9 0.8 copy-start.16
  86.6 0.7 copy-start.10
  153.5 44.2 %copy-start.6 = (bf16[384,3,128]{2,0,1:T(8,128)(2,1)S(1)}, bf16[384,3,128]{2,0,1:T(8,128)(2,1)}, u32[]{:S(2)}) copy-start(bf16[384,3,128]{2,0,1:T(8,128)(2,1)} %copy-done.5) | copy-start | bytes 884740
  197.5 2.0 copy-start.4
  197.5 2.4 collective-permute-start.2
  197.6 2.3 copy-start.11
  198.2 1.4 collective-permute-start.1
  198.7 1.2 collective-permute-start.3
  200.0 25.4 %copy-start.3 = (bf16[384,1536]{1,0:T(8,128)(2,1)S(1)}, bf16[384,1536]{1,0:T(8,128)(2,1)}, u32[]{:S(2)}) copy-start(bf16[384,1536]{1,0:T(8,128)(2,1)} %all-gather.13.cloned.1.call-done) | copy-start | bytes 3538948
  202.5 91.7 %all-gather.19.cloned.1.call-start = ((), (), s32[]{:S(2)}) async-start(), calls=%async_computation.7 | async-start | bytes 2949120 | tf_op jit(solution)/shard_map/all_gather | solution.py:215
  286.7 3.4 copy-start.20
  299.8 6.2 %copy-start.14 = (f32[384,4]{0,1:T(4,128)S(1)}, f32[384,4]{0,1:T(4,128)}, u32[]{:S(2)}) copy-start(f32[384,4]{0,1:T(4,128)} %param.30) | copy-start | bytes 18436
  299.8 37.2 %all-to-all-start.2 = ((bf16[32,18,1536]{2,1,0:T(8,128)(2,1)}), bf16[32,18,1536]{2,1,0:T(8,128)(2,1)}, u32[]{:S(2)}, u32[]{:S(2)}) async-start(bf16[32,18,1536]{2,1,0:T(8,128)(2,1)} %reshape.341), calls=%async_computation.2 | async-start | bytes 4718592 | tf_op jit(solution)/shard_map/all_to_all | solution.py:240
  305.7 71.6 %reduce-scatter.2.cloned.1.call-start = ((), (), s32[]{:S(2)}) async-start(), calls=%async_computation.8 | async-start | bytes 2949120 | tf_op jit(solution)/shard_map/reduce_scatter | solution.py:257
  340.9 38.5 %copy-start.1 = (bf16[16,2,2,128,128]{4,3,2,1,0:T(8,128)(2,1)S(1)}, bf16[16,2,2,128,128]{4,3,2,1,0:T(8,128)(2,1)}, u32[]{:S(2)}) copy-start(bf16[16,2,2,128,128]{4,3,2,1,0:T(8,128)(2,1)} %param.24) | copy-start | bytes 6291460
Sparse Core Ops, SparseCore 0:
  9.0 26.3 all-gather.12
  37.1 72.6 all-gather.20
  111.5 32.2 all-gather.22
  145.3 51.7 all-gather.14
  202.6 22.6 all-gather.16
  231.7 57.4 all-gather.18
  347.0 30.2 reduce-scatter.1

commit v7 on v6

--- a/solution.py
+++ b/solution.py
@@ -161,7 +161,6 @@
         values_pre.reshape(block_count, block_len, HD),
     )
     gate_full = lax.all_gather(w_gate[0], "tp", axis=1, tiled=True)
-    up_full = lax.all_gather(w_up[0], "tp", axis=1, tiled=True)
     expert_count = w_gate.shape[0] * req_count
     capacity = 3 * rows_here * TOP // (2 * expert_count)
     sub = capacity // tp_count
@@ -187,8 +186,8 @@
     )
     (pre_max, pre_sum, pre_weighted), _ = lax.scan(absorb, start_state, block_inputs)
     out_full = lax.all_gather(w_out, "tp", axis=0, tiled=True)
-    gate_full, up_full, out_full, pre_max, pre_sum, pre_weighted = lax.optimization_barrier(
-        (gate_full, up_full, out_full, pre_max, pre_sum, pre_weighted)
+    gate_full, out_full, pre_max, pre_sum, pre_weighted = lax.optimization_barrier(
+        (gate_full, out_full, pre_max, pre_sum, pre_weighted)
     )
     back = lax.ppermute(
         (pre_max[:, heads_here:], pre_sum[:, heads_here:], pre_weighted[:, heads_here:]),
@@ -211,7 +210,10 @@
         (weighted / row_sum[:, :, None]).astype(jnp.bfloat16).reshape(rows_here, heads_here * HD)
     )
     attention_all = lax.all_gather(attention, "tp", axis=1, tiled=True)
-    down_local, attention_all = lax.optimization_barrier((w_down[0], attention_all))
+    up_local, down_local, attention_all = lax.optimization_barrier(
+        (w_up[0], w_down[0], attention_all)
+    )
+    up_full = lax.all_gather(up_local, "tp", axis=1, tiled=True)
     down_full = lax.all_gather(down_local, "tp", axis=0, tiled=True)
     attn_full = jnp.dot(attention_all, out_full, preferred_element_type=jnp.float32)
     residual_full = full_in + attn_full

time: 387 us -> 393 us (1.016)
    all_gather x1, waiting for transfers between devices: 43.6 us -> 11 us  [body(): out_full = lax.all_gather(w_out, 'tp', axis=0, tiled=True)]
    all_gather x1, waiting for transfers between devices: 0.02 us -> 20.3 us  [body(): down_full = lax.all_gather(down_local, 'tp', axis=0, tiled=True)]
    all_gather x1, waiting for transfers between devices: 22.6 us -> 33.9 us  [body(): attention_all = lax.all_gather(attention, 'tp', axis=1, tiled=True)]
  transfers between devices with their start and end apart: 13 -> 13, of which waited for: 8 -> 9; matrix products, arithmetic and copies ran while one was open for 32% -> 34% of each run, Pallas kernels for 0% -> 0%
where the time goes in v7:
time: 393 us; the launch traced here: 392 us
  waiting for transfers between devices  129 us (33%)
  matrix products  72 us (18%)
  blocking collectives  69.9 us (18%)
  other arithmetic  45.5 us (12%)
  local copies, waits for them, and re-layouts  36 us (9%)
  starting transfers between devices  22.7 us (6%)
  between operations  16.7 us (4%)
    all_to_all x1, blocking collectives, body(): lax.all_to_all(outgoing_rows, 'req', split_axis=0, concat_axis=0, tiled=T...  41.3 us
    all_gather x1, waiting for transfers between devices, body(): attention_all = lax.all_gather(attention, 'tp', axis=1, tiled=True)  33.9 us
    all_to_all x1, waiting for transfers between devices, body(): lax.all_to_all(expert_out.reshape(src_count, item_count, width_all), 'req...  30.2 us
    reduce_scatter x1, waiting for transfers between devices, body(): moe_part = lax.psum_scatter(moe_full, 'tp', scatter_dimension=1, tiled=True)  29.7 us
    unnamed x2, blocking collectives  28.6 us
    dot_general x2, matrix products, absorb(): jnp.einsum('thd,kd->thk', query_six, key_block, preferred_element_type=jn...  20.3 us
    all_gather x1, waiting for transfers between devices, body(): down_full = lax.all_gather(down_local, 'tp', axis=0, tiled=True)  20.3 us
    reduce_sum x2, other arithmetic, absorb(): new_sum = old_sum * rescale + jnp.sum(block_weights, axis=2)  19 us
  transfers between devices with their start and end apart: 13, of which 9 were waited for; matrix products, arithmetic and copies ran while one was open for 34% of the time, Pallas kernels for 0%

profile of v7, /device:TPU:1, one launch (start us, length us, event | category | flops | bytes accessed | tf_op | source)
XLA Modules:
  0.0 392.1 jit_solution(10053266542937013786)
XLA Ops:
  6.5 0.7 all-gather.12.cloned.1.call-update
  7.3 0.7 all-gather.22.cloned.1.call-update
  8.9 0.6 multiply_reduce_fusion.1
  9.5 3.2 convolution_convert_fusion
  12.6 3.4 copy.99
  16.1 2.9 copy.85
  19.0 11.4 %all-to-all-start = ((bf16[32,4,2,64,128]{4,3,2,1,0:T(8,128)(2,1)}), bf16[32,4,2,64,128]{4,3,2,1,0:T(8,128)(2,1)}, u32[]{:S(2)}, u32[]{:S(2)}) async-start(bf16[32,4,2,64,128]{4,3,2,1,0:T(8,128)(2,1)} %copy.85), calls=%async_computation | async-start | bytes 8388608 | tf_op jit(solution)/shard_map/all_to_all | solution.py:103
  30.5 0.7 all-gather.14.cloned.1.call-update
  31.8 23.3 %all-gather.3 = f32[4,1,384]{2,1,0:T(1,128)S(1)} all-gather(f32[1,1,384]{2,1,0:T(1,128)S(1)} %reshape.362), channel_id=2, replica_groups=mesh['req'=32,'tp'=4] {'tp'}, dimensions={0}, use_global_device_ids=true | all-gather | bytes 7680 | tf_op args[1]
  55.1 0.6 dynamic_slice.30
  58.2 0.6 pad_clamp_fusion.1
  58.8 9.1 %reduce-window.18 = s32[32,12,128]{2,1,0:T(8,128)S(1)} reduce-window(s32[32,12,128]{2,1,0:T(8,128)S(1)} %fusion.41, s32[]{:T(128)} %constant.196.clone.1), window={size=1x1x128 pad=0_0x0_0x127_0}, to_apply=%region_2.3 | reduce-window | flops 6242304 | bytes 393220 | tf_op jit(solution)/shard_map/reduce-window
  68.4 5.3 %all-gather.4 = f32[4,1,384]{2,1,0:T(1,128)S(1)} all-gather(f32[1,1,384]{2,1,0:T(1,128)S(1)} %reshape.364), channel_id=3, replica_groups=mesh['req'=32,'tp'=4] {'tp'}, dimensions={0}, use_global_device_ids=true | all-gather | bytes 7680 | tf_op args[10]
  74.0 0.8 select_reduce_fusion.1
  74.8 1.5 multiply_cosine_fusion
  76.3 2.0 constant_dynamic-slice_fusion.2
  78.3 1.6 fusion.18
  79.9 2.5 fusion.39
  82.7 1.1 copy.97
  83.8 1.4 subtract_convert_fusion
  85.4 0.4 collective-permute-start
  85.9 0.7 fusion.30
  86.7 0.4 fusion.49
  87.5 1.5 all-to-all-done
  89.0 4.6 %gather_fusion = bf16[16,4,2,64,128]{4,3,2,1,0:T(8,128)(2,1)} fusion(bf16[32,4,2,64,128]{4,3,2,1,0:T(8,128)(2,1)} %all-to-all-done, s32[1024]{0:T(1024)} %pad_clamp_fusion.1), kind=kCustom, calls=%fused_computation | custom fusion | bytes 4194368 | tf_op jit(solution)/shard_map/jit(_take)/gather | solution.py:117
  93.7 1.9 broadcast_select_fusion.1
  95.6 1.1 fusion.83
  96.7 56.3 %while.15 = (s32[]{:T(128)}, f32[384,6]{0,1:T(8,128)S(1)}, f32[384,6]{0,1:T(8,128)S(1)}, f32[384,6,128]{2,0,1:T(8,128)S(1)}, bf16[2,2048,128]{2,1,0:T(8,128)(2,1...) while((s32[]{:T(128)}, f32[384,6]{0,1:T(8,128)S(1)}, ...), condition=%wide.region_14.15_spmd.clone, body=%wide.region_11.14_spmd.clone.sunk | while | flops 2454564096 | bytes 60775016 | solution.py:187
  96.7 10.1 %bitcast_reduce_fusion.2 = (f32[384,6]{0,1:T(8,128)S(1)}, f32[2048,384,6]{1,0,2:T(8,128)}) fusion(bf16[384,6,128]{2,0,1:T(8,128)(2,1)S(1)} %get-tuple-element.217, bf16[2,2048,128]{2,1,0:T(8,128)(2,1)} %get-tuple-element.216, s32[]{:T(128)} %get-tuple-element.203), kind=kOutput, calls=%fused_computation.3.clone.1 | convolution fusion | flops 1217394432 | bytes 19998208 | tf_op jit(solution)/shard_map/while/body/eval_jaxpr/thd,kd->thk/dot_general | solution.py:144
  106.8 9.4 %fusion.110 = f32[384,6]{0,1:T(8,128)S(1)} fusion(f32[2048,384,6]{1,0,2:T(8,128)} %get-tuple-element.191, f32[384,6]{0,1:T(8,128)S(1)} %select_maximum_fusion.2), kind=kLoop, calls=%fused_computation.6.clone.1 | loop fusion | flops 14153472 | bytes 18892800 | tf_op jit(solution)/shard_map/while/body/eval_jaxpr/reduce_sum | solution.py:150
  116.3 8.5 %fusion.112 = f32[384,6,128]{2,0,1:T(8,128)S(1)} fusion(f32[2048,384,6]{1,0,2:T(8,128)} %get-tuple-element.191, f32[384,6]{0,1:T(8,128)S(1)} %select_maximum_fusion.2, f32[384,6,128]{2,0,1:T(8,128)S(1)} %get-tuple-element.206, f32[384,6]{0,1:T(8,128)S(1)} %get-tuple-element.193, pred[]{:T(512)S(6)} %compare.13, ...), kind=kOutput, calls=%fused_computation.8.clone.1 | convolution fusion | flops 1223000064 | bytes 21782532 | tf_op jit(solution)/shard_map/while/body/eval_jaxpr/thk,kd->thd/dot_general | solution.py:151
  124.8 10.1 %bitcast_reduce_fusion.2 = (f32[384,6]{0,1:T(8,128)S(1)}, f32[2048,384,6]{1,0,2:T(8,128)}) fusion(bf16[384,6,128]{2,0,1:T(8,128)(2,1)S(1)} %get-tuple-element.217, bf16[2,2048,128]{2,1,0:T(8,128)(2,1)} %get-tuple-element.216, s32[]{:T(128)} %get-tuple-element.203), kind=kOutput, calls=%fused_computation.3.clone.1 | convolution fusion | flops 1217394432 | bytes 19998208 | tf_op jit(solution)/shard_map/while/body/eval_jaxpr/thd,kd->thk/dot_general | solution.py:144
  135.0 9.6 %fusion.110 = f32[384,6]{0,1:T(8,128)S(1)} fusion(f32[2048,384,6]{1,0,2:T(8,128)} %get-tuple-element.191, f32[384,6]{0,1:T(8,128)S(1)} %select_maximum_fusion.2), kind=kLoop, calls=%fused_computation.6.clone.1 | loop fusion | flops 14153472 | bytes 18892800 | tf_op jit(solution)/shard_map/while/body/eval_jaxpr/reduce_sum | solution.py:150
  144.6 8.4 %fusion.112 = f32[384,6,128]{2,0,1:T(8,128)S(1)} fusion(f32[2048,384,6]{1,0,2:T(8,128)} %get-tuple-element.191, f32[384,6]{0,1:T(8,128)S(1)} %select_maximum_fusion.2, f32[384,6,128]{2,0,1:T(8,128)S(1)} %get-tuple-element.206, f32[384,6]{0,1:T(8,128)S(1)} %get-tuple-element.193, pred[]{:T(512)S(6)} %compare.13, ...), kind=kOutput, calls=%fused_computation.8.clone.1 | convolution fusion | flops 1223000064 | bytes 21782532 | tf_op jit(solution)/shard_map/while/body/eval_jaxpr/thk,kd->thd/dot_general | solution.py:151
  153.0 11.0 %all-gather.14.cloned.1.call-done = bf16[1536,1536]{1,0:T(8,128)(2,1)} async-done(((bf16[384,1536]{1,0:T(8,128)(2,1)}), bf16[1536,1536]{1,0:T(8,128)(2,1)}) %all-gather.14.cloned.1.call-update) | async-done | bytes 4718608 | tf_op jit(solution)/shard_map/all_gather | solution.py:188
  164.1 0.4 copy.86
  164.6 0.5 fusion.21
  165.2 0.6 collective-permute-start.1
  165.7 0.3 collective-permute-start.3
  166.0 0.4 fusion.22
  166.6 0.3 collective-permute-done.3
  166.9 2.5 fusion.37
  169.5 33.9 %all-gather.16.cloned.1.call-done = bf16[384,1536]{0,1:T(8,128)(2,1)} async-done(((bf16[384,384]{0,1:T(8,128)(2,1)}), bf16[384,1536]{0,1:T(8,128)(2,1)}) %all-gather.16.cloned.1.call-update) | async-done | bytes 1179664 | tf_op jit(solution)/shard_map/all_gather | solution.py:212
  203.6 6.2 %multiply_reduce_fusion = (f32[384]{0:T(512)S(1)}, f32[384,1536]{1,0:T(8,128)}) fusion(bf16[384,1536]{0,1:T(8,128)(2,1)} %all-gather.16.cloned.1.call-done, bf16[1536,1536]{1,0:T(8,128)(2,1)} %all-gather.14.cloned.1.call-done, bf16[384,1536]{1,0:T(8,128)(2,1)S(1)} %copy-done.3), kind=kOutput, calls=%fused_computation.36 | convolution fusion | flops 1814298240 | bytes 9438720 | tf_op jit(solution)/shard_map/dot_general | solution.py:218
  209.9 1.9 multiply_convert_fusion
  211.8 3.6 gather_fusion.1
  215.5 3.7 gather.12
  219.2 1.9 broadcast_select_fusion
  221.1 41.3 %all_to_all.15 = bf16[32,18,1536]{2,1,0:T(8,128)(2,1)} all-to-all(bf16[32,18,1536]{2,1,0:T(8,128)(2,1)S(1)} %broadcast_select_fusion), channel_id=1, replica_groups=mesh['req'=32,'tp'=4] {'req'}, dimensions={0} | all-to-all | bytes 3538944 | tf_op jit(solution)/shard_map/all_to_all | solution.py:228
  262.5 2.6 reshape.338
  265.1 4.5 %fusion.85 = f32[576,768]{1,0:T(8,128)} fusion(bf16[576,1536]{1,0:T(8,128)(2,1)S(1)} %reshape.338, bf16[1536,768]{0,1:T(8,128)(2,1)} %bitcast.121), kind=kOutput, calls=%fused_computation.164 | convolution fusion | flops 1358954496 | bytes 5898240 | tf_op jit(solution)/shard_map/dot_general | solution.py:231
  269.6 4.8 %multiply_convert_fusion.1 = bf16[576,768]{1,0:T(8,128)(2,1)} fusion(f32[576,768]{1,0:T(8,128)} %fusion.85, bf16[576,1536]{1,0:T(8,128)(2,1)S(1)} %reshape.338, bf16[1536,768]{0,1:T(8,128)(2,1)} %all-gather.18.cloned.1.call-done), kind=kOutput, calls=%fused_computation.39 | convolution fusion | flops 1360281600 | bytes 6782976 | tf_op jit(solution)/shard_map/dot_general | solution.py:232
  274.4 1.6 copy.91
  275.9 20.3 %all-gather.20.cloned.1.call-done = bf16[768,1536]{1,0:T(8,128)(2,1)} async-done(((bf16[192,1536]{1,0:T(8,128)(2,1)}), bf16[768,1536]{1,0:T(8,128)(2,1)}) %all-gather.20.cloned.1.call-update) | async-done | bytes 2359312 | tf_op jit(solution)/shard_map/all_gather | solution.py:217
  296.2 3.9 convert_reduce_fusion
  300.1 1.7 reshape.341
  301.8 9.4 %all-to-all-start.2 = ((bf16[32,18,1536]{2,1,0:T(8,128)(2,1)}), bf16[32,18,1536]{2,1,0:T(8,128)(2,1)}, u32[]{:S(2)}, u32[]{:S(2)}) async-start(bf16[32,18,1536]{2,1,0:T(8,128)(2,1)} %reshape.341), calls=%async_computation.2 | async-start | bytes 4718592 | tf_op jit(solution)/shard_map/all_to_all | solution.py:242
  311.1 0.3 reduce-scatter.2.cloned.1.call-start
  312.3 0.6 select_reduce_fusion
  312.9 30.2 %all-to-all-done.2 = bf16[32,18,1536]{2,1,0:T(8,128)(2,1)} async-done(((bf16[32,18,1536]{2,1,0:T(8,128)(2,1)}), bf16[32,18,1536]{2,1,0:T(8,128)(2,1)}, u32[]{:S(2)}, u32[]{:S(2)}) %all-to-all-start.2) | async-done | bytes 1769504 | tf_op jit(solution)/shard_map/all_to_all | solution.py:242
  343.1 3.8 reshape.342
  346.9 6.0 %fusion.86 = f32[384,1536]{1,0:T(8,128)} fusion(f32[384,576]{0,1:T(8,128)S(1)} %select_reduce_fusion, bf16[576,1536]{1,0:T(8,128)(2,1)} %reshape.342), kind=kOutput, calls=%fused_computation.165 | convolution fusion | flops 4076863488 | bytes 5013504 | tf_op jit(solution)/shard_map/dot_general | solution.py:253
  353.5 29.7 %reduce-scatter.2.cloned.1.call-done = f32[384,384]{1,0:T(8,128)} async-done(((f32[384,1536]{1,0:T(8,128)}), f32[384,384]{1,0:T(8,128)}) %reduce-scatter.2.cloned.1.call-update) | async-done | bytes 589840 | tf_op jit(solution)/shard_map/reduce_scatter | solution.py:259
  383.2 2.1 select_convert_fusion
  (126 shorter events, 5.0 us)
Async XLA Ops:
  6.5 1.6 copy-start
  6.5 2.0 copy-start.12
  6.5 2.9 copy-start.19
  6.5 71.8 %all-gather.12.cloned.1.call-start = ((), (), s32[]{:S(2)}) async-start(), calls=%async_computation.4 | async-start | bytes 1474560 | tf_op jit(solution)/shard_map/all_gather | solution.py:63
  7.3 145.8 %all-gather.22.cloned.1.call-start = ((), (), s32[]{:S(2)}) async-start(), calls=%async_computation.10 | async-start | bytes 2949120 | tf_op jit(solution)/shard_map/all_gather | solution.py:163
  19.0 12.3 %copy-start.13 = (s32[384,4]{0,1:T(4,128)S(1)}, s32[384,4]{0,1:T(4,128)}, u32[]{:S(2)}) copy-start(s32[384,4]{0,1:T(4,128)} %param.29) | copy-start | bytes 18436
  19.0 12.8 %copy-start.17 = (f32[384]{0:T(512)S(1)}, f32[384]{0:T(512)}, u32[]{:S(2)}) copy-start(f32[384]{0:T(512)} %param.19) | copy-start | bytes 4612
  19.0 70.0 %all-to-all-start = ((bf16[32,4,2,64,128]{4,3,2,1,0:T(8,128)(2,1)}), bf16[32,4,2,64,128]{4,3,2,1,0:T(8,128)(2,1)}, u32[]{:S(2)}, u32[]{:S(2)}) async-start(bf16[32,4,2,64,128]{4,3,2,1,0:T(8,128)(2,1)} %copy.85), calls=%async_computation | async-start | bytes 8388608 | tf_op jit(solution)/shard_map/all_to_all | solution.py:103
  30.4 37.9 %copy-start.18 = (f32[384]{0:T(512)S(1)}, f32[384]{0:T(512)}, u32[]{:S(2)}) copy-start(f32[384]{0:T(512)} %param.28) | copy-start | bytes 4612
  30.5 133.6 %all-gather.14.cloned.1.call-start = ((), (), s32[]{:S(2)}) async-start(), calls=%async_computation.5 | async-start | bytes 5898240 | tf_op jit(solution)/shard_map/all_gather | solution.py:188
  31.2 45.1 %copy-start.9 = (bf16[1536,256]{1,0:T(8,128)(2,1)S(1)}, bf16[1536,256]{1,0:T(8,128)(2,1)}, u32[]{:S(2)}) copy-start(bf16[1536,256]{1,0:T(8,128)(2,1)} %param.22) | copy-start | bytes 2359300
  31.2 172.2 %all-gather.16.cloned.1.call-start = ((), (), s32[]{:S(2)}) async-start(), calls=%async_computation.6 | async-start | bytes 1474560 | tf_op jit(solution)/shard_map/all_gather | solution.py:212
  31.3 47.0 %copy-start.15 = (f32[64]{0:T(128)}, f32[64]{0:T(128)S(1)}, u32[]{:S(2)}) copy-start(f32[64]{0:T(128)S(1)} %multiply_power_fusion) | copy-start | bytes 772
  82.7 3.2 copy-start.2
  83.8 2.1 copy-start.7
  83.8 2.1 copy-start.8
  85.4 1.2 copy-start.5
  85.4 1.8 collective-permute-start
  85.9 0.8 copy-start.16
  86.6 0.7 copy-start.10
  153.0 11.6 %copy-start.6 = (bf16[384,3,128]{2,0,1:T(8,128)(2,1)S(1)}, bf16[384,3,128]{2,0,1:T(8,128)(2,1)}, u32[]{:S(2)}) copy-start(bf16[384,3,128]{2,0,1:T(8,128)(2,1)} %copy-done.5) | copy-start | bytes 884740
  164.4 2.0 copy-start.4
  164.5 2.4 collective-permute-start.2
  164.6 2.3 copy-start.11
  165.2 1.4 collective-permute-start.1
  165.7 1.2 collective-permute-start.3
  166.9 36.7 %copy-start.3 = (bf16[384,1536]{1,0:T(8,128)(2,1)S(1)}, bf16[384,1536]{1,0:T(8,128)(2,1)}, u32[]{:S(2)}) copy-start(bf16[384,1536]{1,0:T(8,128)(2,1)} %all-gather.12.cloned.1.call-done) | copy-start | bytes 3538948
  169.5 100.1 %all-gather.18.cloned.1.call-start = ((), (), s32[]{:S(2)}) async-start(), calls=%async_computation.7 | async-start | bytes 2949120 | tf_op jit(solution)/shard_map/all_gather | solution.py:216
  203.4 92.7 %all-gather.20.cloned.1.call-start = ((), (), s32[]{:S(2)}) async-start(), calls=%async_computation.8 | async-start | bytes 2949120 | tf_op jit(solution)/shard_map/all_gather | solution.py:217
  301.8 9.7 %copy-start.14 = (f32[384,4]{0,1:T(4,128)S(1)}, f32[384,4]{0,1:T(4,128)}, u32[]{:S(2)}) copy-start(f32[384,4]{0,1:T(4,128)} %param.30) | copy-start | bytes 18436
  301.8 41.3 %all-to-all-start.2 = ((bf16[32,18,1536]{2,1,0:T(8,128)(2,1)}), bf16[32,18,1536]{2,1,0:T(8,128)(2,1)}, u32[]{:S(2)}, u32[]{:S(2)}) async-start(bf16[32,18,1536]{2,1,0:T(8,128)(2,1)} %reshape.341), calls=%async_computation.2 | async-start | bytes 4718592 | tf_op jit(solution)/shard_map/all_to_all | solution.py:242
  311.1 72.1 %reduce-scatter.2.cloned.1.call-start = ((), (), s32[]{:S(2)}) async-start(), calls=%async_computation.9 | async-start | bytes 2949120 | tf_op jit(solution)/shard_map/reduce_scatter | solution.py:259
  346.9 38.4 %copy-start.1 = (bf16[16,2,2,128,128]{4,3,2,1,0:T(8,128)(2,1)S(1)}, bf16[16,2,2,128,128]{4,3,2,1,0:T(8,128)(2,1)}, u32[]{:S(2)}) copy-start(bf16[16,2,2,128,128]{4,3,2,1,0:T(8,128)(2,1)} %param.24) | copy-start | bytes 6291460
Sparse Core Ops, SparseCore 0:
  9.0 44.2 all-gather.11
  55.0 55.5 all-gather.21
  112.2 51.8 all-gather.13
  169.6 33.7 all-gather.15
  204.9 57.7 all-gather.17
  264.2 31.8 all-gather.19
  353.0 30.1 reduce-scatter.1
